TPU v7x, 512 devices: a whole 4x8x8 slice. The times are simulated.
512 devices in a mesh: rows: 64 (over y, x, core), grp: 8 (over z).
Axes of the slice: x: 4, y: 8, z: 8, core: 2. Of those that a mesh axis runs over, the one named last changes fastest.
Arguments:
- panel_block: float32 [98304, 512], P(('rows', 'grp')), may hold values from -1000 to 1000, as said below
- trailing: float32 [98304, 768], P(('rows', 'grp')), may hold values from -1000 to 1000
Outputs:
- r_factor: float32 [512, 512], replicated
- updated_trailing: float32 [98304, 768], P(('rows', 'grp'))
Inputs may be any that keep to these rules, and one draw needn't show every extreme that they name: panel_block has full column rank and is well conditioned.
All inputs are finite; a program needn't handle non-finite values.
Results may differ from a plain program's by a relative error of at most 0.000092.
Values sent between devices are 32-bit elements; how exact they have to be, the bound alone decides.
No kernel may reach another device: no remote copies, remote signals or barrier semaphores. Data moves between devices by JAX's collectives and lax.ppermute only.
A program may use at most 64 MiB of HBM per device.

v0:
```python
import jax
import jax.numpy as jnp
from jax import lax
from jax.sharding import PartitionSpec as P


def local(panel_block, trailing):
    highest = lax.Precision.HIGHEST
    row_count = panel_block.shape[0] * lax.axis_size("rows") * lax.axis_size("grp")
    gram_part = (
        jnp.dot(panel_block.T, panel_block, precision=highest, preferred_element_type=jnp.float32)
        / row_count
    )
    gram = lax.psum(gram_part, ("rows", "grp"))
    lower_factor = jnp.linalg.cholesky(gram)
    orthogonal = jax.scipy.linalg.solve_triangular(lower_factor, panel_block.T, lower=True).T
    local_terms = (
        jnp.dot(orthogonal.T, trailing, precision=highest, preferred_element_type=jnp.float32)
        / row_count
    )
    projected = lax.psum(local_terms, ("rows", "grp"))
    updated_trailing = trailing - jnp.dot(
        orthogonal, projected, precision=highest, preferred_element_type=jnp.float32
    )
    return (lower_factor.T, updated_trailing)


def solution(mesh):
    in_specs = (P(("rows", "grp"), None), P(("rows", "grp"), None))
    out_specs = (P(), P(("rows", "grp"), None))
    return jax.shard_map(local, mesh=mesh, in_specs=in_specs, out_specs=out_specs, check_vma=False)
```

profile of v0, /device:TPU:1, one launch (start us, length us, event | category | flops | bytes accessed | tf_op | source)
XLA Modules:
  0.0 725.4 jit_solution(13783917243216974403)
XLA Ops:
  7.2 3.2 convolution_multiply_fusion.1
  10.5 284.1 %all-reduce.4.cloned.1.call-done = f32[512,512]{0,1:T(8,128)} async-done(((f32[512,512]{0,1:T(8,128)}), f32[512,512]{0,1:T(8,128)}) %all-reduce.4.cloned.1.call-update) | async-done | bytes 1048592 | tf_op jit(solution)/shard_map/psum | solution.py:14
  294.6 1.6 copy.5
  296.5 11.7 %cholesky.104 = f32[128,128]{1,0:T(8,128)S(1)} custom-call(f32[128,128]{1,0:T(8,128)S(1)} %cholesky.266), custom_call_target="Cholesky" | custom-call | tf_op jit(solution)/shard_map/jit(cholesky)/cholesky | solution.py:15
  308.2 9.8 %custom-call.31 = f32[1,128,128]{1,2,0:T(8,128)S(1)} custom-call(f32[1,128,128]{2,1,0:T(8,128)S(1)} %get-tuple-element.33), custom_call_target="InvertDiagBlocksLowerTriangular" | custom-call | tf_op jit(solution)/shard_map/jit(cholesky)/cholesky | solution.py:15
  318.8 11.7 %cholesky.217 = f32[128,128]{1,0:T(8,128)S(1)} custom-call(f32[128,128]{1,0:T(8,128)S(1)} %cholesky.270), custom_call_target="Cholesky" | custom-call | tf_op jit(solution)/shard_map/jit(cholesky)/cholesky | solution.py:15
  330.6 10.0 %custom-call.32 = f32[1,128,128]{1,2,0:T(8,128)S(1)} custom-call(f32[1,128,128]{2,1,0:T(8,128)S(1)} %get-tuple-element.30), custom_call_target="InvertDiagBlocksLowerTriangular" | custom-call | tf_op jit(solution)/shard_map/jit(cholesky)/cholesky | solution.py:15
  341.2 11.7 %cholesky.238 = f32[128,128]{1,0:T(8,128)S(1)} custom-call(f32[128,128]{1,0:T(8,128)S(1)} %cholesky.275), custom_call_target="Cholesky" | custom-call | tf_op jit(solution)/shard_map/jit(cholesky)/cholesky | solution.py:15
  353.0 0.7 compare_reduce_fusion.1
  353.7 9.8 %custom-call.33 = f32[1,128,128]{1,2,0:T(8,128)S(1)} custom-call(f32[1,128,128]{2,1,0:T(8,128)S(1)} %get-tuple-element.27), custom_call_target="InvertDiagBlocksLowerTriangular" | custom-call | tf_op jit(solution)/shard_map/jit(cholesky)/cholesky | solution.py:15
  364.1 11.7 %cholesky.255 = f32[128,128]{1,0:T(8,128)S(1)} custom-call(f32[128,128]{1,0:T(8,128)S(1)} %convolution_subtract_fusion.6), custom_call_target="Cholesky" | custom-call | tf_op jit(solution)/shard_map/jit(cholesky)/cholesky | solution.py:15
  380.2 10.9 %while.1 = (s32[]{:T(128)}, f32[512,512]{1,0:T(8,128)S(1)}, s32[4,2]{0,1:T(2,128)S(1)}, f32[4,128,128]{2,1,0:T(8,128)}, s32[]{:T(128)}) while((s32[]{:T(128)}, f32[512,512]{1,0:T(8,128)S(1)}, s32[4,2]{0,1:T(2,128)S(1)}, f32[4,128,128]{2,1,0:T(8,128)}, s32[]{:T(128)}) %tuple.33), condition=%wide.while_cond, body=%wide.while_body.sunk | while | flops 2 | bytes 132205 | solution.py:16
  380.9 2.1 bitcast_dynamic-update-slice_fusion.2
  383.6 2.1 bitcast_dynamic-update-slice_fusion.2
  386.3 2.1 bitcast_dynamic-update-slice_fusion.2
  389.1 2.1 bitcast_dynamic-update-slice_fusion.2
  391.1 40.1 %custom-call.34 = f32[4,128,128]{1,2,0:T(8,128)S(1)} custom-call(f32[4,128,128]{2,1,0:T(8,128)} %get-tuple-element.9), custom_call_target="InvertDiagBlocksLowerTriangular" | custom-call | tf_op jit(solution)/shard_map/jit(_solve_triangular)/triangular_solve | solution.py:16
  432.5 1.1 fusion.24
  433.9 1.1 fusion.22
  435.4 1.1 fusion.21
  436.5 2.6 convolution_multiply_fusion
  439.1 1.3 copy.6
  440.4 274.7 %all-reduce.6.cloned.1.call-done = f32[512,768]{1,0:T(8,128)} async-done(((f32[512,768]{1,0:T(8,128)}), f32[512,768]{1,0:T(8,128)}) %all-reduce.6.cloned.1.call-update) | async-done | bytes 1572880 | tf_op jit(solution)/shard_map/psum | solution.py:21
  715.2 3.4 convolution_subtract_fusion
  (45 shorter events, 8.9 us)
Async XLA Ops:
  7.2 287.4 %all-reduce.4.cloned.1.call-start = ((), (), s32[]{:S(2)}) async-start(), calls=%async_computation | async-start | bytes 2097152 | tf_op jit(solution)/shard_map/psum | solution.py:14
  10.4 704.7 %all-reduce.6.cloned.1.call-start = ((), (), s32[]{:S(2)}) async-start(), calls=%async_computation.1 | async-start | bytes 3145728 | tf_op jit(solution)/shard_map/psum | solution.py:21
  294.6 1.7 copy-start
  379.7 52.3 %copy-start.1 = (f32[192,512]{1,0:T(8,128)S(1)}, f32[192,512]{1,0:T(8,128)}, u32[]{:S(2)}) copy-start(f32[192,512]{1,0:T(8,128)} %param.2) | copy-start | bytes 1179652
  380.2 56.3 %copy-start.2 = (f32[192,768]{1,0:T(8,128)S(1)}, f32[192,768]{1,0:T(8,128)}, u32[]{:S(2)}) copy-start(f32[192,768]{1,0:T(8,128)} %param.3) | copy-start | bytes 1769476
  431.2 0.7 copy-start.3
Sparse Core Ops, SparseCore 0:
  13.6 280.8 all-reduce.3
  439.3 275.8 all-reduce.5
where the time goes:
time: 726 us; the launch traced here: 725 us
  waiting for transfers between devices  559 us (77%)
  other arithmetic  119 us (16%)
  between operations  16.8 us (2%)
  matrix products  15.6 us (2%)
  local copies, waits for them, and re-layouts  14.7 us (2%)
    psum x1, waiting for transfers between devices, local(): gram = lax.psum(gram_part, ('rows', 'grp'))  284 us
    psum x1, waiting for transfers between devices, local(): projected = lax.psum(local_terms, ('rows', 'grp'))  275 us
    another operation x14, other arithmetic, local(): lower_factor = jnp.linalg.cholesky(gram)  78.6 us
    another operation x3, other arithmetic, local(): jax.scipy.linalg.solve_triangular(lower_factor, panel_block.T, lower=True)  40.6 us
  transfers between devices with their start and end apart: 2, of which 2 were waited for; matrix products, arithmetic and copies ran while one was open for 0% of the time, Pallas kernels for 0%

commit v1 on v0

v1 whole, which is shorter than its diff:
```python
import jax
import jax.numpy as jnp
from jax import lax
from jax.experimental import pallas as pl
from jax.experimental.pallas import tpu as pltpu
from jax.sharding import Mesh, PartitionSpec as P

HI = lax.Precision.HIGHEST
B = 128
NP = 4
NC = 6
G_BLOCKS = [(i, j) for i in range(NP) for j in range(i, NP)]
C_BLOCKS = [(i, j) for i in range(NP) for j in range(NC)]
G_HALF = 6
C_HALF = 12


def split_half(blocks, half):
    n = (len(blocks) + 1) // 2
    return [(b, 0 if k < n else 1, k if k < n else k - n) for k, b in enumerate(blocks)]


def gram_kernel(core_ref, a_ref, t_ref, gk_ref, gs_ref, ck_ref, cs_ref):
    core = core_ref[0]
    at = a_ref[...].T

    def put(value, owner, slot, keep_ref, send_ref):
        rows = pl.ds(slot * B, B)

        @pl.when(core == owner)
        def _():
            keep_ref[rows, :] = value

        @pl.when(core != owner)
        def _():
            send_ref[rows, :] = value

    for (i, j), owner, slot in split_half(G_BLOCKS, G_HALF):
        value = jnp.dot(at[i * B : (i + 1) * B], a_ref[:, j * B : (j + 1) * B], precision=HI, preferred_element_type=jnp.float32)
        put(value, owner, slot, gk_ref, gs_ref)
    for ref in (gk_ref, gs_ref):
        ref[(G_HALF - 1) * B :, :] = jnp.zeros((B, B), jnp.float32)
    for (i, j), owner, slot in split_half(C_BLOCKS, C_HALF):
        value = jnp.dot(at[i * B : (i + 1) * B], t_ref[:, j * B : (j + 1) * B], precision=HI, preferred_element_type=jnp.float32)
        put(value, owner, slot, ck_ref, cs_ref)


def gram(core, a, t):
    g = jax.ShapeDtypeStruct((G_HALF * B, B), jnp.float32)
    c = jax.ShapeDtypeStruct((C_HALF * B, B), jnp.float32)
    vmem = pl.BlockSpec(memory_space=pltpu.VMEM)
    return pl.pallas_call(
        gram_kernel,
        out_shape=(g, g, c, c),
        in_specs=[pl.BlockSpec(memory_space=pltpu.SMEM), vmem, vmem],
        out_specs=[vmem] * 4,
        cost_estimate=pl.CostEstimate(flops=2 * 192 * 512 * 1280, bytes_accessed=4 << 20, transcendentals=0),
    )(core, a, t)


def diag_factor(load, store_u, store_e):
    s = [load(g) for g in range(16)]
    lane = lax.broadcasted_iota(jnp.int32, (8, B), 1)
    sub = lax.broadcasted_iota(jnp.int32, (8, B), 0)
    e = [jnp.where(lane == sub + 8 * g, 1.0, 0.0).astype(jnp.float32) for g in range(16)]
    for g0 in range(16):
        us, es = [], []
        for t in range(8):
            j = 8 * g0 + t
            cols = [jnp.broadcast_to(s[g][:, j : j + 1], (8, B)) for g in range(g0, 16)]
            inv = lax.rsqrt(jnp.broadcast_to(cols[0][t : t + 1, :], (8, B)))
            u = jnp.broadcast_to(s[g0][t : t + 1, :], (8, B)) * inv
            v = jnp.broadcast_to(e[g0][t : t + 1, :], (8, B)) * inv
            us.append(u)
            es.append(v)
            for g in range(g0, 16):
                l = cols[g - g0] * inv
                if g == g0:
                    l = jnp.where(sub > t, l, 0.0)
                s[g] = s[g] - l * u
                e[g] = e[g] - l * v
        u, v = us[0], es[0]
        for t in range(1, 8):
            u = jnp.where(sub == t, us[t], u)
            v = jnp.where(sub == t, es[t], v)
        store_u(g0, jnp.where(lane >= sub + 8 * g0, u, 0.0))
        store_e(g0, v)


def dot(x, y):
    return jnp.dot(x, y, precision=HI, preferred_element_type=jnp.float32)


def dot_t(x, y):
    return lax.dot_general(x, y, (((0,), (0,)), ((), ())), precision=HI, preferred_element_type=jnp.float32)


def panel_step(k, x, rkk, lkk):
    r0 = k * B
    r1 = r0 + B

    def store_u(g, v):
        rkk[8 * g : 8 * g + 8, :] = v

    def store_e(g, v):
        lkk[8 * g : 8 * g + 8, :] = v

    diag_factor(lambda g: x[r0 + 8 * g : r0 + 8 * g + 8, r0:r1], store_u, store_e)
    linv = lkk[...]
    if k > 0:
        x[r0:r1, :r0] = dot(linv, x[r0:r1, :r0])
    if k < NP - 1:
        x[r0:r1, r1:] = dot(linv, x[r0:r1, r1:])
    x[r0:r1, r0:r1] = linv
    for i in range(k + 1, NP):
        c0 = i * B
        left = x[r0:r1, c0 : c0 + B]
        x[c0 : c0 + B, c0:] = x[c0 : c0 + B, c0:] - dot_t(left, x[r0:r1, c0:])
        low = dot_t(left, x[r0:r1, :r1])
        if k > 0:
            x[c0 : c0 + B, :r0] = x[c0 : c0 + B, :r0] - low[:, :r0]
        x[c0 : c0 + B, r0:r1] = -low[:, r0:]


def first_kernel(row_count, core_ref, gm_ref, go_ref, x_ref, r_ref, lkk):
    core = core_ref[0]
    scale = 1.0 / row_count
    x_ref[...] = jnp.zeros_like(x_ref)
    for (i, j), owner, slot in split_half(G_BLOCKS, G_HALF):
        rows = slice(slot * B, (slot + 1) * B)
        value = jnp.where(core == owner, gm_ref[rows, :], go_ref[rows, :])
        x_ref[i * B : (i + 1) * B, j * B : (j + 1) * B] = value * scale
    panel_step(0, x_ref, r_ref, lkk)


def mid_kernel(k, xi_ref, x_ref, r_ref, lkk):
    x_ref[...] = xi_ref[...]
    panel_step(k, x_ref, r_ref, lkk)


def last_kernel(xi_ref, ra_ref, rb_ref, rc_ref, x_ref, r_ref, rkk, lkk):
    x_ref[...] = xi_ref[...]
    panel_step(NP - 1, x_ref, rkk, lkk)
    r_ref[...] = jnp.zeros_like(r_ref)
    for i, ref in enumerate((ra_ref, rb_ref, rc_ref, rkk)):
        r_ref[i * B : (i + 1) * B, i * B : (i + 1) * B] = ref[...]
        if i < NP - 1:
            r_ref[i * B : (i + 1) * B, (i + 1) * B :] = x_ref[i * B : (i + 1) * B, (i + 1) * B :]


VM = pl.BlockSpec(memory_space=pltpu.VMEM)
SM = pl.BlockSpec(memory_space=pltpu.SMEM)


def factor(row_count, core, gm, go):
    full = jax.ShapeDtypeStruct((NP * B, NP * B), jnp.float32)
    block = jax.ShapeDtypeStruct((B, B), jnp.float32)
    scratch = pltpu.VMEM((B, B), jnp.float32)
    cost = pl.CostEstimate(flops=20_000_000_000, bytes_accessed=2 << 20, transcendentals=0)
    x, ra = pl.pallas_call(
        lambda *refs: first_kernel(row_count, *refs),
        out_shape=(full, block), in_specs=[SM, VM, VM], out_specs=[VM, VM],
        scratch_shapes=[scratch], cost_estimate=cost, name="factor0",
    )(core, gm, go)
    diag = [ra]
    for k in (1, 2):
        x, rk = pl.pallas_call(
            lambda *refs, k=k: mid_kernel(k, *refs),
            out_shape=(full, block), in_specs=[VM], out_specs=[VM, VM],
            scratch_shapes=[scratch], cost_estimate=cost, name=f"factor{k}",
        )(x)
        diag.append(rk)
    return pl.pallas_call(
        last_kernel,
        out_shape=(full, full), in_specs=[VM] * 4, out_specs=[VM, VM],
        scratch_shapes=[scratch, scratch], cost_estimate=cost, name="factor3",
    )(x, *diag)


def update_kernel(row_count, core_ref, x_ref, cm_ref, co_ref, a_ref, t_ref, out_ref, q, p):
    core = core_ref[0]
    scale = 1.0 / row_count
    for i in range(NP):
        li = x_ref[i * B : (i + 1) * B, : (i + 1) * B]
        q[:, i * B : (i + 1) * B] = lax.dot_general(
            a_ref[:, : (i + 1) * B], li, (((1,), (1,)), ((), ())), precision=HI, preferred_element_type=jnp.float32
        )
    c = {}
    for b, owner, slot in split_half(C_BLOCKS, C_HALF):
        rows = slice(slot * B, (slot + 1) * B)
        c[b] = jnp.where(core == owner, cm_ref[rows, :], co_ref[rows, :]) * scale
    for j in range(NC):
        col = jnp.concatenate([c[(i, j)] for i in range(NP)], axis=0)
        for i in range(NP):
            p[i * B : (i + 1) * B, j * B : (j + 1) * B] = dot(x_ref[i * B : (i + 1) * B, : (i + 1) * B], col[: (i + 1) * B])
    for j in range(NC):
        cols = slice(j * B, (j + 1) * B)
        out_ref[:, cols] = t_ref[:, cols] - dot(q[...], p[:, cols])


def update(row_count, core, x, cm, co, a, t):
    return pl.pallas_call(
        lambda *refs: update_kernel(row_count, *refs),
        out_shape=jax.ShapeDtypeStruct(t.shape, jnp.float32),
        in_specs=[SM] + [VM] * 5, out_specs=VM,
        scratch_shapes=[pltpu.VMEM(a.shape, jnp.float32), pltpu.VMEM((NP * B, NC * B), jnp.float32)],
        cost_estimate=pl.CostEstimate(flops=4_000_000_000, bytes_accessed=4 << 20, transcendentals=0), name="update",
    )(core, x, cm, co, a, t)


def reduce_all(keep, send):
    half = keep + lax.ppermute(send, "c", [(0, 1), (1, 0)])
    n = half.shape[0] // 32
    parts = lax.all_to_all(half.reshape(32, n, B), ("y", "x"), 0, 0)
    mine = jnp.sum(parts, axis=0)
    parts = lax.all_to_all(jnp.broadcast_to(mine[None], (8, n, B)), "z", 0, 0)
    mine = jnp.sum(parts, axis=0)
    half = lax.all_to_all(jnp.broadcast_to(mine[None], (32, n, B)), ("y", "x"), 0, 0)
    mine = half.reshape(32 * n, B)
    return mine, lax.ppermute(mine, "c", [(0, 1), (1, 0)])


def local(row_count, panel_block, trailing):
    core = lax.axis_index("c").astype(jnp.int32).reshape(1)
    gk, gs, ck, cs = gram(core, panel_block, trailing)
    gm, go = reduce_all(gk, gs)
    cm, co = reduce_all(ck, cs)
    x, r = factor(row_count, core, gm, go)
    return r, update(row_count, core, x, cm, co, panel_block, trailing)


def solution(mesh):
    fine = Mesh(mesh.devices.reshape(8, 4, 2, 8), ("y", "x", "c", "z"))
    axes = ("y", "x", "c", "z")

    def run(panel_block, trailing):
        rows = panel_block.shape[0]
        f = jax.shard_map(
            lambda a, t: local(rows, a, t),
            mesh=fine,
            in_specs=(P(axes, None), P(axes, None)),
            out_specs=(P(), P(axes, None)),
            check_vma=False,
        )
        return f(panel_block, trailing)

    return run
```

time: 726 us -> 216 us (0.30)
  waiting for transfers between devices: 559 us -> 28.2 us
  other arithmetic: 119 us -> 2.14 us
  Pallas kernels: 0 us -> 103 us
  starting transfers between devices: 0.08 us -> 58.2 us
  blocking collectives: 0 us -> 18.1 us
  between operations: 16.8 us -> 0.78 us
  matrix products: 15.6 us -> 0 us
  local copies, waits for them, and re-layouts: 14.7 us -> 4.73 us
    psum x2 -> x0, waiting for transfers between devices: 559 us -> none  [the longest x1 284 us: local(): gram = lax.psum(gram_part, ('rows', 'grp'))]
    another operation x17 -> x0, other arithmetic: 119 us -> none  [the longest x14 78.6 us: local(): lower_factor = jnp.linalg.cholesky(gram)]
    pallas_call x0 -> x6, Pallas kernels: none -> 103 us  [the longest x2 40 us: factor(): pl.pallas_call(lambda *refs, k=k: mid_kernel(k, *refs), out_shape=(full,...]
    all_to_all x0 -> x5, starting transfers between devices: none -> 33.2 us  [the longest x2 15.6 us: reduce_all(): parts = lax.all_to_all(jnp.broadcast_to(mine[None], (8, n, B)), 'z', 0, 0)]
    all_to_all x0 -> x5, waiting for transfers between devices: none -> 26.7 us  [the longest x1 13.2 us: reduce_all(): parts = lax.all_to_all(half.reshape(32, n, B), ('y', 'x'), 0, 0)]
    ppermute x0 -> x4, starting transfers between devices: none -> 24.9 us  [the longest x2 13.3 us: reduce_all(): half = keep + lax.ppermute(send, 'c', [(0, 1), (1, 0)])]
    all_to_all x0 -> x1, blocking collectives: none -> 18.1 us  [reduce_all(): parts = lax.all_to_all(half.reshape(32, n, B), ('y', 'x'), 0, 0)]
    another operation x17 -> x0, local copies, waits for them, and re-layouts: 11.1 us -> none
  transfers between devices with their start and end apart: 2 -> 9, of which waited for: 2 -> 4; matrix products, arithmetic and copies ran while one was open for 0% -> 1% of each run, Pallas kernels for 0% -> 37%
where the time goes in v1:
time: 216 us; the launch traced here: 215 us
  Pallas kernels  103 us (48%)
  starting transfers between devices  58.2 us (27%)
  waiting for transfers between devices  28.2 us (13%)
  blocking collectives  18.1 us (8%)
  local copies, waits for them, and re-layouts  4.73 us (2%)
    pallas_call x2, Pallas kernels, factor(): pl.pallas_call(lambda *refs, k=k: mid_kernel(k, *refs), out_shape=(full,...  40 us
    pallas_call x1, Pallas kernels, factor(): pl.pallas_call(lambda *refs: first_kernel(row_count, *refs), out_shape=(f...  20.1 us
    pallas_call x1, Pallas kernels, factor(): pl.pallas_call(last_kernel, out_shape=(full, full), in_specs=[VM] * 4, ou...  19.9 us
    all_to_all x1, blocking collectives, reduce_all(): parts = lax.all_to_all(half.reshape(32, n, B), ('y', 'x'), 0, 0)  18.1 us
    all_to_all x2, starting transfers between devices, reduce_all(): parts = lax.all_to_all(jnp.broadcast_to(mine[None], (8, n, B)), 'z', 0, 0)  15.6 us
    pallas_call x1, Pallas kernels, gram(): pl.pallas_call(gram_kernel, out_shape=(g, g, c, c), in_specs=[pl.BlockSpe...  14.3 us
    ppermute x2, starting transfers between devices, reduce_all(): half = keep + lax.ppermute(send, 'c', [(0, 1), (1, 0)])  13.3 us
    all_to_all x1, waiting for transfers between devices, reduce_all(): parts = lax.all_to_all(half.reshape(32, n, B), ('y', 'x'), 0, 0)  13.2 us
  transfers between devices with their start and end apart: 9, of which 4 were waited for; matrix products, arithmetic and copies ran while one was open for 1% of the time, Pallas kernels for 37%

profile of v1, /device:TPU:1, one launch (start us, length us, event | category | flops | bytes accessed | tf_op | source)
XLA Modules:
  0.0 215.3 jit_solution(14011106426912164262)
XLA Ops:
  0.6 14.3 %shard_map.41 = (f32[768,128]{1,0:T(8,128)}, f32[768,128]{1,0:T(8,128)}, f32[1536,128]{1,0:T(8,128)}, f32[1536,128]{1,0:T(8,128)}) custom-call(s32[1]{0:T(128)} %bitcast.core_ref.refs_0_, f32[192,512]{1,0:T(8,128)} %refs_4_.1, f32[192,768]{1,0:T(8,128)} %refs_5_.1), custom_call_target="tpu_custom_call" | custom-call | flops 251658240 | bytes 4194304 | tf_op jit(solution)/shard_map/pallas_call | solution.py:52
  15.0 8.7 %collective-permute-start = (f32[768,128]{1,0:T(8,128)}, f32[768,128]{1,0:T(8,128)S(1)}, u32[]{:S(2)}, u32[]{:S(2)}) collective-permute-start(f32[768,128]{1,0:T(8,128)} %get-tuple-element.15), channel_id=1, source_target_pairs={{0,8},{8,0},{1,9},{9,1},{2,10},{10,2},{3,11},{11,3},{4,12},{12,4},... | collective-permute-start | bytes 1179656 | tf_op jit(solution)/shard_map/ppermute | solution.py:212
  23.7 1.5 collective-permute-done
  25.3 1.1 add.6
  26.3 18.1 %all_to_all.30 = f32[32,24,128]{2,1,0:T(8,128)S(1)} all-to-all(f32[32,24,128]{2,1,0:T(8,128)S(1)} %bitcast.5), channel_id=1, replica_groups=mesh['y'=8,'x'=4,'c'=2,'z'=8] {'y','x'}, dimensions={0} | all-to-all | bytes 786432 | tf_op jit(solution)/shard_map/all_to_all | solution.py:214
  45.2 10.0 %all-to-all-start.1 = ((f32[8,24,128]{2,1,0:T(8,128)}), f32[8,24,128]{2,1,0:T(8,128)S(1)}, u32[]{:S(2)}, u32[]{:S(2)}) async-start(f32[8,24,128]{2,1,0:T(8,128)} %broadcast_in_dim.8), calls=%async_computation.1 | async-start | bytes 196608 | tf_op jit(solution)/shard_map/all_to_all | solution.py:216
  55.2 4.5 %collective-permute-start.2 = (f32[1536,128]{1,0:T(8,128)S(1)}, f32[1536,128]{1,0:T(8,128)S(1)}, u32[]{:S(2)}, u32[]{:S(2)}) collective-permute-start(f32[1536,128]{1,0:T(8,128)S(1)} %copy-done.3), channel_id=1, source_target_pairs={{0,8},{8,0},{1,9},{9,1},{2,10},{10,2},{3,11},{11,3},{4,12},{12,4},... | collective-permute-start | bytes 2359304 | tf_op jit(solution)/shard_map/ppermute | solution.py:212
  59.7 3.0 %all-to-all-done.1 = f32[8,24,128]{2,1,0:T(8,128)S(1)} async-done(((f32[8,24,128]{2,1,0:T(8,128)}), f32[8,24,128]{2,1,0:T(8,128)S(1)}, u32[]{:S(2)}, u32[]{:S(2)}) %all-to-all-start.1) | async-done | bytes 98336 | tf_op jit(solution)/shard_map/all_to_all | solution.py:216
  63.6 5.1 %all-to-all-start.2 = ((f32[32,24,128]{2,1,0:T(8,128)}), f32[32,24,128]{2,1,0:T(8,128)S(1)}, u32[]{:S(2)}, u32[]{:S(2)}) async-start(f32[32,24,128]{2,1,0:T(8,128)} %broadcast_in_dim.9), calls=%async_computation.2 | async-start | bytes 786432 | tf_op jit(solution)/shard_map/all_to_all | solution.py:218
  68.7 1.0 add.7
  69.6 10.5 %all-to-all-done.2 = f32[32,24,128]{2,1,0:T(8,128)S(1)} async-done(((f32[32,24,128]{2,1,0:T(8,128)}), f32[32,24,128]{2,1,0:T(8,128)S(1)}, u32[]{:S(2)}, u32[]{:S(2)}) %all-to-all-start.2) | async-done | bytes 393248 | tf_op jit(solution)/shard_map/all_to_all | solution.py:218
  80.1 5.8 %all-to-all-start.3 = ((f32[32,48,128]{2,1,0:T(8,128)}), f32[32,48,128]{2,1,0:T(8,128)S(1)}, u32[]{:S(2)}, u32[]{:S(2)}) async-start(f32[32,48,128]{2,1,0:T(8,128)} %bitcast.3), calls=%async_computation.3 | async-start | bytes 1572864 | tf_op jit(solution)/shard_map/all_to_all | solution.py:214
  85.9 5.3 %collective-permute-start.1 = (f32[768,128]{1,0:T(8,128)S(1)}, f32[768,128]{1,0:T(8,128)S(1)}, u32[]{:S(2)}, u32[]{:S(2)}) collective-permute-start(f32[768,128]{1,0:T(8,128)S(1)} %bitcast.8), channel_id=1, source_target_pairs={{0,8},{8,0},{1,9},{9,1},{2,10},{10,2},{3,11},{11,3},{4,12},{12,4},... | collective-permute-start | bytes 1179656 | tf_op jit(solution)/shard_map/ppermute | solution.py:220
  91.2 13.2 %all-to-all-done.3 = f32[32,48,128]{2,1,0:T(8,128)S(1)} async-done(((f32[32,48,128]{2,1,0:T(8,128)}), f32[32,48,128]{2,1,0:T(8,128)S(1)}, u32[]{:S(2)}, u32[]{:S(2)}) %all-to-all-start.3) | async-done | bytes 786464 | tf_op jit(solution)/shard_map/all_to_all | solution.py:214
  105.2 5.6 %all-to-all-start.4 = ((f32[8,48,128]{2,1,0:T(8,128)}), f32[8,48,128]{2,1,0:T(8,128)S(1)}, u32[]{:S(2)}, u32[]{:S(2)}) async-start(f32[8,48,128]{2,1,0:T(8,128)} %broadcast_in_dim.10), calls=%async_computation.4 | async-start | bytes 393216 | tf_op jit(solution)/shard_map/all_to_all | solution.py:216
  111.5 20.1 %factor0.1 = (f32[512,512]{1,0:T(8,128)}, f32[128,128]{1,0:T(8,128)}) custom-call(s32[1]{0:T(128)} %bitcast.core_ref.refs_0_, f32[768,128]{1,0:T(8,128)} %bitcast.9, f32[768,128]{1,0:T(8,128)} %copy-done.5), custom_call_target="tpu_custom_call" | custom-call | flops 20000000000 | bytes 2097152 | tf_op jit(solution)/shard_map/factor0/pallas_call | solution.py:160
  131.6 20.1 %factor1.1 = (f32[512,512]{1,0:T(8,128)}, f32[128,128]{1,0:T(8,128)}) custom-call(f32[512,512]{1,0:T(8,128)} %get-tuple-element.16.refs_0_), custom_call_target="tpu_custom_call" | custom-call | flops 20000000000 | bytes 2097152 | tf_op jit(solution)/shard_map/factor1/pallas_call | solution.py:167
  151.7 0.9 broadcast_in_dim.11
  152.6 6.8 %all-to-all-start.5 = ((f32[32,48,128]{2,1,0:T(8,128)}), f32[32,48,128]{2,1,0:T(8,128)S(1)}, u32[]{:S(2)}, u32[]{:S(2)}) async-start(f32[32,48,128]{2,1,0:T(8,128)} %broadcast_in_dim.11), calls=%async_computation.5 | async-start | bytes 1572864 | tf_op jit(solution)/shard_map/all_to_all | solution.py:218
  159.4 19.9 %factor2.1 = (f32[512,512]{1,0:T(8,128)}, f32[128,128]{1,0:T(8,128)}) custom-call(f32[512,512]{1,0:T(8,128)} %get-tuple-element.17.refs_0_), custom_call_target="tpu_custom_call" | custom-call | flops 20000000000 | bytes 2097152 | tf_op jit(solution)/shard_map/factor2/pallas_call | solution.py:167
  179.3 6.3 %collective-permute-start.3 = (f32[1536,128]{1,0:T(8,128)S(1)}, f32[1536,128]{1,0:T(8,128)S(1)}, u32[]{:S(2)}, u32[]{:S(2)}) collective-permute-start(f32[1536,128]{1,0:T(8,128)S(1)} %bitcast.6), channel_id=1, source_target_pairs={{0,8},{8,0},{1,9},{9,1},{2,10},{10,2},{3,11},{11,3},{4,12},{12,4},... | collective-permute-start | bytes 2359304 | tf_op jit(solution)/shard_map/ppermute | solution.py:220
  185.7 19.9 %factor3.1 = (f32[512,512]{1,0:T(8,128)}, f32[512,512]{1,0:T(8,128)}) custom-call(f32[512,512]{1,0:T(8,128)} %get-tuple-element.18.xi_ref, f32[128,128]{1,0:T(8,128)} %get-tuple-element.19.ra_ref, f32[128,128]{1,0:T(8,128)} %get-tuple-element.20.rb_ref, f32[128,128]{1,0:T(8,128)} %get-tuple-element.21.rc_ref), custom_call_target="tpu_custom_call" | custom-call | flops 20000000000 | bytes 2097152 | tf_op jit(solution)/shard_map/factor3/pallas_call | solution.py:173
  205.5 0.9 copy-done.4
  206.5 8.8 %update.1 = f32[192,768]{1,0:T(8,128)} custom-call(s32[1]{0:T(128)} %bitcast.core_ref.refs_0_, f32[512,512]{1,0:T(8,128)} %get-tuple-element.23.refs_1_, f32[1536,128]{1,0:T(8,128)} %bitcast.7, f32[1536,128]{1,0:T(8,128)} %copy-done.4, f32[192,512]{1,0:T(8,128)} %refs_4_.1, f32[192,768]{1,0:T(8,128)} %refs_5_.1), custom_call_target="tpu_custom_call" | custom-call | flops 4000000000 | bytes 4194304 | tf_op jit(solution)/shard_map/update/pallas_call | solution.py:202
  (23 shorter events, 3.0 us)
Async XLA Ops:
  15.0 10.3 %collective-permute-start = (f32[768,128]{1,0:T(8,128)}, f32[768,128]{1,0:T(8,128)S(1)}, u32[]{:S(2)}, u32[]{:S(2)}) collective-permute-start(f32[768,128]{1,0:T(8,128)} %get-tuple-element.15), channel_id=1, source_target_pairs={{0,8},{8,0},{1,9},{9,1},{2,10},{10,2},{3,11},{11,3},{4,12},{12,4},... | collective-permute-start | bytes 1179656 | tf_op jit(solution)/shard_map/ppermute | solution.py:212
  26.3 28.9 %copy-start.3 = (f32[1536,128]{1,0:T(8,128)S(1)}, f32[1536,128]{1,0:T(8,128)}, u32[]{:S(2)}) copy-start(f32[1536,128]{1,0:T(8,128)} %get-tuple-element.25) | copy-start | bytes 2359300
  44.5 24.2 %copy-start.1 = (f32[1536,128]{1,0:T(8,128)S(1)}, f32[1536,128]{1,0:T(8,128)}, u32[]{:S(2)}) copy-start(f32[1536,128]{1,0:T(8,128)} %get-tuple-element.24) | copy-start | bytes 2359300
  45.2 17.6 %all-to-all-start.1 = ((f32[8,24,128]{2,1,0:T(8,128)}), f32[8,24,128]{2,1,0:T(8,128)S(1)}, u32[]{:S(2)}, u32[]{:S(2)}) async-start(f32[8,24,128]{2,1,0:T(8,128)} %broadcast_in_dim.8), calls=%async_computation.1 | async-start | bytes 196608 | tf_op jit(solution)/shard_map/all_to_all | solution.py:216
  55.2 13.5 %collective-permute-start.2 = (f32[1536,128]{1,0:T(8,128)S(1)}, f32[1536,128]{1,0:T(8,128)S(1)}, u32[]{:S(2)}, u32[]{:S(2)}) collective-permute-start(f32[1536,128]{1,0:T(8,128)S(1)} %copy-done.3), channel_id=1, source_target_pairs={{0,8},{8,0},{1,9},{9,1},{2,10},{10,2},{3,11},{11,3},{4,12},{12,4},... | collective-permute-start | bytes 2359304 | tf_op jit(solution)/shard_map/ppermute | solution.py:212
  63.6 16.5 %all-to-all-start.2 = ((f32[32,24,128]{2,1,0:T(8,128)}), f32[32,24,128]{2,1,0:T(8,128)S(1)}, u32[]{:S(2)}, u32[]{:S(2)}) async-start(f32[32,24,128]{2,1,0:T(8,128)} %broadcast_in_dim.9), calls=%async_computation.2 | async-start | bytes 786432 | tf_op jit(solution)/shard_map/all_to_all | solution.py:218
  80.1 5.8 %copy-start.2 = (f32[32,24,128]{2,1,0:T(8,128)}, f32[32,24,128]{2,1,0:T(8,128)S(1)}, u32[]{:S(2)}) copy-start(f32[32,24,128]{2,1,0:T(8,128)S(1)} %all-to-all-done.2) | copy-start | bytes 1179652
  80.1 24.3 %all-to-all-start.3 = ((f32[32,48,128]{2,1,0:T(8,128)}), f32[32,48,128]{2,1,0:T(8,128)S(1)}, u32[]{:S(2)}, u32[]{:S(2)}) async-start(f32[32,48,128]{2,1,0:T(8,128)} %bitcast.3), calls=%async_computation.3 | async-start | bytes 1572864 | tf_op jit(solution)/shard_map/all_to_all | solution.py:214
  85.9 24.8 %collective-permute-start.1 = (f32[768,128]{1,0:T(8,128)S(1)}, f32[768,128]{1,0:T(8,128)S(1)}, u32[]{:S(2)}, u32[]{:S(2)}) collective-permute-start(f32[768,128]{1,0:T(8,128)S(1)} %bitcast.8), channel_id=1, source_target_pairs={{0,8},{8,0},{1,9},{9,1},{2,10},{10,2},{3,11},{11,3},{4,12},{12,4},... | collective-permute-start | bytes 1179656 | tf_op jit(solution)/shard_map/ppermute | solution.py:220
  105.2 46.5 %all-to-all-start.4 = ((f32[8,48,128]{2,1,0:T(8,128)}), f32[8,48,128]{2,1,0:T(8,128)S(1)}, u32[]{:S(2)}, u32[]{:S(2)}) async-start(f32[8,48,128]{2,1,0:T(8,128)} %broadcast_in_dim.10), calls=%async_computation.4 | async-start | bytes 393216 | tf_op jit(solution)/shard_map/all_to_all | solution.py:216
  110.8 0.7 copy-start.5
  152.6 26.7 %all-to-all-start.5 = ((f32[32,48,128]{2,1,0:T(8,128)}), f32[32,48,128]{2,1,0:T(8,128)S(1)}, u32[]{:S(2)}, u32[]{:S(2)}) async-start(f32[32,48,128]{2,1,0:T(8,128)} %broadcast_in_dim.11), calls=%async_computation.5 | async-start | bytes 1572864 | tf_op jit(solution)/shard_map/all_to_all | solution.py:218
  179.3 26.2 %copy-start = (f32[32,48,128]{2,1,0:T(8,128)}, f32[32,48,128]{2,1,0:T(8,128)S(1)}, u32[]{:S(2)}) copy-start(f32[32,48,128]{2,1,0:T(8,128)S(1)} %all-to-all-done.5) | copy-start | bytes 2359300
  179.3 26.2 %collective-permute-start.3 = (f32[1536,128]{1,0:T(8,128)S(1)}, f32[1536,128]{1,0:T(8,128)S(1)}, u32[]{:S(2)}, u32[]{:S(2)}) collective-permute-start(f32[1536,128]{1,0:T(8,128)S(1)} %bitcast.6), channel_id=1, source_target_pairs={{0,8},{8,0},{1,9},{9,1},{2,10},{10,2},{3,11},{11,3},{4,12},{12,4},... | collective-permute-start | bytes 2359304 | tf_op jit(solution)/shard_map/ppermute | solution.py:220
  205.5 0.9 copy-start.4

commit v2 on v1

v2 whole, which is shorter than its diff:
```python
import jax
import jax.numpy as jnp
from jax import lax
from jax.experimental import pallas as pl
from jax.experimental.pallas import tpu as pltpu
from jax.sharding import Mesh, PartitionSpec as P

HI = lax.Precision.HIGHEST
B = 128
NP = 4
NC = 6
G_BLOCKS = [(i, j) for i in range(NP) for j in range(i, NP)]
C_BLOCKS = [(i, j) for i in range(NP) for j in range(NC)]
G_HALF = 6
C_HALF = 12
VM = pl.BlockSpec(memory_space=pltpu.VMEM)
SM = pl.BlockSpec(memory_space=pltpu.SMEM)


def split_half(blocks):
    n = (len(blocks) + 1) // 2
    return [(b, 0 if k < n else 1, k if k < n else k - n) for k, b in enumerate(blocks)]


PARTS = 32
G_ROWS = G_HALF * B // PARTS
C_ROWS = C_HALF * B // PARTS


def gram_kernel(core_ref, a_ref, t_ref, keep_ref, send_ref):
    g_place = {b: (owner, slot) for b, owner, slot in split_half(G_BLOCKS)}
    c_place = {b: (owner, slot) for b, owner, slot in split_half(C_BLOCKS)}

    def put(ref, value, slot, start, rows):
        for p in range(0, B, 8):
            part, at = divmod(slot * B + p, rows)
            ref[part, start + at : start + at + 8, :] = value[p : p + 8]

    def fill(me):
        refs = (keep_ref, send_ref) if me == 0 else (send_ref, keep_ref)
        for i in range(NP):
            left = a_ref[:, i * B : (i + 1) * B]
            g = dot_t(left, a_ref[:, i * B :])
            for j in range(i, NP):
                owner, slot = g_place[(i, j)]
                put(refs[owner], g[:, (j - i) * B : (j - i + 1) * B], slot, 0, G_ROWS)
            c = dot_t(left, t_ref[...])
            for j in range(NC):
                owner, slot = c_place[(i, j)]
                put(refs[owner], c[:, j * B : (j + 1) * B], slot, G_ROWS, C_ROWS)
        for ref in refs:
            put(ref, jnp.zeros((B, B), jnp.float32), G_HALF - 1, 0, G_ROWS)

    for me in range(2):
        pl.when(core_ref[0] == me)(lambda me=me: fill(me))


def gram(core, a, t):
    out = jax.ShapeDtypeStruct((PARTS, G_ROWS + C_ROWS, B), jnp.float32)
    return pl.pallas_call(
        gram_kernel,
        out_shape=(out, out),
        in_specs=[SM, VM, VM],
        out_specs=[VM] * 2,
        cost_estimate=pl.CostEstimate(flops=2 * 192 * 512 * 1280, bytes_accessed=4 << 20, transcendentals=0),
        name="gram",
    )(core, a, t)


def stack_pieces(u, order):
    high = u.astype(jnp.bfloat16).astype(jnp.float32)
    rest = u - high
    mid = rest.astype(jnp.bfloat16).astype(jnp.float32)
    part = (high, mid, rest - mid)
    return jnp.concatenate([part[k] for k in order], axis=0).astype(jnp.bfloat16)


LEFT = (0, 0, 1, 0, 2, 1)
RIGHT = (0, 1, 0, 2, 0, 1)


def row_of(v, t):
    return jnp.broadcast_to(v[t : t + 1, :], v.shape)


def eliminate_rows(w_rows, v_rows, base):
    sub = lax.broadcasted_iota(jnp.int32, (8, B), 0)
    d = {}
    for k in range(8):
        col = jnp.take_along_axis(w_rows, jnp.full((8, B), base + k, jnp.int32), axis=1, mode="promise_in_bounds")
        for i in range(k + 1):
            d[i, k] = row_of(col, i)
    w = [row_of(w_rows, t) for t in range(8)]
    v = [row_of(v_rows, t) for t in range(8)]
    for t in range(8):
        inv = lax.rsqrt(d[t, t])
        u = {k: d[t, k] * inv for k in range(t + 1, 8)}
        for i in range(t + 1, 8):
            for k in range(i, 8):
                d[i, k] = d[i, k] - u[i] * u[k]
        w[t] = w[t] * inv
        v[t] = v[t] * inv
        for i in range(t + 1, 8):
            w[i] = w[i] - u[i] * w[t]
            v[i] = v[i] - u[i] * v[t]
    wo, vo = w[0], v[0]
    for t in range(1, 8):
        wo = jnp.where(sub == t, w[t], wo)
        vo = jnp.where(sub == t, v[t], vo)
    return wo, vo


def diag_factor(s, e, rkk):
    lane = lax.broadcasted_iota(jnp.int32, (8, B), 1)
    sub = lax.broadcasted_iota(jnp.int32, (8, B), 0)
    e[...] = jnp.where(
        lax.broadcasted_iota(jnp.int32, (B, B), 0) == lax.broadcasted_iota(jnp.int32, (B, B), 1), 1.0, 0.0
    ).astype(jnp.float32)

    def body(g, _):
        base = pl.multiple_of(g * 8, 8)
        rows = pl.ds(base, 8)
        u, v = eliminate_rows(s[rows, :], e[rows, :], base)
        rkk[rows, :] = jnp.where(lane >= sub + base, u, 0.0)
        left = stack_pieces(jnp.where(lane >= base + 8, u, 0.0), LEFT)
        right = jnp.concatenate([stack_pieces(u, RIGHT), stack_pieces(v, RIGHT)], axis=1)
        change = lax.dot_general(left, right, (((0,), (0,)), ((), ())), preferred_element_type=jnp.float32)
        s[...] = s[...] - change[:, :B]
        e[...] = e[...] - change[:, B:]
        e[rows, :] = v
        return 0

    lax.fori_loop(0, B // 8, body, 0)


def dot(x, y):
    return jnp.dot(x, y, precision=HI, preferred_element_type=jnp.float32)


def dot_t(x, y):
    return lax.dot_general(x, y, (((0,), (0,)), ((), ())), precision=HI, preferred_element_type=jnp.float32)


def panel_step(k, x, rkk, s, lkk):
    r0 = k * B
    r1 = r0 + B
    s[...] = x[r0:r1, r0:r1]
    diag_factor(s, lkk, rkk)
    linv = lkk[...]
    if k > 0:
        x[r0:r1, :r0] = dot(linv, x[r0:r1, :r0])
    if k < NP - 1:
        x[r0:r1, r1:] = dot(linv, x[r0:r1, r1:])
    x[r0:r1, r0:r1] = linv
    for i in range(k + 1, NP):
        c0 = i * B
        left = x[r0:r1, c0 : c0 + B]
        x[c0 : c0 + B, c0:] = x[c0 : c0 + B, c0:] - dot_t(left, x[r0:r1, c0:])
        low = dot_t(left, x[r0:r1, :r1])
        if k > 0:
            x[c0 : c0 + B, :r0] = x[c0 : c0 + B, :r0] - low[:, :r0]
        x[c0 : c0 + B, r0:r1] = -low[:, r0:]


def first_kernel(row_count, core_ref, gm_ref, go_ref, x_ref, r_ref, s, lkk):
    core = core_ref[0]
    scale = 1.0 / row_count
    x_ref[...] = jnp.zeros_like(x_ref)
    for (i, j), owner, slot in split_half(G_BLOCKS):
        rows = slice(slot * B, (slot + 1) * B)
        value = jnp.where(core == owner, gm_ref[rows, :], go_ref[rows, :])
        x_ref[i * B : (i + 1) * B, j * B : (j + 1) * B] = value * scale
    panel_step(0, x_ref, r_ref, s, lkk)


def mid_kernel(k, xi_ref, x_ref, r_ref, s, lkk):
    x_ref[...] = xi_ref[...]
    panel_step(k, x_ref, r_ref, s, lkk)


def last_kernel(xi_ref, ra_ref, rb_ref, rc_ref, x_ref, r_ref, rkk, s, lkk):
    x_ref[...] = xi_ref[...]
    panel_step(NP - 1, x_ref, rkk, s, lkk)
    r_ref[...] = jnp.zeros_like(r_ref)
    for i, ref in enumerate((ra_ref, rb_ref, rc_ref, rkk)):
        r_ref[i * B : (i + 1) * B, i * B : (i + 1) * B] = ref[...]
        if i < NP - 1:
            r_ref[i * B : (i + 1) * B, (i + 1) * B :] = x_ref[i * B : (i + 1) * B, (i + 1) * B :]


def factor(row_count, core, gm, go):
    full = jax.ShapeDtypeStruct((NP * B, NP * B), jnp.float32)
    block = jax.ShapeDtypeStruct((B, B), jnp.float32)
    scratch = pltpu.VMEM((B, B), jnp.float32)
    cost = pl.CostEstimate(flops=4_000_000_000, bytes_accessed=2 << 20, transcendentals=0)
    x, ra = pl.pallas_call(
        lambda *refs: first_kernel(row_count, *refs),
        out_shape=(full, block), in_specs=[SM, VM, VM], out_specs=[VM, VM],
        scratch_shapes=[scratch] * 2, cost_estimate=cost, name="factor0",
    )(core, gm, go)
    diag = [ra]
    for k in (1, 2):
        x, rk = pl.pallas_call(
            lambda *refs, k=k: mid_kernel(k, *refs),
            out_shape=(full, block), in_specs=[VM], out_specs=[VM, VM],
            scratch_shapes=[scratch] * 2, cost_estimate=cost,
        )(x)
        diag.append(rk)
    return pl.pallas_call(
        last_kernel,
        out_shape=(full, full), in_specs=[VM] * 4, out_specs=[VM, VM],
        scratch_shapes=[scratch] * 3, cost_estimate=cost, name="factor3",
    )(x, *diag)


def update_kernel(row_count, core_ref, x_ref, cm_ref, co_ref, a_ref, t_ref, out_ref, q, p):
    core = core_ref[0]
    scale = 1.0 / row_count
    for i in range(NP):
        li = x_ref[i * B : (i + 1) * B, : (i + 1) * B]
        q[:, i * B : (i + 1) * B] = lax.dot_general(
            a_ref[:, : (i + 1) * B], li, (((1,), (1,)), ((), ())), precision=HI, preferred_element_type=jnp.float32
        )
    c = {}
    for b, owner, slot in split_half(C_BLOCKS):
        rows = slice(slot * B, (slot + 1) * B)
        c[b] = jnp.where(core == owner, cm_ref[rows, :], co_ref[rows, :]) * scale
    for j in range(NC):
        col = jnp.concatenate([c[(i, j)] for i in range(NP)], axis=0)
        for i in range(NP):
            p[i * B : (i + 1) * B, j * B : (j + 1) * B] = dot(x_ref[i * B : (i + 1) * B, : (i + 1) * B], col[: (i + 1) * B])
    for j in range(NC):
        cols = slice(j * B, (j + 1) * B)
        out_ref[:, cols] = t_ref[:, cols] - dot(q[...], p[:, cols])


def update(row_count, core, x, cm, co, a, t):
    return pl.pallas_call(
        lambda *refs: update_kernel(row_count, *refs),
        out_shape=jax.ShapeDtypeStruct(t.shape, jnp.float32),
        in_specs=[SM] + [VM] * 5, out_specs=VM,
        scratch_shapes=[pltpu.VMEM(a.shape, jnp.float32), pltpu.VMEM((NP * B, NC * B), jnp.float32)],
        cost_estimate=pl.CostEstimate(flops=4_000_000_000, bytes_accessed=4 << 20, transcendentals=0), name="update",
    )(core, x, cm, co, a, t)


def reduce_over_devices(keep, send):
    half = keep + lax.ppermute(send, "c", [(0, 1), (1, 0)])
    mine = jnp.sum(lax.all_to_all(half, ("y", "x"), 0, 0), axis=0)
    parts = lax.all_to_all(jnp.broadcast_to(mine[None], (8,) + mine.shape), "z", 0, 0)
    return jnp.sum(parts, axis=0)


def spread(mine):
    half = lax.all_to_all(jnp.broadcast_to(mine[None], (PARTS,) + mine.shape), ("y", "x"), 0, 0)
    half = half.reshape(-1, B)
    return half, lax.ppermute(half, "c", [(0, 1), (1, 0)])


def local(row_count, panel_block, trailing):
    core = lax.axis_index("c").astype(jnp.int32).reshape(1)
    mine = reduce_over_devices(*gram(core, panel_block, trailing))
    gm, go = spread(mine[:G_ROWS])
    cm, co = spread(mine[G_ROWS:])
    x, r = factor(row_count, core, gm, go)
    return r, update(row_count, core, x, cm, co, panel_block, trailing)


def solution(mesh):
    fine = Mesh(mesh.devices.reshape(8, 4, 2, 8), ("y", "x", "c", "z"))
    axes = ("y", "x", "c", "z")

    def run(panel_block, trailing):
        rows = panel_block.shape[0]
        f = jax.shard_map(
            lambda a, t: local(rows, a, t),
            mesh=fine,
            in_specs=(P(axes, None), P(axes, None)),
            out_specs=(P(), P(axes, None)),
            check_vma=False,
        )
        return f(panel_block, trailing)

    return run
```

time: 216 us -> 160 us (0.74)
  Pallas kernels: 103 us -> 48.1 us
  blocking collectives: 18.1 us -> 56.6 us
  starting transfers between devices: 58.2 us -> 31.6 us
  waiting for transfers between devices: 28.2 us -> 17.8 us
    all_to_all x1 -> x2, blocking collectives: 18.1 us -> 56.6 us  [the longest x1 36.5 us: reduce_over_devices(): mine = jnp.sum(lax.all_to_all(half, ('y', 'x'), 0, 0), axis=0)]
    all_to_all x5 -> x2, starting transfers between devices: 33.2 us -> 9.91 us  [spread(): lax.all_to_all(jnp.broadcast_to(mine[None], (PARTS,) + mine.shape), ('y',...]
    pallas_call x2, Pallas kernels: 40 us -> 17.4 us  [factor(): pl.pallas_call(lambda *refs, k=k: mid_kernel(k, *refs), out_shape=(full,...]
    all_to_all x5 -> x2, waiting for transfers between devices: 26.7 us -> 13.8 us  [spread(): lax.all_to_all(jnp.broadcast_to(mine[None], (PARTS,) + mine.shape), ('y',...]
    pallas_call x1, Pallas kernels: 19.9 us -> 8.47 us  [factor(): pl.pallas_call(last_kernel, out_shape=(full, full), in_specs=[VM] * 4, ou...]
    pallas_call x1, Pallas kernels: 20.1 us -> 8.79 us  [factor(): pl.pallas_call(lambda *refs: first_kernel(row_count, *refs), out_shape=(f...]
    pallas_call x1, Pallas kernels: 14.3 us -> 4.69 us  [gram(): pl.pallas_call(gram_kernel, out_shape=(out, out), in_specs=[SM, VM, VM],...]
    ppermute x4 -> x3, starting transfers between devices: 24.9 us -> 21.7 us  [the longest x2 13 us: spread(): return (half, lax.ppermute(half, 'c', [(0, 1), (1, 0)]))]
  transfers between devices with their start and end apart: 9 -> 5, of which waited for: 4 -> 4; matrix products, arithmetic and copies ran while one was open for 1% -> 0% of each run, Pallas kernels for 37% -> 22%
where the time goes in v2:
time: 160 us
  blocking collectives  56.6 us (35%)
  Pallas kernels  48.1 us (30%)
  starting transfers between devices  31.6 us (20%)
  waiting for transfers between devices  17.8 us (11%)
  local copies, waits for them, and re-layouts  3.48 us (2%)
    all_to_all x1, blocking collectives, reduce_over_devices(): mine = jnp.sum(lax.all_to_all(half, ('y', 'x'), 0, 0), axis=0)  36.5 us
    all_to_all x1, blocking collectives, reduce_over_devices(): lax.all_to_all(jnp.broadcast_to(mine[None], (8,) + mine.shape), 'z', 0, 0)  20.1 us
    pallas_call x2, Pallas kernels, factor(): pl.pallas_call(lambda *refs, k=k: mid_kernel(k, *refs), out_shape=(full,...  17.4 us
    all_to_all x2, waiting for transfers between devices, spread(): lax.all_to_all(jnp.broadcast_to(mine[None], (PARTS,) + mine.shape), ('y',...  13.8 us
    ppermute x2, starting transfers between devices, spread(): return (half, lax.ppermute(half, 'c', [(0, 1), (1, 0)]))  13 us
    all_to_all x2, starting transfers between devices, spread(): lax.all_to_all(jnp.broadcast_to(mine[None], (PARTS,) + mine.shape), ('y',...  9.91 us
    pallas_call x1, Pallas kernels, update(): pl.pallas_call(lambda *refs: update_kernel(row_count, *refs), out_shape=j...  8.83 us
    pallas_call x1, Pallas kernels, factor(): pl.pallas_call(lambda *refs: first_kernel(row_count, *refs), out_shape=(f...  8.79 us
  transfers between devices with their start and end apart: 5, of which 4 were waited for; matrix products, arithmetic and copies ran while one was open for 0% of the time, Pallas kernels for 22%

profile of v2, /device:TPU:1, one launch (start us, length us, event | category | flops | bytes accessed | tf_op | source)
XLA Modules:
  0.0 159.8 jit_solution(2214663193930558235)
XLA Ops:
  0.6 4.7 %gram.1 = (f32[32,72,128]{2,1,0:T(8,128)}, f32[32,72,128]{2,1,0:T(8,128)}) custom-call(s32[1]{0:T(128)} %bitcast.core_ref.refs_0_, f32[192,512]{1,0:T(8,128)} %refs_4_.1, f32[192,768]{1,0:T(8,128)} %refs_5_.1), custom_call_target="tpu_custom_call" | custom-call | flops 251658240 | bytes 4194304 | tf_op jit(solution)/shard_map/gram/pallas_call | solution.py:60
  5.3 8.7 %collective-permute-start = (f32[32,72,128]{2,1,0:T(8,128)}, f32[32,72,128]{2,1,0:T(8,128)S(1)}, u32[]{:S(2)}, u32[]{:S(2)}) collective-permute-start(f32[32,72,128]{2,1,0:T(8,128)} %get-tuple-element.13), channel_id=1, source_target_pairs={{0,8},{8,0},{1,9},{9,1},{2,10},{10,2},{3,11},{11,3},{4,12},{12,4},... | collective-permute-start | bytes 3538952 | tf_op jit(solution)/shard_map/ppermute | solution.py:248
  14.1 2.7 %collective-permute-done = f32[32,72,128]{2,1,0:T(8,128)S(1)} collective-permute-done((f32[32,72,128]{2,1,0:T(8,128)}, f32[32,72,128]{2,1,0:T(8,128)S(1)}, u32[]{:S(2)}, u32[]{:S(2)}) %collective-permute-start) | collective-permute-done | bytes 1179680 | tf_op jit(solution)/shard_map/ppermute | solution.py:248
  16.7 1.4 add.3
  18.1 36.5 %all_to_all.20 = f32[32,72,128]{2,1,0:T(8,128)S(1)} all-to-all(f32[32,72,128]{2,1,0:T(8,128)S(1)} %add.3), channel_id=1, replica_groups=mesh['y'=8,'x'=4,'c'=2,'z'=8] {'y','x'}, dimensions={0} | all-to-all | bytes 2359296 | tf_op jit(solution)/shard_map/all_to_all | solution.py:249
  54.6 0.1 reduce_sum.18
  54.7 20.1 %all_to_all.21 = f32[8,72,128]{2,1,0:T(8,128)S(1)} all-to-all(f32[8,72,128]{2,1,0:T(8,128)S(1)} %broadcast_in_dim.6), channel_id=1, replica_groups=mesh['y'=8,'x'=4,'c'=2,'z'=8] {'z'}, dimensions={0} | all-to-all | bytes 589824 | tf_op jit(solution)/shard_map/all_to_all | solution.py:250
  74.9 0.8 broadcast_in_dim.7
  75.6 4.1 %all-to-all-start.2 = ((f32[32,24,128]{2,1,0:T(8,128)}), f32[32,24,128]{2,1,0:T(8,128)S(1)}, u32[]{:S(2)}, u32[]{:S(2)}) async-start(f32[32,24,128]{2,1,0:T(8,128)} %broadcast_in_dim.7), calls=%async_computation.2 | async-start | bytes 786432 | tf_op jit(solution)/shard_map/all_to_all | solution.py:255
  79.7 11.4 %all-to-all-done.2 = f32[32,24,128]{2,1,0:T(8,128)S(1)} async-done(((f32[32,24,128]{2,1,0:T(8,128)}), f32[32,24,128]{2,1,0:T(8,128)S(1)}, u32[]{:S(2)}, u32[]{:S(2)}) %all-to-all-start.2) | async-done | bytes 393248 | tf_op jit(solution)/shard_map/all_to_all | solution.py:255
  91.2 1.0 broadcast_in_dim.8
  92.1 5.8 %all-to-all-start.3 = ((f32[32,48,128]{2,1,0:T(8,128)}), f32[32,48,128]{2,1,0:T(8,128)S(1)}, u32[]{:S(2)}, u32[]{:S(2)}) async-start(f32[32,48,128]{2,1,0:T(8,128)} %broadcast_in_dim.8), calls=%async_computation.3 | async-start | bytes 1572864 | tf_op jit(solution)/shard_map/all_to_all | solution.py:255
  98.0 5.3 %collective-permute-start.1 = (f32[768,128]{1,0:T(8,128)S(1)}, f32[768,128]{1,0:T(8,128)S(1)}, u32[]{:S(2)}, u32[]{:S(2)}) collective-permute-start(f32[768,128]{1,0:T(8,128)S(1)} %bitcast.5), channel_id=1, source_target_pairs={{0,8},{8,0},{1,9},{9,1},{2,10},{10,2},{3,11},{11,3},{4,12},{12,4},... | collective-permute-start | bytes 1179656 | tf_op jit(solution)/shard_map/ppermute | solution.py:257
  103.3 1.3 collective-permute-done.1.refs_2_
  104.6 0.8 copy-done.3
  105.4 8.8 %factor0.1 = (f32[512,512]{1,0:T(8,128)}, f32[128,128]{1,0:T(8,128)}) custom-call(s32[1]{0:T(128)} %bitcast.core_ref.refs_0_, f32[768,128]{1,0:T(8,128)} %bitcast.6, f32[768,128]{1,0:T(8,128)} %copy-done.3), custom_call_target="tpu_custom_call" | custom-call | flops 4000000000 | bytes 2097152 | tf_op jit(solution)/shard_map/factor0/pallas_call | solution.py:196
  114.2 2.4 %all-to-all-done.3 = f32[32,48,128]{2,1,0:T(8,128)S(1)} async-done(((f32[32,48,128]{2,1,0:T(8,128)}), f32[32,48,128]{2,1,0:T(8,128)S(1)}, u32[]{:S(2)}, u32[]{:S(2)}) %all-to-all-start.3) | async-done | bytes 786464 | tf_op jit(solution)/shard_map/all_to_all | solution.py:255
  116.5 7.7 %collective-permute-start.2 = (f32[1536,128]{1,0:T(8,128)S(1)}, f32[1536,128]{1,0:T(8,128)S(1)}, u32[]{:S(2)}, u32[]{:S(2)}) collective-permute-start(f32[1536,128]{1,0:T(8,128)S(1)} %bitcast.3), channel_id=1, source_target_pairs={{0,8},{8,0},{1,9},{9,1},{2,10},{10,2},{3,11},{11,3},{4,12},{12,4},... | collective-permute-start | bytes 2359304 | tf_op jit(solution)/shard_map/ppermute | solution.py:257
  124.2 8.8 %shard_map.41 = (f32[512,512]{1,0:T(8,128)}, f32[128,128]{1,0:T(8,128)}) custom-call(f32[512,512]{1,0:T(8,128)} %get-tuple-element.14.refs_0_), custom_call_target="tpu_custom_call" | custom-call | flops 4000000000 | bytes 2097152 | tf_op jit(solution)/shard_map/pallas_call | solution.py:203
  133.0 8.6 %shard_map.42 = (f32[512,512]{1,0:T(8,128)}, f32[128,128]{1,0:T(8,128)}) custom-call(f32[512,512]{1,0:T(8,128)} %get-tuple-element.15.refs_0_), custom_call_target="tpu_custom_call" | custom-call | flops 4000000000 | bytes 2097152 | tf_op jit(solution)/shard_map/pallas_call | solution.py:203
  141.6 8.5 %factor3.1 = (f32[512,512]{1,0:T(8,128)}, f32[512,512]{1,0:T(8,128)}) custom-call(f32[512,512]{1,0:T(8,128)} %get-tuple-element.16.xi_ref, f32[128,128]{1,0:T(8,128)} %get-tuple-element.17.ra_ref, f32[128,128]{1,0:T(8,128)} %get-tuple-element.18.rb_ref, f32[128,128]{1,0:T(8,128)} %get-tuple-element.19.rc_ref), custom_call_target="tpu_custom_call" | custom-call | flops 4000000000 | bytes 2097152 | tf_op jit(solution)/shard_map/factor3/pallas_call | solution.py:209
  150.0 0.0 collective-permute-done.2.refs_3_
  150.1 0.9 copy-done.2
  151.0 8.8 %update.1 = f32[192,768]{1,0:T(8,128)} custom-call(s32[1]{0:T(128)} %bitcast.core_ref.refs_0_, f32[512,512]{1,0:T(8,128)} %get-tuple-element.21.refs_1_, f32[1536,128]{1,0:T(8,128)} %bitcast.4, f32[1536,128]{1,0:T(8,128)} %copy-done.2, f32[192,512]{1,0:T(8,128)} %refs_4_.1, f32[192,768]{1,0:T(8,128)} %refs_5_.1), custom_call_target="tpu_custom_call" | custom-call | flops 4000000000 | bytes 4194304 | tf_op jit(solution)/shard_map/update/pallas_call | solution.py:238
  (10 shorter events, 0.1 us)
Async XLA Ops:
  5.3 11.4 %collective-permute-start = (f32[32,72,128]{2,1,0:T(8,128)}, f32[32,72,128]{2,1,0:T(8,128)S(1)}, u32[]{:S(2)}, u32[]{:S(2)}) collective-permute-start(f32[32,72,128]{2,1,0:T(8,128)} %get-tuple-element.13), channel_id=1, source_target_pairs={{0,8},{8,0},{1,9},{9,1},{2,10},{10,2},{3,11},{11,3},{4,12},{12,4},... | collective-permute-start | bytes 3538952 | tf_op jit(solution)/shard_map/ppermute | solution.py:248
  75.6 15.5 %all-to-all-start.2 = ((f32[32,24,128]{2,1,0:T(8,128)}), f32[32,24,128]{2,1,0:T(8,128)S(1)}, u32[]{:S(2)}, u32[]{:S(2)}) async-start(f32[32,24,128]{2,1,0:T(8,128)} %broadcast_in_dim.7), calls=%async_computation.2 | async-start | bytes 786432 | tf_op jit(solution)/shard_map/all_to_all | solution.py:255
  91.2 6.8 %copy-start.1 = (f32[32,24,128]{2,1,0:T(8,128)}, f32[32,24,128]{2,1,0:T(8,128)S(1)}, u32[]{:S(2)}) copy-start(f32[32,24,128]{2,1,0:T(8,128)S(1)} %all-to-all-done.2) | copy-start | bytes 1179652
  92.1 24.4 %all-to-all-start.3 = ((f32[32,48,128]{2,1,0:T(8,128)}), f32[32,48,128]{2,1,0:T(8,128)S(1)}, u32[]{:S(2)}, u32[]{:S(2)}) async-start(f32[32,48,128]{2,1,0:T(8,128)} %broadcast_in_dim.8), calls=%async_computation.3 | async-start | bytes 1572864 | tf_op jit(solution)/shard_map/all_to_all | solution.py:255
  98.0 6.6 %collective-permute-start.1 = (f32[768,128]{1,0:T(8,128)S(1)}, f32[768,128]{1,0:T(8,128)S(1)}, u32[]{:S(2)}, u32[]{:S(2)}) collective-permute-start(f32[768,128]{1,0:T(8,128)S(1)} %bitcast.5), channel_id=1, source_target_pairs={{0,8},{8,0},{1,9},{9,1},{2,10},{10,2},{3,11},{11,3},{4,12},{12,4},... | collective-permute-start | bytes 1179656 | tf_op jit(solution)/shard_map/ppermute | solution.py:257
  104.6 0.8 copy-start.3
  116.5 16.5 %copy-start = (f32[32,48,128]{2,1,0:T(8,128)}, f32[32,48,128]{2,1,0:T(8,128)S(1)}, u32[]{:S(2)}) copy-start(f32[32,48,128]{2,1,0:T(8,128)S(1)} %all-to-all-done.3) | copy-start | bytes 2359300
  116.5 33.5 %collective-permute-start.2 = (f32[1536,128]{1,0:T(8,128)S(1)}, f32[1536,128]{1,0:T(8,128)S(1)}, u32[]{:S(2)}, u32[]{:S(2)}) collective-permute-start(f32[1536,128]{1,0:T(8,128)S(1)} %bitcast.3), channel_id=1, source_target_pairs={{0,8},{8,0},{1,9},{9,1},{2,10},{10,2},{3,11},{11,3},{4,12},{12,4},... | collective-permute-start | bytes 2359304 | tf_op jit(solution)/shard_map/ppermute | solution.py:257
  150.0 0.9 copy-start.2

commit v3 on v2

--- a/solution.py
+++ b/solution.py
@@ -162,97 +162,114 @@
         x[c0 : c0 + B, r0:r1] = -low[:, r0:]
 
 
-def first_kernel(row_count, core_ref, gm_ref, go_ref, x_ref, r_ref, s, lkk):
-    core = core_ref[0]
+LAST = NP - 1
+
+
+def first_kernel(row_count, core_ref, gm_ref, go_ref, x_ref, d_ref, s, lkk):
     scale = 1.0 / row_count
-    x_ref[...] = jnp.zeros_like(x_ref)
-    for (i, j), owner, slot in split_half(G_BLOCKS):
-        rows = slice(slot * B, (slot + 1) * B)
-        value = jnp.where(core == owner, gm_ref[rows, :], go_ref[rows, :])
-        x_ref[i * B : (i + 1) * B, j * B : (j + 1) * B] = value * scale
-    panel_step(0, x_ref, r_ref, s, lkk)
-
-
-def mid_kernel(k, xi_ref, x_ref, r_ref, s, lkk):
-    x_ref[...] = xi_ref[...]
-    panel_step(k, x_ref, r_ref, s, lkk)
-
-
-def last_kernel(xi_ref, ra_ref, rb_ref, rc_ref, x_ref, r_ref, rkk, s, lkk):
-    x_ref[...] = xi_ref[...]
-    panel_step(NP - 1, x_ref, rkk, s, lkk)
-    r_ref[...] = jnp.zeros_like(r_ref)
-    for i, ref in enumerate((ra_ref, rb_ref, rc_ref, rkk)):
-        r_ref[i * B : (i + 1) * B, i * B : (i + 1) * B] = ref[...]
-        if i < NP - 1:
-            r_ref[i * B : (i + 1) * B, (i + 1) * B :] = x_ref[i * B : (i + 1) * B, (i + 1) * B :]
+    for me in range(2):
+
+        @pl.when(core_ref[0] == me)
+        def _(me=me):
+            refs = (gm_ref, go_ref) if me == 0 else (go_ref, gm_ref)
+            for (i, j), owner, slot in split_half(G_BLOCKS):
+                x_ref[i * B : (i + 1) * B, j * B : (j + 1) * B] = refs[owner][slot * B : (slot + 1) * B, :] * scale
+
+    for i in range(NP):
+        for j in range(i):
+            x_ref[i * B : (i + 1) * B, j * B : (j + 1) * B] = jnp.zeros((B, B), jnp.float32)
+    for k in range(LAST):
+        panel_step(k, x_ref, d_ref.at[pl.ds(k * B, B), :], s, lkk)
+
+
+def last_kernel(xi_ref, d_ref, li_ref, r_ref, rkk, s, lkk):
+    r0 = LAST * B
+    for i in range(LAST):
+        rows = slice(i * B, (i + 1) * B)
+        r_ref[rows, :] = xi_ref[rows, :]
+        r_ref[rows, rows] = d_ref[rows, :]
+        if i > 0:
+            r_ref[rows, : i * B] = jnp.zeros((B, i * B), jnp.float32)
+    li_ref[...] = xi_ref[...]
+    panel_step(LAST, li_ref, rkk, s, lkk)
+    r_ref[r0:, :r0] = jnp.zeros((B, r0), jnp.float32)
+    r_ref[r0:, r0:] = rkk[...]
+    for i in (0, 2):
+        li_ref[i * B : (i + 1) * B, (i + 1) * B : (i + 2) * B] = jnp.zeros((B, B), jnp.float32)
 
 
 def factor(row_count, core, gm, go):
     full = jax.ShapeDtypeStruct((NP * B, NP * B), jnp.float32)
-    block = jax.ShapeDtypeStruct((B, B), jnp.float32)
     scratch = pltpu.VMEM((B, B), jnp.float32)
     cost = pl.CostEstimate(flops=4_000_000_000, bytes_accessed=2 << 20, transcendentals=0)
-    x, ra = pl.pallas_call(
+    x, d = pl.pallas_call(
         lambda *refs: first_kernel(row_count, *refs),
-        out_shape=(full, block), in_specs=[SM, VM, VM], out_specs=[VM, VM],
+        out_shape=(full, jax.ShapeDtypeStruct((LAST * B, B), jnp.float32)), in_specs=[SM, VM, VM], out_specs=[VM, VM],
         scratch_shapes=[scratch] * 2, cost_estimate=cost, name="factor0",
     )(core, gm, go)
-    diag = [ra]
-    for k in (1, 2):
-        x, rk = pl.pallas_call(
-            lambda *refs, k=k: mid_kernel(k, *refs),
-            out_shape=(full, block), in_specs=[VM], out_specs=[VM, VM],
-            scratch_shapes=[scratch] * 2, cost_estimate=cost,
-        )(x)
-        diag.append(rk)
     return pl.pallas_call(
         last_kernel,
-        out_shape=(full, full), in_specs=[VM] * 4, out_specs=[VM, VM],
+        out_shape=(full, full), in_specs=[VM] * 2, out_specs=[VM, VM],
         scratch_shapes=[scratch] * 3, cost_estimate=cost, name="factor3",
-    )(x, *diag)
-
-
-def update_kernel(row_count, core_ref, x_ref, cm_ref, co_ref, a_ref, t_ref, out_ref, q, p):
-    core = core_ref[0]
+    )(x, d)
+
+
+def update_kernel(row_count, core_ref, x_ref, cm_ref, co_ref, a_ref, t_ref, out_ref, c, q, p):
     scale = 1.0 / row_count
-    for i in range(NP):
-        li = x_ref[i * B : (i + 1) * B, : (i + 1) * B]
-        q[:, i * B : (i + 1) * B] = lax.dot_general(
-            a_ref[:, : (i + 1) * B], li, (((1,), (1,)), ((), ())), precision=HI, preferred_element_type=jnp.float32
+    h = NP * B // 2
+    for me in range(2):
+
+        @pl.when(core_ref[0] == me)
+        def _(me=me):
+            refs = (cm_ref, co_ref) if me == 0 else (co_ref, cm_ref)
+            for (i, j), owner, slot in split_half(C_BLOCKS):
+                c[i * B : (i + 1) * B, j * B : (j + 1) * B] = refs[owner][slot * B : (slot + 1) * B, :] * scale
+
+    for r0 in (0, h):
+        r1 = r0 + h
+        q[:, r0:r1] = lax.dot_general(
+            a_ref[:, :r1], x_ref[r0:r1, :r1], (((1,), (1,)), ((), ())), precision=HI, preferred_element_type=jnp.float32
         )
-    c = {}
-    for b, owner, slot in split_half(C_BLOCKS):
-        rows = slice(slot * B, (slot + 1) * B)
-        c[b] = jnp.where(core == owner, cm_ref[rows, :], co_ref[rows, :]) * scale
-    for j in range(NC):
-        col = jnp.concatenate([c[(i, j)] for i in range(NP)], axis=0)
-        for i in range(NP):
-            p[i * B : (i + 1) * B, j * B : (j + 1) * B] = dot(x_ref[i * B : (i + 1) * B, : (i + 1) * B], col[: (i + 1) * B])
-    for j in range(NC):
-        cols = slice(j * B, (j + 1) * B)
-        out_ref[:, cols] = t_ref[:, cols] - dot(q[...], p[:, cols])
+        p[r0:r1, :] = dot(x_ref[r0:r1, :r1], c[:r1, :])
+    out_ref[...] = t_ref[...] - dot(q[...], p[...])
 
 
 def update(row_count, core, x, cm, co, a, t):
+    wide = pltpu.VMEM((NP * B, NC * B), jnp.float32)
     return pl.pallas_call(
         lambda *refs: update_kernel(row_count, *refs),
         out_shape=jax.ShapeDtypeStruct(t.shape, jnp.float32),
         in_specs=[SM] + [VM] * 5, out_specs=VM,
-        scratch_shapes=[pltpu.VMEM(a.shape, jnp.float32), pltpu.VMEM((NP * B, NC * B), jnp.float32)],
+        scratch_shapes=[wide, pltpu.VMEM(a.shape, jnp.float32), wide],
         cost_estimate=pl.CostEstimate(flops=4_000_000_000, bytes_accessed=4 << 20, transcendentals=0), name="update",
     )(core, x, cm, co, a, t)
 
 
+ALL = ("y", "x", "c", "z")
+
+
+def device(y, x, c, z):
+    return ((y * 4 + x) * 2 + c) * 8 + z
+
+
+PLANES = [[device(y, x, 0, z) for y in range(8) for x in range(4)] for z in range(8)] + [
+    [device(y, x, 1, z) for z in range(8) for x in range(4)] for y in range(8)
+]
+LINES = [[device(y, x, 0, z) for z in range(8)] for y in range(8) for x in range(4)] + [
+    [device(y, x, 1, z) for y in range(8)] for z in range(8) for x in range(4)
+]
+
+
 def reduce_over_devices(keep, send):
     half = keep + lax.ppermute(send, "c", [(0, 1), (1, 0)])
-    mine = jnp.sum(lax.all_to_all(half, ("y", "x"), 0, 0), axis=0)
-    parts = lax.all_to_all(jnp.broadcast_to(mine[None], (8,) + mine.shape), "z", 0, 0)
+    mine = jnp.sum(lax.all_to_all(half, ALL, 0, 0, axis_index_groups=PLANES), axis=0)
+    parts = lax.all_to_all(jnp.broadcast_to(mine[None], (8,) + mine.shape), ALL, 0, 0, axis_index_groups=LINES)
     return jnp.sum(parts, axis=0)
 
 
 def spread(mine):
-    half = lax.all_to_all(jnp.broadcast_to(mine[None], (PARTS,) + mine.shape), ("y", "x"), 0, 0)
+    copies = jnp.broadcast_to(mine[None], (PARTS,) + mine.shape)
+    half = lax.all_to_all(copies, ALL, 0, 0, axis_index_groups=PLANES)
     half = half.reshape(-1, B)
     return half, lax.ppermute(half, "c", [(0, 1), (1, 0)])
 

time: 160 us -> 145 us (0.906)
  blocking collectives: 56.6 us -> 44.2 us
  Pallas kernels: 48.1 us -> 41.5 us
  waiting for transfers between devices: 17.8 us -> 23.4 us
  starting transfers between devices: 31.6 us -> 29.8 us
    pallas_call x3 -> x1, Pallas kernels: 25.8 us -> 8.49 us  [factor(): pl.pallas_call(last_kernel, out_shape=(full, full), in_specs=[VM] * 2, ou...]
    pallas_call x1, Pallas kernels: 8.79 us -> 21.6 us  [factor(): pl.pallas_call(lambda *refs: first_kernel(row_count, *refs), out_shape=(f...]
    all_to_all x2, blocking collectives: 56.6 us -> 44.2 us  [the longest x1 27.4 us: reduce_over_devices(): lax.all_to_all(half, ALL, 0, 0, axis_index_groups=PLANES)]
    all_to_all x2, waiting for transfers between devices: 13.8 us -> 20.8 us  [spread(): half = lax.all_to_all(copies, ALL, 0, 0, axis_index_groups=PLANES)]
    all_to_all x2, starting transfers between devices: 9.91 us -> 7.79 us  [spread(): half = lax.all_to_all(copies, ALL, 0, 0, axis_index_groups=PLANES)]
    pallas_call x1, Pallas kernels: 8.83 us -> 6.72 us  [update(): pl.pallas_call(lambda *refs: update_kernel(row_count, *refs), out_shape=j...]
  transfers between devices with their start and end apart: 5 -> 5, of which waited for: 4 -> 3; matrix products, arithmetic and copies ran while one was open for 0% -> 0% of each run, Pallas kernels for 22% -> 21%
where the time goes in v3:
time: 145 us
  blocking collectives  44.2 us (30%)
  Pallas kernels  41.5 us (29%)
  starting transfers between devices  29.8 us (21%)
  waiting for transfers between devices  23.4 us (16%)
  local copies, waits for them, and re-layouts  3.45 us (2%)
  other arithmetic  1.48 us (1%)
    all_to_all x1, blocking collectives, reduce_over_devices(): lax.all_to_all(half, ALL, 0, 0, axis_index_groups=PLANES)  27.4 us
    pallas_call x1, Pallas kernels, factor(): pl.pallas_call(lambda *refs: first_kernel(row_count, *refs), out_shape=(f...  21.6 us
    all_to_all x2, waiting for transfers between devices, spread(): half = lax.all_to_all(copies, ALL, 0, 0, axis_index_groups=PLANES)  20.8 us
    all_to_all x1, blocking collectives, reduce_over_devices(): lax.all_to_all(jnp.broadcast_to(mine[None], (8,) + mine.shape), ALL, 0, 0...  16.8 us
    ppermute x2, starting transfers between devices, spread(): return (half, lax.ppermute(half, 'c', [(0, 1), (1, 0)]))  13.2 us
    ppermute x1, starting transfers between devices, reduce_over_devices(): half = keep + lax.ppermute(send, 'c', [(0, 1), (1, 0)])  8.74 us
    pallas_call x1, Pallas kernels, factor(): pl.pallas_call(last_kernel, out_shape=(full, full), in_specs=[VM] * 2, ou...  8.49 us
    all_to_all x2, starting transfers between devices, spread(): half = lax.all_to_all(copies, ALL, 0, 0, axis_index_groups=PLANES)  7.79 us
  transfers between devices with their start and end apart: 5, of which 3 were waited for; matrix products, arithmetic and copies ran while one was open for 0% of the time, Pallas kernels for 21%

profile of v3, /device:TPU:1, one launch (start us, length us, event | category | flops | bytes accessed | tf_op | source)
XLA Modules:
  0.0 144.6 jit_solution(14357546648517386600)
XLA Ops:
  0.6 4.7 %gram.1 = (f32[32,72,128]{2,1,0:T(8,128)}, f32[32,72,128]{2,1,0:T(8,128)}) custom-call(s32[1]{0:T(128)} %bitcast.core_ref.refs_0_, f32[192,512]{1,0:T(8,128)} %refs_4_.1, f32[192,768]{1,0:T(8,128)} %refs_5_.1), custom_call_target="tpu_custom_call" | custom-call | flops 251658240 | bytes 4194304 | tf_op jit(solution)/shard_map/gram/pallas_call | solution.py:60
  5.3 8.7 %collective-permute-start = (f32[32,72,128]{2,1,0:T(8,128)}, f32[32,72,128]{2,1,0:T(8,128)S(1)}, u32[]{:S(2)}, u32[]{:S(2)}) collective-permute-start(f32[32,72,128]{2,1,0:T(8,128)} %get-tuple-element.9), channel_id=1, source_target_pairs={{0,8},{8,0},{1,9},{9,1},{2,10},{10,2},{3,11},{11,3},{4,12},{12,4},... | collective-permute-start | bytes 3538952 | tf_op jit(solution)/shard_map/ppermute | solution.py:264
  14.1 2.7 %collective-permute-done = f32[32,72,128]{2,1,0:T(8,128)S(1)} collective-permute-done((f32[32,72,128]{2,1,0:T(8,128)}, f32[32,72,128]{2,1,0:T(8,128)S(1)}, u32[]{:S(2)}, u32[]{:S(2)}) %collective-permute-start) | collective-permute-done | bytes 1179680 | tf_op jit(solution)/shard_map/ppermute | solution.py:264
  16.7 1.4 add.3
  18.1 27.4 %all_to_all.20 = f32[32,72,128]{2,1,0:T(8,128)S(1)} all-to-all(f32[32,72,128]{2,1,0:T(8,128)S(1)} %add.3), channel_id=1, replica_groups={{0,16,32,48,64,80,96,112,128,144,160,176,192,208,224,240,256,272,288,30..., dimensions={0} | all-to-all | bytes 2359296 | tf_op jit(solution)/shard_map/all_to_all | solution.py:265
  45.6 0.1 reduce_sum.18
  45.7 16.8 %all_to_all.21 = f32[8,72,128]{2,1,0:T(8,128)S(1)} all-to-all(f32[8,72,128]{2,1,0:T(8,128)S(1)} %broadcast_in_dim.6), channel_id=1, replica_groups={{0,1,2,3,4,5,6,7},{16,17,18,19,20,21,22,23},{32,33,34,35,36,37,38,39},{..., dimensions={0} | all-to-all | bytes 589824 | tf_op jit(solution)/shard_map/all_to_all | solution.py:266
  62.5 0.8 broadcast_in_dim.7
  63.3 3.9 %all-to-all-start.2 = ((f32[32,24,128]{2,1,0:T(8,128)}), f32[32,24,128]{2,1,0:T(8,128)S(1)}, u32[]{:S(2)}, u32[]{:S(2)}) async-start(f32[32,24,128]{2,1,0:T(8,128)} %broadcast_in_dim.7), calls=%async_computation.2 | async-start | bytes 786432 | tf_op jit(solution)/shard_map/all_to_all | solution.py:272
  67.2 11.8 %all-to-all-done.2 = f32[32,24,128]{2,1,0:T(8,128)S(1)} async-done(((f32[32,24,128]{2,1,0:T(8,128)}), f32[32,24,128]{2,1,0:T(8,128)S(1)}, u32[]{:S(2)}, u32[]{:S(2)}) %all-to-all-start.2) | async-done | bytes 393248 | tf_op jit(solution)/shard_map/all_to_all | solution.py:272
  79.0 1.0 broadcast_in_dim.8
  79.9 3.9 %all-to-all-start.3 = ((f32[32,48,128]{2,1,0:T(8,128)}), f32[32,48,128]{2,1,0:T(8,128)S(1)}, u32[]{:S(2)}, u32[]{:S(2)}) async-start(f32[32,48,128]{2,1,0:T(8,128)} %broadcast_in_dim.8), calls=%async_computation.3 | async-start | bytes 1572864 | tf_op jit(solution)/shard_map/all_to_all | solution.py:272
  83.9 0.0 copy-done.1
  83.9 6.2 %collective-permute-start.1 = (f32[768,128]{1,0:T(8,128)S(1)}, f32[768,128]{1,0:T(8,128)S(1)}, u32[]{:S(2)}, u32[]{:S(2)}) collective-permute-start(f32[768,128]{1,0:T(8,128)S(1)} %bitcast.5), channel_id=1, source_target_pairs={{0,8},{8,0},{1,9},{9,1},{2,10},{10,2},{3,11},{11,3},{4,12},{12,4},... | collective-permute-start | bytes 1179656 | tf_op jit(solution)/shard_map/ppermute | solution.py:274
  90.1 9.0 %all-to-all-done.3 = f32[32,48,128]{2,1,0:T(8,128)S(1)} async-done(((f32[32,48,128]{2,1,0:T(8,128)}), f32[32,48,128]{2,1,0:T(8,128)S(1)}, u32[]{:S(2)}, u32[]{:S(2)}) %all-to-all-start.3) | async-done | bytes 786464 | tf_op jit(solution)/shard_map/all_to_all | solution.py:272
  99.1 7.0 %collective-permute-start.2 = (f32[1536,128]{1,0:T(8,128)S(1)}, f32[1536,128]{1,0:T(8,128)S(1)}, u32[]{:S(2)}, u32[]{:S(2)}) collective-permute-start(f32[1536,128]{1,0:T(8,128)S(1)} %bitcast.3), channel_id=1, source_target_pairs={{0,8},{8,0},{1,9},{9,1},{2,10},{10,2},{3,11},{11,3},{4,12},{12,4},... | collective-permute-start | bytes 2359304 | tf_op jit(solution)/shard_map/ppermute | solution.py:274
  106.1 0.0 collective-permute-done.1.refs_2_
  106.1 0.0 copy-start.3
  106.1 0.7 copy-done.3
  106.8 21.6 %factor0.1 = (f32[512,512]{1,0:T(8,128)}, f32[384,128]{1,0:T(8,128)}) custom-call(s32[1]{0:T(128)} %bitcast.core_ref.refs_0_, f32[768,128]{1,0:T(8,128)} %bitcast.6, f32[768,128]{1,0:T(8,128)} %copy-done.3), custom_call_target="tpu_custom_call" | custom-call | flops 4000000000 | bytes 2097152 | tf_op jit(solution)/shard_map/factor0/pallas_call | solution.py:205
  128.4 8.5 %factor3.1 = (f32[512,512]{1,0:T(8,128)}, f32[512,512]{1,0:T(8,128)}) custom-call(f32[512,512]{1,0:T(8,128)} %get-tuple-element.10.xi_ref, f32[384,128]{1,0:T(8,128)} %get-tuple-element.11.d_ref), custom_call_target="tpu_custom_call" | custom-call | flops 4000000000 | bytes 2097152 | tf_op jit(solution)/shard_map/factor3/pallas_call | solution.py:210
  136.9 0.0 collective-permute-done.2.refs_3_
  136.9 0.9 copy-done.2
  137.8 6.7 %update.1 = f32[192,768]{1,0:T(8,128)} custom-call(s32[1]{0:T(128)} %bitcast.core_ref.refs_0_, f32[512,512]{1,0:T(8,128)} %get-tuple-element.13.refs_1_, f32[1536,128]{1,0:T(8,128)} %bitcast.4, f32[1536,128]{1,0:T(8,128)} %copy-done.2, f32[192,512]{1,0:T(8,128)} %refs_4_.1, f32[192,768]{1,0:T(8,128)} %refs_5_.1), custom_call_target="tpu_custom_call" | custom-call | flops 4000000000 | bytes 4194304 | tf_op jit(solution)/shard_map/update/pallas_call | solution.py:239
  (8 shorter events, 0.1 us)
Async XLA Ops:
  5.3 11.4 %collective-permute-start = (f32[32,72,128]{2,1,0:T(8,128)}, f32[32,72,128]{2,1,0:T(8,128)S(1)}, u32[]{:S(2)}, u32[]{:S(2)}) collective-permute-start(f32[32,72,128]{2,1,0:T(8,128)} %get-tuple-element.9), channel_id=1, source_target_pairs={{0,8},{8,0},{1,9},{9,1},{2,10},{10,2},{3,11},{11,3},{4,12},{12,4},... | collective-permute-start | bytes 3538952 | tf_op jit(solution)/shard_map/ppermute | solution.py:264
  63.3 15.7 %all-to-all-start.2 = ((f32[32,24,128]{2,1,0:T(8,128)}), f32[32,24,128]{2,1,0:T(8,128)S(1)}, u32[]{:S(2)}, u32[]{:S(2)}) async-start(f32[32,24,128]{2,1,0:T(8,128)} %broadcast_in_dim.7), calls=%async_computation.2 | async-start | bytes 786432 | tf_op jit(solution)/shard_map/all_to_all | solution.py:272
  78.9 4.9 %copy-start.1 = (f32[32,24,128]{2,1,0:T(8,128)}, f32[32,24,128]{2,1,0:T(8,128)S(1)}, u32[]{:S(2)}) copy-start(f32[32,24,128]{2,1,0:T(8,128)S(1)} %all-to-all-done.2) | copy-start | bytes 1179652
  79.9 19.2 %all-to-all-start.3 = ((f32[32,48,128]{2,1,0:T(8,128)}), f32[32,48,128]{2,1,0:T(8,128)S(1)}, u32[]{:S(2)}, u32[]{:S(2)}) async-start(f32[32,48,128]{2,1,0:T(8,128)} %broadcast_in_dim.8), calls=%async_computation.3 | async-start | bytes 1572864 | tf_op jit(solution)/shard_map/all_to_all | solution.py:272
  83.9 22.2 %collective-permute-start.1 = (f32[768,128]{1,0:T(8,128)S(1)}, f32[768,128]{1,0:T(8,128)S(1)}, u32[]{:S(2)}, u32[]{:S(2)}) collective-permute-start(f32[768,128]{1,0:T(8,128)S(1)} %bitcast.5), channel_id=1, source_target_pairs={{0,8},{8,0},{1,9},{9,1},{2,10},{10,2},{3,11},{11,3},{4,12},{12,4},... | collective-permute-start | bytes 1179656 | tf_op jit(solution)/shard_map/ppermute | solution.py:274
  99.1 29.3 %copy-start = (f32[32,48,128]{2,1,0:T(8,128)}, f32[32,48,128]{2,1,0:T(8,128)S(1)}, u32[]{:S(2)}) copy-start(f32[32,48,128]{2,1,0:T(8,128)S(1)} %all-to-all-done.3) | copy-start | bytes 2359300
  99.1 37.8 %collective-permute-start.2 = (f32[1536,128]{1,0:T(8,128)S(1)}, f32[1536,128]{1,0:T(8,128)S(1)}, u32[]{:S(2)}, u32[]{:S(2)}) collective-permute-start(f32[1536,128]{1,0:T(8,128)S(1)} %bitcast.3), channel_id=1, source_target_pairs={{0,8},{8,0},{1,9},{9,1},{2,10},{10,2},{3,11},{11,3},{4,12},{12,4},... | collective-permute-start | bytes 2359304 | tf_op jit(solution)/shard_map/ppermute | solution.py:274
  106.1 0.7 copy-start.3
  136.9 0.9 copy-start.2

commit v4 on v3

--- a/solution.py
+++ b/solution.py
@@ -23,6 +23,7 @@
 
 
 PARTS = 32
+ROOM = pltpu.CompilerParams(vmem_limit_bytes=20 << 20)
 G_ROWS = G_HALF * B // PARTS
 C_ROWS = C_HALF * B // PARTS
 
@@ -63,7 +64,7 @@
         in_specs=[SM, VM, VM],
         out_specs=[VM] * 2,
         cost_estimate=pl.CostEstimate(flops=2 * 192 * 512 * 1280, bytes_accessed=4 << 20, transcendentals=0),
-        name="gram",
+        compiler_params=ROOM, name="gram",
     )(core, a, t)
 
 
@@ -205,12 +206,12 @@
     x, d = pl.pallas_call(
         lambda *refs: first_kernel(row_count, *refs),
         out_shape=(full, jax.ShapeDtypeStruct((LAST * B, B), jnp.float32)), in_specs=[SM, VM, VM], out_specs=[VM, VM],
-        scratch_shapes=[scratch] * 2, cost_estimate=cost, name="factor0",
+        scratch_shapes=[scratch] * 2, cost_estimate=cost, compiler_params=ROOM, name="factor0",
     )(core, gm, go)
     return pl.pallas_call(
         last_kernel,
         out_shape=(full, full), in_specs=[VM] * 2, out_specs=[VM, VM],
-        scratch_shapes=[scratch] * 3, cost_estimate=cost, name="factor3",
+        scratch_shapes=[scratch] * 3, cost_estimate=cost, compiler_params=ROOM, name="factor3",
     )(x, d)
 
 
@@ -241,7 +242,7 @@
         out_shape=jax.ShapeDtypeStruct(t.shape, jnp.float32),
         in_specs=[SM] + [VM] * 5, out_specs=VM,
         scratch_shapes=[wide, pltpu.VMEM(a.shape, jnp.float32), wide],
-        cost_estimate=pl.CostEstimate(flops=4_000_000_000, bytes_accessed=4 << 20, transcendentals=0), name="update",
+        cost_estimate=pl.CostEstimate(flops=4_000_000_000, bytes_accessed=4 << 20, transcendentals=0), compiler_params=ROOM, name="update",
     )(core, x, cm, co, a, t)
 
 

time: 145 us -> 136 us (0.938)
  Pallas kernels: 41.5 us -> 33.3 us
    pallas_call x1, Pallas kernels: 4.7 us -> 2.17 us  [gram(): pl.pallas_call(gram_kernel, out_shape=(out, out), in_specs=[SM, VM, VM],...]
    pallas_call x1, Pallas kernels: 21.6 us -> 19.5 us  [factor(): pl.pallas_call(lambda *refs: first_kernel(row_count, *refs), out_shape=(f...]
    pallas_call x1, Pallas kernels: 6.72 us -> 4.78 us  [update(): pl.pallas_call(lambda *refs: update_kernel(row_count, *refs), out_shape=j...]
    pallas_call x1, Pallas kernels: 8.49 us -> 6.91 us  [factor(): pl.pallas_call(last_kernel, out_shape=(full, full), in_specs=[VM] * 2, ou...]
  transfers between devices with their start and end apart: 5 -> 5, of which waited for: 3 -> 3; matrix products, arithmetic and copies ran while one was open for 0% -> 0% of each run, Pallas kernels for 21% -> 19%
where the time goes in v4:
time: 136 us; the launch traced here: 135 us
  blocking collectives  44.2 us (32%)
  Pallas kernels  33.3 us (24%)
  starting transfers between devices  29.8 us (22%)
  waiting for transfers between devices  23.2 us (17%)
  local copies, waits for them, and re-layouts  3.8 us (3%)
    all_to_all x1, blocking collectives, reduce_over_devices(): lax.all_to_all(half, ALL, 0, 0, axis_index_groups=PLANES)  27.4 us
    all_to_all x2, waiting for transfers between devices, spread(): half = lax.all_to_all(copies, ALL, 0, 0, axis_index_groups=PLANES)  20.8 us
    pallas_call x1, Pallas kernels, factor(): pl.pallas_call(lambda *refs: first_kernel(row_count, *refs), out_shape=(f...  19.5 us
    all_to_all x1, blocking collectives, reduce_over_devices(): lax.all_to_all(jnp.broadcast_to(mine[None], (8,) + mine.shape), ALL, 0, 0...  16.8 us
    ppermute x2, starting transfers between devices, spread(): return (half, lax.ppermute(half, 'c', [(0, 1), (1, 0)]))  13.2 us
    ppermute x1, starting transfers between devices, reduce_over_devices(): half = keep + lax.ppermute(send, 'c', [(0, 1), (1, 0)])  8.75 us
    all_to_all x2, starting transfers between devices, spread(): half = lax.all_to_all(copies, ALL, 0, 0, axis_index_groups=PLANES)  7.79 us
    pallas_call x1, Pallas kernels, factor(): pl.pallas_call(last_kernel, out_shape=(full, full), in_specs=[VM] * 2, ou...  6.91 us
  transfers between devices with their start and end apart: 5, of which 3 were waited for; matrix products, arithmetic and copies ran while one was open for 0% of the time, Pallas kernels for 19%

profile of v4, /device:TPU:1, one launch (start us, length us, event | category | flops | bytes accessed | tf_op | source)
XLA Modules:
  0.0 135.4 jit_solution(5043291912185282910)
XLA Ops:
  0.6 0.0 copy-start
  0.6 1.1 copy-done
  1.7 1.0 copy-done.2
  2.7 2.2 %gram.1 = (f32[32,72,128]{2,1,0:T(8,128)S(1)}, f32[32,72,128]{2,1,0:T(8,128)S(1)}) custom-call(s32[1]{0:T(128)} %bitcast.core_ref.refs_0_, f32[192,512]{1,0:T(8,128)S(1)} %copy-done.2, f32[192,768]{1,0:T(8,128)S(1)} %copy-done), custom_call_target="tpu_custom_call" | custom-call | flops 251658240 | bytes 4194304 | tf_op jit(solution)/shard_map/gram/pallas_call | solution.py:61
  4.9 8.8 %collective-permute-start = (f32[32,72,128]{2,1,0:T(8,128)S(1)}, f32[32,72,128]{2,1,0:T(8,128)S(1)}, u32[]{:S(2)}, u32[]{:S(2)}) collective-permute-start(f32[32,72,128]{2,1,0:T(8,128)S(1)} %get-tuple-element.9), channel_id=1, source_target_pairs={{0,8},{8,0},{1,9},{9,1},{2,10},{10,2},{3,11},{11,3},{4,12},{12,4},... | collective-permute-start | bytes 3538952 | tf_op jit(solution)/shard_map/ppermute | solution.py:265
  13.6 2.5 %collective-permute-done = f32[32,72,128]{2,1,0:T(8,128)S(1)} collective-permute-done((f32[32,72,128]{2,1,0:T(8,128)S(1)}, f32[32,72,128]{2,1,0:T(8,128)S(1)}, u32[]{:S(2)}, u32[]{:S(2)}) %collective-permute-start) | collective-permute-done | bytes 1179680 | tf_op jit(solution)/shard_map/ppermute | solution.py:265
  16.1 0.2 add.3
  16.2 27.4 %all_to_all.20 = f32[32,72,128]{2,1,0:T(8,128)S(1)} all-to-all(f32[32,72,128]{2,1,0:T(8,128)S(1)} %add.3), channel_id=1, replica_groups={{0,16,32,48,64,80,96,112,128,144,160,176,192,208,224,240,256,272,288,30..., dimensions={0} | all-to-all | bytes 2359296 | tf_op jit(solution)/shard_map/all_to_all | solution.py:266
  43.7 0.1 reduce_sum.18
  43.8 16.8 %all_to_all.21 = f32[8,72,128]{2,1,0:T(8,128)S(1)} all-to-all(f32[8,72,128]{2,1,0:T(8,128)S(1)} %broadcast_in_dim.6), channel_id=1, replica_groups={{0,1,2,3,4,5,6,7},{16,17,18,19,20,21,22,23},{32,33,34,35,36,37,38,39},{..., dimensions={0} | all-to-all | bytes 589824 | tf_op jit(solution)/shard_map/all_to_all | solution.py:267
  60.6 0.8 broadcast_in_dim.7
  61.4 3.9 %all-to-all-start.2 = ((f32[32,24,128]{2,1,0:T(8,128)}), f32[32,24,128]{2,1,0:T(8,128)S(1)}, u32[]{:S(2)}, u32[]{:S(2)}) async-start(f32[32,24,128]{2,1,0:T(8,128)} %broadcast_in_dim.7), calls=%async_computation.2 | async-start | bytes 786432 | tf_op jit(solution)/shard_map/all_to_all | solution.py:273
  65.3 11.8 %all-to-all-done.2 = f32[32,24,128]{2,1,0:T(8,128)S(1)} async-done(((f32[32,24,128]{2,1,0:T(8,128)}), f32[32,24,128]{2,1,0:T(8,128)S(1)}, u32[]{:S(2)}, u32[]{:S(2)}) %all-to-all-start.2) | async-done | bytes 393248 | tf_op jit(solution)/shard_map/all_to_all | solution.py:273
  77.1 0.9 broadcast_in_dim.8
  78.0 3.9 %all-to-all-start.3 = ((f32[32,48,128]{2,1,0:T(8,128)}), f32[32,48,128]{2,1,0:T(8,128)S(1)}, u32[]{:S(2)}, u32[]{:S(2)}) async-start(f32[32,48,128]{2,1,0:T(8,128)} %broadcast_in_dim.8), calls=%async_computation.3 | async-start | bytes 1572864 | tf_op jit(solution)/shard_map/all_to_all | solution.py:273
  81.9 6.2 %collective-permute-start.1 = (f32[768,128]{1,0:T(8,128)S(1)}, f32[768,128]{1,0:T(8,128)S(1)}, u32[]{:S(2)}, u32[]{:S(2)}) collective-permute-start(f32[768,128]{1,0:T(8,128)S(1)} %bitcast.5), channel_id=1, source_target_pairs={{0,8},{8,0},{1,9},{9,1},{2,10},{10,2},{3,11},{11,3},{4,12},{12,4},... | collective-permute-start | bytes 1179656 | tf_op jit(solution)/shard_map/ppermute | solution.py:275
  88.2 9.0 %all-to-all-done.3 = f32[32,48,128]{2,1,0:T(8,128)S(1)} async-done(((f32[32,48,128]{2,1,0:T(8,128)}), f32[32,48,128]{2,1,0:T(8,128)S(1)}, u32[]{:S(2)}, u32[]{:S(2)}) %all-to-all-start.3) | async-done | bytes 786464 | tf_op jit(solution)/shard_map/all_to_all | solution.py:273
  97.1 7.0 %collective-permute-start.2 = (f32[1536,128]{1,0:T(8,128)S(1)}, f32[1536,128]{1,0:T(8,128)S(1)}, u32[]{:S(2)}, u32[]{:S(2)}) collective-permute-start(f32[1536,128]{1,0:T(8,128)S(1)} %bitcast.3), channel_id=1, source_target_pairs={{0,8},{8,0},{1,9},{9,1},{2,10},{10,2},{3,11},{11,3},{4,12},{12,4},... | collective-permute-start | bytes 2359304 | tf_op jit(solution)/shard_map/ppermute | solution.py:275
  104.1 19.5 %factor0.1 = (f32[512,512]{1,0:T(8,128)S(1)}, f32[384,128]{1,0:T(8,128)S(1)}) custom-call(s32[1]{0:T(128)} %bitcast.core_ref.refs_0_, f32[768,128]{1,0:T(8,128)S(1)} %bitcast.6, f32[768,128]{1,0:T(8,128)S(1)} %collective-permute-done.1.refs_2_), custom_call_target="tpu_custom_call" | custom-call | flops 4000000000 | bytes 2097152 | tf_op jit(solution)/shard_map/factor0/pallas_call | solution.py:206
  123.6 0.0 copy-start.1
  123.6 0.0 copy-start.3
  123.7 6.9 %factor3.1 = (f32[512,512]{1,0:T(8,128)S(1)}, f32[512,512]{1,0:T(8,128)}) custom-call(f32[512,512]{1,0:T(8,128)S(1)} %get-tuple-element.10.xi_ref, f32[384,128]{1,0:T(8,128)S(1)} %get-tuple-element.11.d_ref), custom_call_target="tpu_custom_call" | custom-call | flops 4000000000 | bytes 2097152 | tf_op jit(solution)/shard_map/factor3/pallas_call | solution.py:211
  130.6 0.0 collective-permute-done.2.refs_3_
  130.6 4.8 %update.1 = f32[192,768]{1,0:T(8,128)} custom-call(s32[1]{0:T(128)} %bitcast.core_ref.refs_0_, f32[512,512]{1,0:T(8,128)S(1)} %get-tuple-element.13.refs_1_, f32[1536,128]{1,0:T(8,128)S(1)} %bitcast.4, f32[1536,128]{1,0:T(8,128)S(1)} %collective-permute-done.2.refs_3_, f32[192,512]{1,0:T(8,128)S(1)} %copy-done.3, f32[192,768]{1,0:T(8,128)S(1)} %copy-done.1), custom_call_target="tpu_custom_call" | custom-call | flops 4000000000 | bytes 4194304 | tf_op jit(solution)/shard_map/update/pallas_call | solution.py:240
  (8 shorter events, 0.1 us)
Async XLA Ops:
  0.6 1.1 copy-start
  1.7 1.0 copy-start.2
  4.9 11.2 %collective-permute-start = (f32[32,72,128]{2,1,0:T(8,128)S(1)}, f32[32,72,128]{2,1,0:T(8,128)S(1)}, u32[]{:S(2)}, u32[]{:S(2)}) collective-permute-start(f32[32,72,128]{2,1,0:T(8,128)S(1)} %get-tuple-element.9), channel_id=1, source_target_pairs={{0,8},{8,0},{1,9},{9,1},{2,10},{10,2},{3,11},{11,3},{4,12},{12,4},... | collective-permute-start | bytes 3538952 | tf_op jit(solution)/shard_map/ppermute | solution.py:265
  61.4 15.7 %all-to-all-start.2 = ((f32[32,24,128]{2,1,0:T(8,128)}), f32[32,24,128]{2,1,0:T(8,128)S(1)}, u32[]{:S(2)}, u32[]{:S(2)}) async-start(f32[32,24,128]{2,1,0:T(8,128)} %broadcast_in_dim.7), calls=%async_computation.2 | async-start | bytes 786432 | tf_op jit(solution)/shard_map/all_to_all | solution.py:273
  78.0 19.2 %all-to-all-start.3 = ((f32[32,48,128]{2,1,0:T(8,128)}), f32[32,48,128]{2,1,0:T(8,128)S(1)}, u32[]{:S(2)}, u32[]{:S(2)}) async-start(f32[32,48,128]{2,1,0:T(8,128)} %broadcast_in_dim.8), calls=%async_computation.3 | async-start | bytes 1572864 | tf_op jit(solution)/shard_map/all_to_all | solution.py:273
  81.9 22.2 %collective-permute-start.1 = (f32[768,128]{1,0:T(8,128)S(1)}, f32[768,128]{1,0:T(8,128)S(1)}, u32[]{:S(2)}, u32[]{:S(2)}) collective-permute-start(f32[768,128]{1,0:T(8,128)S(1)} %bitcast.5), channel_id=1, source_target_pairs={{0,8},{8,0},{1,9},{9,1},{2,10},{10,2},{3,11},{11,3},{4,12},{12,4},... | collective-permute-start | bytes 1179656 | tf_op jit(solution)/shard_map/ppermute | solution.py:275
  97.1 33.4 %collective-permute-start.2 = (f32[1536,128]{1,0:T(8,128)S(1)}, f32[1536,128]{1,0:T(8,128)S(1)}, u32[]{:S(2)}, u32[]{:S(2)}) collective-permute-start(f32[1536,128]{1,0:T(8,128)S(1)} %bitcast.3), channel_id=1, source_target_pairs={{0,8},{8,0},{1,9},{9,1},{2,10},{10,2},{3,11},{11,3},{4,12},{12,4},... | collective-permute-start | bytes 2359304 | tf_op jit(solution)/shard_map/ppermute | solution.py:275
  123.6 6.9 %copy-start.1 = (f32[192,768]{1,0:T(8,128)S(1)}, f32[192,768]{1,0:T(8,128)}, u32[]{:S(2)}) copy-start(f32[192,768]{1,0:T(8,128)} %refs_5_.1) | copy-start | bytes 1769476
  123.6 6.9 %copy-start.3 = (f32[192,512]{1,0:T(8,128)S(1)}, f32[192,512]{1,0:T(8,128)}, u32[]{:S(2)}) copy-start(f32[192,512]{1,0:T(8,128)} %refs_4_.1) | copy-start | bytes 1179652

commit v5 on v4

--- a/solution.py
+++ b/solution.py
@@ -28,44 +28,66 @@
 C_ROWS = C_HALF * B // PARTS
 
 
-def gram_kernel(core_ref, a_ref, t_ref, keep_ref, send_ref):
+def products(mine, core, a_ref, t_ref, out_ref, ready):
     g_place = {b: (owner, slot) for b, owner, slot in split_half(G_BLOCKS)}
     c_place = {b: (owner, slot) for b, owner, slot in split_half(C_BLOCKS)}
 
-    def put(ref, value, slot, start, rows):
+    def put(value, slot, start, rows):
         for p in range(0, B, 8):
             part, at = divmod(slot * B + p, rows)
-            ref[part, start + at : start + at + 8, :] = value[p : p + 8]
+            out_ref[part, start + at : start + at + 8, :] = value[p : p + 8]
 
     def fill(me):
-        refs = (keep_ref, send_ref) if me == 0 else (send_ref, keep_ref)
+        owner = me if mine else 1 - me
+        ready(0)
         for i in range(NP):
-            left = a_ref[:, i * B : (i + 1) * B]
-            g = dot_t(left, a_ref[:, i * B :])
-            for j in range(i, NP):
-                owner, slot = g_place[(i, j)]
-                put(refs[owner], g[:, (j - i) * B : (j - i + 1) * B], slot, 0, G_ROWS)
-            c = dot_t(left, t_ref[...])
-            for j in range(NC):
-                owner, slot = c_place[(i, j)]
-                put(refs[owner], c[:, j * B : (j + 1) * B], slot, G_ROWS, C_ROWS)
-        for ref in refs:
-            put(ref, jnp.zeros((B, B), jnp.float32), G_HALF - 1, 0, G_ROWS)
+            cols = [j for j in range(i, NP) if g_place[(i, j)][0] == owner]
+            if cols:
+                lo, hi = min(cols), max(cols) + 1
+                g = dot_t(a_ref[:, i * B : (i + 1) * B], a_ref[:, lo * B : hi * B])
+                for j in cols:
+                    put(g[:, (j - lo) * B : (j - lo + 1) * B], g_place[(i, j)][1], 0, G_ROWS)
+        put(jnp.zeros((B, B), jnp.float32), G_HALF - 1, 0, G_ROWS)
+        ready(1)
+        for i in range(NP):
+            cols = [j for j in range(NC) if c_place[(i, j)][0] == owner]
+            if cols:
+                lo, hi = min(cols), max(cols) + 1
+                c = dot_t(a_ref[:, i * B : (i + 1) * B], t_ref[:, lo * B : hi * B])
+                for j in cols:
+                    put(c[:, (j - lo) * B : (j - lo + 1) * B], c_place[(i, j)][1], G_ROWS, C_ROWS)
 
     for me in range(2):
-        pl.when(core_ref[0] == me)(lambda me=me: fill(me))
+        pl.when(core == me)(lambda me=me: fill(me))
+
+
+def send_kernel(core_ref, a_hbm, t_hbm, out_ref, a_ref, t_ref, sem):
+    copies = [pltpu.make_async_copy(a_hbm, a_ref, sem.at[0]), pltpu.make_async_copy(t_hbm, t_ref, sem.at[1])]
+    for copy in copies:
+        copy.start()
+    products(False, core_ref[0], a_ref, t_ref, out_ref, lambda k: copies[k].wait())
+
+
+def keep_kernel(core_ref, a_ref, t_ref, out_ref):
+    products(True, core_ref[0], a_ref, t_ref, out_ref, lambda k: None)
 
 
 def gram(core, a, t):
     out = jax.ShapeDtypeStruct((PARTS, G_ROWS + C_ROWS, B), jnp.float32)
-    return pl.pallas_call(
-        gram_kernel,
-        out_shape=(out, out),
-        in_specs=[SM, VM, VM],
-        out_specs=[VM] * 2,
-        cost_estimate=pl.CostEstimate(flops=2 * 192 * 512 * 1280, bytes_accessed=4 << 20, transcendentals=0),
-        compiler_params=ROOM, name="gram",
+    cost = pl.CostEstimate(flops=192 * 512 * 1280, bytes_accessed=2 << 20, transcendentals=0)
+    hbm = pl.BlockSpec(memory_space=pltpu.HBM)
+    send = pl.pallas_call(
+        send_kernel,
+        out_shape=out, in_specs=[SM, hbm, hbm], out_specs=VM,
+        scratch_shapes=[pltpu.VMEM(a.shape, a.dtype), pltpu.VMEM(t.shape, t.dtype), pltpu.SemaphoreType.DMA((2,))],
+        cost_estimate=cost, name="gram_send",
     )(core, a, t)
+    keep = pl.pallas_call(
+        keep_kernel,
+        out_shape=out, in_specs=[SM, VM, VM], out_specs=VM,
+        compiler_params=ROOM, cost_estimate=cost, name="gram_keep",
+    )(core, a, t)
+    return keep, send
 
 
 def stack_pieces(u, order):
@@ -84,11 +106,16 @@
     return jnp.broadcast_to(v[t : t + 1, :], v.shape)
 
 
-def eliminate_rows(w_rows, v_rows, base):
+def lane_of(v, index):
+    return jnp.take_along_axis(v, index, axis=1, mode="promise_in_bounds")
+
+
+def eliminate(w_rows, v_rows, w_next, v_next, base):
     sub = lax.broadcasted_iota(jnp.int32, (8, B), 0)
+    ahead = jnp.minimum(base + 8 + sub, B - 1)
     d = {}
     for k in range(8):
-        col = jnp.take_along_axis(w_rows, jnp.full((8, B), base + k, jnp.int32), axis=1, mode="promise_in_bounds")
+        col = lane_of(w_rows, jnp.full((8, B), base + k, jnp.int32))
         for i in range(k + 1):
             d[i, k] = row_of(col, i)
     w = [row_of(w_rows, t) for t in range(8)]
@@ -104,34 +131,54 @@
         for i in range(t + 1, 8):
             w[i] = w[i] - u[i] * w[t]
             v[i] = v[i] - u[i] * v[t]
+        weight = lane_of(w[t], ahead)
+        w_next = w_next - weight * w[t]
+        v_next = v_next - weight * v[t]
     wo, vo = w[0], v[0]
     for t in range(1, 8):
         wo = jnp.where(sub == t, w[t], wo)
         vo = jnp.where(sub == t, v[t], vo)
-    return wo, vo
-
-
-def diag_factor(s, e, rkk):
+    return wo, vo, w_next, v_next
+
+
+def apply_rows(w, v, w_next, v_next, base):
+    sub = lax.broadcasted_iota(jnp.int32, (8, B), 0)
+    ahead = jnp.minimum(base + 8 + sub, B - 1)
+    for t in range(8):
+        row = row_of(w, t)
+        weight = lane_of(row, ahead)
+        w_next = w_next - weight * row
+        v_next = v_next - weight * row_of(v, t)
+    return w_next, v_next
+
+
+def diag_factor(s, e, rkk, lkk):
     lane = lax.broadcasted_iota(jnp.int32, (8, B), 1)
     sub = lax.broadcasted_iota(jnp.int32, (8, B), 0)
-    e[...] = jnp.where(
+    zero = jnp.zeros((8, B), jnp.float32)
+    e[:B, :] = jnp.where(
         lax.broadcasted_iota(jnp.int32, (B, B), 0) == lax.broadcasted_iota(jnp.int32, (B, B), 1), 1.0, 0.0
     ).astype(jnp.float32)
-
-    def body(g, _):
+    s[B:, :] = zero
+    e[B:, :] = zero
+
+    def body(g, carry):
+        w, v, w_last, v_last = carry
         base = pl.multiple_of(g * 8, 8)
         rows = pl.ds(base, 8)
-        u, v = eliminate_rows(s[rows, :], e[rows, :], base)
-        rkk[rows, :] = jnp.where(lane >= sub + base, u, 0.0)
-        left = stack_pieces(jnp.where(lane >= base + 8, u, 0.0), LEFT)
-        right = jnp.concatenate([stack_pieces(u, RIGHT), stack_pieces(v, RIGHT)], axis=1)
+        after = pl.ds(base + 8, 8)
+        left = stack_pieces(w_last, LEFT)
+        right = jnp.concatenate([stack_pieces(w_last, RIGHT), stack_pieces(v_last, RIGHT)], axis=1)
         change = lax.dot_general(left, right, (((0,), (0,)), ((), ())), preferred_element_type=jnp.float32)
-        s[...] = s[...] - change[:, :B]
-        e[...] = e[...] - change[:, B:]
-        e[rows, :] = v
-        return 0
-
-    lax.fori_loop(0, B // 8, body, 0)
+        w_next, v_next = apply_rows(w_last, v_last, s[after, :], e[after, :], base)
+        w, v, w_next, v_next = eliminate(w, v, w_next, v_next, base)
+        rkk[rows, :] = jnp.where(lane >= sub + base, w, 0.0)
+        lkk[rows, :] = v
+        s[:B, :] = s[:B, :] - change[:, :B]
+        e[:B, :] = e[:B, :] - change[:, B:]
+        return w_next, v_next, w, v
+
+    lax.fori_loop(0, B // 8, body, (s[:8, :], e[:8, :], zero, zero))
 
 
 def dot(x, y):
@@ -142,31 +189,32 @@
     return lax.dot_general(x, y, (((0,), (0,)), ((), ())), precision=HI, preferred_element_type=jnp.float32)
 
 
-def panel_step(k, x, rkk, s, lkk):
+def panel_step(k, x, rkk, s, e, lkk):
     r0 = k * B
     r1 = r0 + B
-    s[...] = x[r0:r1, r0:r1]
-    diag_factor(s, lkk, rkk)
+    s[:B, :] = x[r0:r1, r0:r1]
+    diag_factor(s, e, rkk, lkk)
     linv = lkk[...]
-    if k > 0:
-        x[r0:r1, :r0] = dot(linv, x[r0:r1, :r0])
+    if k == NP - 1:
+        x[r0:, :r0] = dot(linv, x[r0:, :r0])
+    else:
+        x[r0:r1, :] = dot(linv, x[r0:r1, :])
+    x[r0:r1, r0:r1] = linv
     if k < NP - 1:
-        x[r0:r1, r1:] = dot(linv, x[r0:r1, r1:])
-    x[r0:r1, r0:r1] = linv
-    for i in range(k + 1, NP):
-        c0 = i * B
-        left = x[r0:r1, c0 : c0 + B]
-        x[c0 : c0 + B, c0:] = x[c0 : c0 + B, c0:] - dot_t(left, x[r0:r1, c0:])
-        low = dot_t(left, x[r0:r1, :r1])
-        if k > 0:
-            x[c0 : c0 + B, :r0] = x[c0 : c0 + B, :r0] - low[:, :r0]
-        x[c0 : c0 + B, r0:r1] = -low[:, r0:]
+        change = dot_t(x[r0:r1, r1:], x[r0:r1, :])
+        for i in range(k + 1, NP):
+            c0 = i * B
+            part = change[c0 - r1 : c0 - r1 + B]
+            x[c0 : c0 + B, c0:] = x[c0 : c0 + B, c0:] - part[:, c0:]
+            if k > 0:
+                x[c0 : c0 + B, :r0] = x[c0 : c0 + B, :r0] - part[:, :r0]
+            x[c0 : c0 + B, r0:r1] = -part[:, r0:r1]
 
 
 LAST = NP - 1
 
 
-def first_kernel(row_count, core_ref, gm_ref, go_ref, x_ref, d_ref, s, lkk):
+def first_kernel(row_count, core_ref, gm_ref, go_ref, x_ref, d_ref, s, e, lkk):
     scale = 1.0 / row_count
     for me in range(2):
 
@@ -180,10 +228,10 @@
         for j in range(i):
             x_ref[i * B : (i + 1) * B, j * B : (j + 1) * B] = jnp.zeros((B, B), jnp.float32)
     for k in range(LAST):
-        panel_step(k, x_ref, d_ref.at[pl.ds(k * B, B), :], s, lkk)
-
-
-def last_kernel(xi_ref, d_ref, li_ref, r_ref, rkk, s, lkk):
+        panel_step(k, x_ref, d_ref.at[pl.ds(k * B, B), :], s, e, lkk)
+
+
+def last_kernel(xi_ref, d_ref, li_ref, r_ref, s, e, lkk, rkk):
     r0 = LAST * B
     for i in range(LAST):
         rows = slice(i * B, (i + 1) * B)
@@ -192,7 +240,7 @@
         if i > 0:
             r_ref[rows, : i * B] = jnp.zeros((B, i * B), jnp.float32)
     li_ref[...] = xi_ref[...]
-    panel_step(LAST, li_ref, rkk, s, lkk)
+    panel_step(LAST, li_ref, rkk, s, e, lkk)
     r_ref[r0:, :r0] = jnp.zeros((B, r0), jnp.float32)
     r_ref[r0:, r0:] = rkk[...]
     for i in (0, 2):
@@ -201,17 +249,17 @@
 
 def factor(row_count, core, gm, go):
     full = jax.ShapeDtypeStruct((NP * B, NP * B), jnp.float32)
-    scratch = pltpu.VMEM((B, B), jnp.float32)
+    work = [pltpu.VMEM((B + 8, B), jnp.float32)] * 2 + [pltpu.VMEM((B, B), jnp.float32)]
     cost = pl.CostEstimate(flops=4_000_000_000, bytes_accessed=2 << 20, transcendentals=0)
     x, d = pl.pallas_call(
         lambda *refs: first_kernel(row_count, *refs),
         out_shape=(full, jax.ShapeDtypeStruct((LAST * B, B), jnp.float32)), in_specs=[SM, VM, VM], out_specs=[VM, VM],
-        scratch_shapes=[scratch] * 2, cost_estimate=cost, compiler_params=ROOM, name="factor0",
+        scratch_shapes=work, cost_estimate=cost, compiler_params=ROOM, name="factor0",
     )(core, gm, go)
     return pl.pallas_call(
         last_kernel,
         out_shape=(full, full), in_specs=[VM] * 2, out_specs=[VM, VM],
-        scratch_shapes=[scratch] * 3, cost_estimate=cost, compiler_params=ROOM, name="factor3",
+        scratch_shapes=work + [pltpu.VMEM((B, B), jnp.float32)], cost_estimate=cost, compiler_params=ROOM, name="factor3",
     )(x, d)
 
 
@@ -278,8 +326,9 @@
 def local(row_count, panel_block, trailing):
     core = lax.axis_index("c").astype(jnp.int32).reshape(1)
     mine = reduce_over_devices(*gram(core, panel_block, trailing))
-    gm, go = spread(mine[:G_ROWS])
-    cm, co = spread(mine[G_ROWS:])
+    mine_g, mine_c = lax.optimization_barrier((mine[:G_ROWS], mine[G_ROWS:]))
+    gm, go = spread(mine_g)
+    cm, co = spread(mine_c)
     x, r = factor(row_count, core, gm, go)
     return r, update(row_count, core, x, cm, co, panel_block, trailing)
 

time: 136 us -> 126 us (0.926)
  blocking collectives: 44.2 us -> 59.2 us
  waiting for transfers between devices: 23.2 us -> 10.2 us
  Pallas kernels: 33.3 us -> 28.1 us
  starting transfers between devices: 29.8 us -> 26.3 us
  local copies, waits for them, and re-layouts: 3.8 us -> 0.99 us
    all_to_all x0 -> x1, blocking collectives: none -> 15 us  [spread(): half = lax.all_to_all(copies, ALL, 0, 0, axis_index_groups=PLANES)]
    all_to_all x2 -> x1, waiting for transfers between devices: 20.8 us -> 8.74 us  [spread(): half = lax.all_to_all(copies, ALL, 0, 0, axis_index_groups=PLANES)]
    pallas_call x1, Pallas kernels: 19.5 us -> 13.7 us  [factor(): pl.pallas_call(lambda *refs: first_kernel(row_count, *refs), out_shape=(f...]
    all_to_all x2 -> x1, starting transfers between devices: 7.79 us -> 4.16 us  [spread(): half = lax.all_to_all(copies, ALL, 0, 0, axis_index_groups=PLANES)]
    pallas_call x1 -> x2, Pallas kernels: 2.17 us -> 4.65 us  [the longest x1 3.48 us: gram(): pl.pallas_call(send_kernel, out_shape=out, in_specs=[SM, hbm, hbm], out_s...]
    unnamed x8 -> x4, local copies, waits for them, and re-layouts: 2.07 us -> 0.01 us
    pallas_call x1, Pallas kernels: 6.91 us -> 4.92 us  [factor(): pl.pallas_call(last_kernel, out_shape=(full, full), in_specs=[VM] * 2, ou...]
  transfers between devices with their start and end apart: 5 -> 4, of which waited for: 3 -> 2; matrix products, arithmetic and copies ran while one was open for 0% -> 0% of each run, Pallas kernels for 19% -> 16%
where the time goes in v5:
time: 126 us
  blocking collectives  59.2 us (47%)
  Pallas kernels  28.1 us (22%)
  starting transfers between devices  26.3 us (21%)
  waiting for transfers between devices  10.2 us (8%)
    all_to_all x1, blocking collectives, reduce_over_devices(): lax.all_to_all(half, ALL, 0, 0, axis_index_groups=PLANES)  27.4 us
    all_to_all x1, blocking collectives, reduce_over_devices(): lax.all_to_all(jnp.broadcast_to(mine[None], (8,) + mine.shape), ALL, 0, 0...  16.8 us
    all_to_all x1, blocking collectives, spread(): half = lax.all_to_all(copies, ALL, 0, 0, axis_index_groups=PLANES)  15 us
    pallas_call x1, Pallas kernels, factor(): pl.pallas_call(lambda *refs: first_kernel(row_count, *refs), out_shape=(f...  13.7 us
    ppermute x2, starting transfers between devices, spread(): return (half, lax.ppermute(half, 'c', [(0, 1), (1, 0)]))  13.4 us
    ppermute x1, starting transfers between devices, reduce_over_devices(): half = keep + lax.ppermute(send, 'c', [(0, 1), (1, 0)])  8.74 us
    all_to_all x1, waiting for transfers between devices, spread(): half = lax.all_to_all(copies, ALL, 0, 0, axis_index_groups=PLANES)  8.74 us
    pallas_call x1, Pallas kernels, factor(): pl.pallas_call(last_kernel, out_shape=(full, full), in_specs=[VM] * 2, ou...  4.92 us
  transfers between devices with their start and end apart: 4, of which 2 were waited for; matrix products, arithmetic and copies ran while one was open for 0% of the time, Pallas kernels for 16%

profile of v5, /device:TPU:1, one launch (start us, length us, event | category | flops | bytes accessed | tf_op | source)
XLA Modules:
  0.0 125.8 jit_solution(17787191456995004018)
XLA Ops:
  0.6 0.0 copy-start.1
  0.6 0.0 copy-start
  0.7 3.5 %gram_send.1 = f32[32,72,128]{2,1,0:T(8,128)} custom-call(s32[1]{0:T(128)} %bitcast.core_ref.refs_0_, f32[192,512]{1,0:T(8,128)} %refs_4_.1, f32[192,768]{1,0:T(8,128)} %refs_5_.1), custom_call_target="tpu_custom_call" | custom-call | flops 125829120 | bytes 2097152 | tf_op jit(solution)/shard_map/gram_send/pallas_call | solution.py:79
  4.1 8.7 %collective-permute-start = (f32[32,72,128]{2,1,0:T(8,128)}, f32[32,72,128]{2,1,0:T(8,128)S(1)}, u32[]{:S(2)}, u32[]{:S(2)}) collective-permute-start(f32[32,72,128]{2,1,0:T(8,128)} %gram_send.1), channel_id=1, source_target_pairs={{0,8},{8,0},{1,9},{9,1},{2,10},{10,2},{3,11},{11,3},{4,12},{12,4},... | collective-permute-start | bytes 3538952 | tf_op jit(solution)/shard_map/ppermute | solution.py:313
  12.9 0.0 copy-done.1
  12.9 0.0 copy-done
  12.9 1.2 gram_keep.1
  14.1 1.5 %collective-permute-done = f32[32,72,128]{2,1,0:T(8,128)S(1)} collective-permute-done((f32[32,72,128]{2,1,0:T(8,128)}, f32[32,72,128]{2,1,0:T(8,128)S(1)}, u32[]{:S(2)}, u32[]{:S(2)}) %collective-permute-start) | collective-permute-done | bytes 1179680 | tf_op jit(solution)/shard_map/ppermute | solution.py:313
  15.6 0.1 add.3
  15.7 27.4 %all_to_all.20 = f32[32,72,128]{2,1,0:T(8,128)S(1)} all-to-all(f32[32,72,128]{2,1,0:T(8,128)S(1)} %add.3), channel_id=1, replica_groups={{0,16,32,48,64,80,96,112,128,144,160,176,192,208,224,240,256,272,288,30..., dimensions={0} | all-to-all | bytes 2359296 | tf_op jit(solution)/shard_map/all_to_all | solution.py:314
  43.1 0.1 reduce_sum.18
  43.2 16.8 %all_to_all.21 = f32[8,72,128]{2,1,0:T(8,128)S(1)} all-to-all(f32[8,72,128]{2,1,0:T(8,128)S(1)} %broadcast_in_dim.6), channel_id=1, replica_groups={{0,1,2,3,4,5,6,7},{16,17,18,19,20,21,22,23},{32,33,34,35,36,37,38,39},{..., dimensions={0} | all-to-all | bytes 589824 | tf_op jit(solution)/shard_map/all_to_all | solution.py:315
  60.1 15.0 %all_to_all.22 = f32[32,24,128]{2,1,0:T(8,128)S(1)} all-to-all(f32[32,24,128]{2,1,0:T(8,128)S(1)} %broadcast_in_dim.7), channel_id=1, replica_groups={{0,16,32,48,64,80,96,112,128,144,160,176,192,208,224,240,256,272,288,30..., dimensions={0} | all-to-all | bytes 786432 | tf_op jit(solution)/shard_map/all_to_all | solution.py:321
  75.1 0.9 broadcast_in_dim.8
  76.0 4.2 %all-to-all-start.3 = ((f32[32,48,128]{2,1,0:T(8,128)}), f32[32,48,128]{2,1,0:T(8,128)S(1)}, u32[]{:S(2)}, u32[]{:S(2)}) async-start(f32[32,48,128]{2,1,0:T(8,128)} %broadcast_in_dim.8), calls=%async_computation.3 | async-start | bytes 1572864 | tf_op jit(solution)/shard_map/all_to_all | solution.py:321
  80.2 6.2 %collective-permute-start.1 = (f32[768,128]{1,0:T(8,128)S(1)}, f32[768,128]{1,0:T(8,128)S(1)}, u32[]{:S(2)}, u32[]{:S(2)}) collective-permute-start(f32[768,128]{1,0:T(8,128)S(1)} %bitcast.5), channel_id=1, source_target_pairs={{0,8},{8,0},{1,9},{9,1},{2,10},{10,2},{3,11},{11,3},{4,12},{12,4},... | collective-permute-start | bytes 1179656 | tf_op jit(solution)/shard_map/ppermute | solution.py:323
  86.4 8.7 %all-to-all-done.3 = f32[32,48,128]{2,1,0:T(8,128)S(1)} async-done(((f32[32,48,128]{2,1,0:T(8,128)}), f32[32,48,128]{2,1,0:T(8,128)S(1)}, u32[]{:S(2)}, u32[]{:S(2)}) %all-to-all-start.3) | async-done | bytes 786464 | tf_op jit(solution)/shard_map/all_to_all | solution.py:321
  95.1 7.3 %collective-permute-start.2 = (f32[1536,128]{1,0:T(8,128)S(1)}, f32[1536,128]{1,0:T(8,128)S(1)}, u32[]{:S(2)}, u32[]{:S(2)}) collective-permute-start(f32[1536,128]{1,0:T(8,128)S(1)} %bitcast.3), channel_id=1, source_target_pairs={{0,8},{8,0},{1,9},{9,1},{2,10},{10,2},{3,11},{11,3},{4,12},{12,4},... | collective-permute-start | bytes 2359304 | tf_op jit(solution)/shard_map/ppermute | solution.py:323
  102.4 0.0 collective-permute-done.1.refs_2_
  102.4 13.7 %factor0.1 = (f32[512,512]{1,0:T(8,128)S(1)}, f32[384,128]{1,0:T(8,128)S(1)}) custom-call(s32[1]{0:T(128)} %bitcast.core_ref.refs_0_, f32[768,128]{1,0:T(8,128)S(1)} %bitcast.6, f32[768,128]{1,0:T(8,128)S(1)} %collective-permute-done.1.refs_2_), custom_call_target="tpu_custom_call" | custom-call | flops 4000000000 | bytes 2097152 | tf_op jit(solution)/shard_map/factor0/pallas_call | solution.py:254
  116.1 4.9 %factor3.1 = (f32[512,512]{1,0:T(8,128)S(1)}, f32[512,512]{1,0:T(8,128)}) custom-call(f32[512,512]{1,0:T(8,128)S(1)} %get-tuple-element.9.xi_ref, f32[384,128]{1,0:T(8,128)S(1)} %get-tuple-element.10.d_ref), custom_call_target="tpu_custom_call" | custom-call | flops 4000000000 | bytes 2097152 | tf_op jit(solution)/shard_map/factor3/pallas_call | solution.py:259
  121.1 0.0 collective-permute-done.2.refs_3_
  121.1 4.8 %update.1 = f32[192,768]{1,0:T(8,128)} custom-call(s32[1]{0:T(128)} %bitcast.core_ref.refs_0_, f32[512,512]{1,0:T(8,128)S(1)} %get-tuple-element.12.refs_1_, f32[1536,128]{1,0:T(8,128)S(1)} %bitcast.4, f32[1536,128]{1,0:T(8,128)S(1)} %collective-permute-done.2.refs_3_, f32[192,512]{1,0:T(8,128)S(1)} %copy-done.1, f32[192,768]{1,0:T(8,128)S(1)} %copy-done), custom_call_target="tpu_custom_call" | custom-call | flops 4000000000 | bytes 4194304 | tf_op jit(solution)/shard_map/update/pallas_call | solution.py:288
  (5 shorter events, 0.1 us)
Async XLA Ops:
  0.6 12.3 %copy-start.1 = (f32[192,512]{1,0:T(8,128)S(1)}, f32[192,512]{1,0:T(8,128)}, u32[]{:S(2)}) copy-start(f32[192,512]{1,0:T(8,128)} %refs_4_.1) | copy-start | bytes 1179652
  0.6 12.3 %copy-start = (f32[192,768]{1,0:T(8,128)S(1)}, f32[192,768]{1,0:T(8,128)}, u32[]{:S(2)}) copy-start(f32[192,768]{1,0:T(8,128)} %refs_5_.1) | copy-start | bytes 1769476
  4.1 11.4 %collective-permute-start = (f32[32,72,128]{2,1,0:T(8,128)}, f32[32,72,128]{2,1,0:T(8,128)S(1)}, u32[]{:S(2)}, u32[]{:S(2)}) collective-permute-start(f32[32,72,128]{2,1,0:T(8,128)} %gram_send.1), channel_id=1, source_target_pairs={{0,8},{8,0},{1,9},{9,1},{2,10},{10,2},{3,11},{11,3},{4,12},{12,4},... | collective-permute-start | bytes 3538952 | tf_op jit(solution)/shard_map/ppermute | solution.py:313
  76.0 19.1 %all-to-all-start.3 = ((f32[32,48,128]{2,1,0:T(8,128)}), f32[32,48,128]{2,1,0:T(8,128)S(1)}, u32[]{:S(2)}, u32[]{:S(2)}) async-start(f32[32,48,128]{2,1,0:T(8,128)} %broadcast_in_dim.8), calls=%async_computation.3 | async-start | bytes 1572864 | tf_op jit(solution)/shard_map/all_to_all | solution.py:321
  80.2 22.2 %collective-permute-start.1 = (f32[768,128]{1,0:T(8,128)S(1)}, f32[768,128]{1,0:T(8,128)S(1)}, u32[]{:S(2)}, u32[]{:S(2)}) collective-permute-start(f32[768,128]{1,0:T(8,128)S(1)} %bitcast.5), channel_id=1, source_target_pairs={{0,8},{8,0},{1,9},{9,1},{2,10},{10,2},{3,11},{11,3},{4,12},{12,4},... | collective-permute-start | bytes 1179656 | tf_op jit(solution)/shard_map/ppermute | solution.py:323
  95.1 26.0 %collective-permute-start.2 = (f32[1536,128]{1,0:T(8,128)S(1)}, f32[1536,128]{1,0:T(8,128)S(1)}, u32[]{:S(2)}, u32[]{:S(2)}) collective-permute-start(f32[1536,128]{1,0:T(8,128)S(1)} %bitcast.3), channel_id=1, source_target_pairs={{0,8},{8,0},{1,9},{9,1},{2,10},{10,2},{3,11},{11,3},{4,12},{12,4},... | collective-permute-start | bytes 2359304 | tf_op jit(solution)/shard_map/ppermute | solution.py:323

commit v6 on v5

--- a/solution.py
+++ b/solution.py
@@ -85,7 +85,7 @@
     keep = pl.pallas_call(
         keep_kernel,
         out_shape=out, in_specs=[SM, VM, VM], out_specs=VM,
-        compiler_params=ROOM, cost_estimate=cost, name="gram_keep",
+        cost_estimate=cost, name="gram_keep",
     )(core, a, t)
     return keep, send
 
@@ -211,10 +211,7 @@
             x[c0 : c0 + B, r0:r1] = -part[:, r0:r1]
 
 
-LAST = NP - 1
-
-
-def first_kernel(row_count, core_ref, gm_ref, go_ref, x_ref, d_ref, s, e, lkk):
+def factor_kernel(row_count, core_ref, gm_ref, go_ref, x_ref, r_ref, s, e, lkk):
     scale = 1.0 / row_count
     for me in range(2):
 
@@ -225,47 +222,52 @@
                 x_ref[i * B : (i + 1) * B, j * B : (j + 1) * B] = refs[owner][slot * B : (slot + 1) * B, :] * scale
 
     for i in range(NP):
-        for j in range(i):
-            x_ref[i * B : (i + 1) * B, j * B : (j + 1) * B] = jnp.zeros((B, B), jnp.float32)
-    for k in range(LAST):
-        panel_step(k, x_ref, d_ref.at[pl.ds(k * B, B), :], s, e, lkk)
-
-
-def last_kernel(xi_ref, d_ref, li_ref, r_ref, s, e, lkk, rkk):
-    r0 = LAST * B
-    for i in range(LAST):
         rows = slice(i * B, (i + 1) * B)
-        r_ref[rows, :] = xi_ref[rows, :]
-        r_ref[rows, rows] = d_ref[rows, :]
         if i > 0:
+            x_ref[rows, : i * B] = jnp.zeros((B, i * B), jnp.float32)
             r_ref[rows, : i * B] = jnp.zeros((B, i * B), jnp.float32)
-    li_ref[...] = xi_ref[...]
-    panel_step(LAST, li_ref, rkk, s, e, lkk)
-    r_ref[r0:, :r0] = jnp.zeros((B, r0), jnp.float32)
-    r_ref[r0:, r0:] = rkk[...]
+    for k in range(NP):
+        r0, r1 = k * B, (k + 1) * B
+        panel_step(k, x_ref, r_ref.at[pl.ds(r0, B), pl.ds(r0, B)], s, e, lkk)
+        if r1 < NP * B:
+            r_ref[r0:r1, r1:] = x_ref[r0:r1, r1:]
     for i in (0, 2):
-        li_ref[i * B : (i + 1) * B, (i + 1) * B : (i + 2) * B] = jnp.zeros((B, B), jnp.float32)
+        x_ref[i * B : (i + 1) * B, (i + 1) * B : (i + 2) * B] = jnp.zeros((B, B), jnp.float32)
 
 
 def factor(row_count, core, gm, go):
     full = jax.ShapeDtypeStruct((NP * B, NP * B), jnp.float32)
-    work = [pltpu.VMEM((B + 8, B), jnp.float32)] * 2 + [pltpu.VMEM((B, B), jnp.float32)]
-    cost = pl.CostEstimate(flops=4_000_000_000, bytes_accessed=2 << 20, transcendentals=0)
-    x, d = pl.pallas_call(
-        lambda *refs: first_kernel(row_count, *refs),
-        out_shape=(full, jax.ShapeDtypeStruct((LAST * B, B), jnp.float32)), in_specs=[SM, VM, VM], out_specs=[VM, VM],
-        scratch_shapes=work, cost_estimate=cost, compiler_params=ROOM, name="factor0",
+    return pl.pallas_call(
+        lambda *refs: factor_kernel(row_count, *refs),
+        out_shape=(full, full), in_specs=[SM, VM, VM], out_specs=[VM, VM],
+        scratch_shapes=[pltpu.VMEM((B + 8, B), jnp.float32)] * 2 + [pltpu.VMEM((B, B), jnp.float32)],
+        cost_estimate=pl.CostEstimate(flops=8_000_000_000, bytes_accessed=2 << 20, transcendentals=0),
+        compiler_params=ROOM, name="factor",
     )(core, gm, go)
+
+
+HALF = NP * B // 2
+
+
+def basis_kernel(x_ref, a_ref, q_ref):
+    for r0 in (0, HALF):
+        r1 = r0 + HALF
+        q_ref[:, r0:r1] = lax.dot_general(
+            a_ref[:, :r1], x_ref[r0:r1, :r1], (((1,), (1,)), ((), ())), precision=HI, preferred_element_type=jnp.float32
+        )
+
+
+def basis(x, a):
     return pl.pallas_call(
-        last_kernel,
-        out_shape=(full, full), in_specs=[VM] * 2, out_specs=[VM, VM],
-        scratch_shapes=work + [pltpu.VMEM((B, B), jnp.float32)], cost_estimate=cost, compiler_params=ROOM, name="factor3",
-    )(x, d)
-
-
-def update_kernel(row_count, core_ref, x_ref, cm_ref, co_ref, a_ref, t_ref, out_ref, c, q, p):
+        basis_kernel,
+        out_shape=jax.ShapeDtypeStruct(a.shape, jnp.float32), in_specs=[VM, VM], out_specs=VM,
+        cost_estimate=pl.CostEstimate(flops=1_000_000_000, bytes_accessed=2 << 20, transcendentals=0),
+        compiler_params=ROOM, name="basis",
+    )(x, a)
+
+
+def update_kernel(row_count, core_ref, x_ref, cm_ref, co_ref, q_ref, t_ref, out_ref, c, p):
     scale = 1.0 / row_count
-    h = NP * B // 2
     for me in range(2):
 
         @pl.when(core_ref[0] == me)
@@ -274,24 +276,22 @@
             for (i, j), owner, slot in split_half(C_BLOCKS):
                 c[i * B : (i + 1) * B, j * B : (j + 1) * B] = refs[owner][slot * B : (slot + 1) * B, :] * scale
 
-    for r0 in (0, h):
-        r1 = r0 + h
-        q[:, r0:r1] = lax.dot_general(
-            a_ref[:, :r1], x_ref[r0:r1, :r1], (((1,), (1,)), ((), ())), precision=HI, preferred_element_type=jnp.float32
-        )
+    for r0 in (0, HALF):
+        r1 = r0 + HALF
         p[r0:r1, :] = dot(x_ref[r0:r1, :r1], c[:r1, :])
-    out_ref[...] = t_ref[...] - dot(q[...], p[...])
-
-
-def update(row_count, core, x, cm, co, a, t):
+    out_ref[...] = t_ref[...] - dot(q_ref[...], p[...])
+
+
+def update(row_count, core, x, cm, co, q, t):
     wide = pltpu.VMEM((NP * B, NC * B), jnp.float32)
     return pl.pallas_call(
         lambda *refs: update_kernel(row_count, *refs),
         out_shape=jax.ShapeDtypeStruct(t.shape, jnp.float32),
         in_specs=[SM] + [VM] * 5, out_specs=VM,
-        scratch_shapes=[wide, pltpu.VMEM(a.shape, jnp.float32), wide],
-        cost_estimate=pl.CostEstimate(flops=4_000_000_000, bytes_accessed=4 << 20, transcendentals=0), compiler_params=ROOM, name="update",
-    )(core, x, cm, co, a, t)
+        scratch_shapes=[wide, wide],
+        cost_estimate=pl.CostEstimate(flops=3_000_000_000, bytes_accessed=4 << 20, transcendentals=0),
+        compiler_params=ROOM, name="update",
+    )(core, x, cm, co, q, t)
 
 
 ALL = ("y", "x", "c", "z")
@@ -330,7 +330,7 @@
     gm, go = spread(mine_g)
     cm, co = spread(mine_c)
     x, r = factor(row_count, core, gm, go)
-    return r, update(row_count, core, x, cm, co, panel_block, trailing)
+    return r, update(row_count, core, x, cm, co, basis(x, panel_block), trailing)
 
 
 def solution(mesh):

time: 126 us -> 128 us (1.016)
  Pallas kernels: 28.1 us -> 30.1 us
    pallas_call x1, Pallas kernels: 1.17 us -> 3.38 us  [gram(): pl.pallas_call(keep_kernel, out_shape=out, in_specs=[SM, VM, VM], out_spe...]
    ppermute x1, waiting for transfers between devices: 1.46 us -> 0.01 us  [reduce_over_devices(): half = keep + lax.ppermute(send, 'c', [(0, 1), (1, 0)])]
  transfers between devices with their start and end apart: 4 -> 4, of which waited for: 2 -> 1; matrix products, arithmetic and copies ran while one was open for 0% -> 0% of each run, Pallas kernels for 16% -> 18%
where the time goes in v6:
time: 128 us; the launch traced here: 127 us
  blocking collectives  59.3 us (46%)
  Pallas kernels  30.1 us (24%)
  starting transfers between devices  25.4 us (20%)
  waiting for transfers between devices  9.2 us (7%)
  other arithmetic  1.48 us (1%)
    all_to_all x1, blocking collectives, reduce_over_devices(): lax.all_to_all(half, ALL, 0, 0, axis_index_groups=PLANES)  27.4 us
    pallas_call x1, Pallas kernels, factor(): pl.pallas_call(lambda *refs: factor_kernel(row_count, *refs), out_shape=(...  18.3 us
    all_to_all x1, blocking collectives, reduce_over_devices(): lax.all_to_all(jnp.broadcast_to(mine[None], (8,) + mine.shape), ALL, 0, 0...  16.8 us
    all_to_all x1, blocking collectives, spread(): half = lax.all_to_all(copies, ALL, 0, 0, axis_index_groups=PLANES)  15.1 us
    ppermute x2, starting transfers between devices, spread(): return (half, lax.ppermute(half, 'c', [(0, 1), (1, 0)]))  12.6 us
    all_to_all x1, waiting for transfers between devices, spread(): half = lax.all_to_all(copies, ALL, 0, 0, axis_index_groups=PLANES)  9.19 us
    ppermute x1, starting transfers between devices, reduce_over_devices(): half = keep + lax.ppermute(send, 'c', [(0, 1), (1, 0)])  8.76 us
    pallas_call x1, Pallas kernels, update(): pl.pallas_call(lambda *refs: update_kernel(row_count, *refs), out_shape=j...  4.14 us
  transfers between devices with their start and end apart: 4, of which 1 were waited for; matrix products, arithmetic and copies ran while one was open for 0% of the time, Pallas kernels for 18%

profile of v6, /device:TPU:1, one launch (start us, length us, event | category | flops | bytes accessed | tf_op | source)
XLA Modules:
  0.0 127.4 jit_solution(9391355511925985833)
XLA Ops:
  0.6 3.4 %gram_send.1 = f32[32,72,128]{2,1,0:T(8,128)} custom-call(s32[1]{0:T(128)} %bitcast.core_ref.refs_0_, f32[192,512]{1,0:T(8,128)} %a_ref.3, f32[192,768]{1,0:T(8,128)} %refs_5_.1), custom_call_target="tpu_custom_call" | custom-call | flops 125829120 | bytes 2097152 | tf_op jit(solution)/shard_map/gram_send/pallas_call | solution.py:79
  4.1 8.8 %collective-permute-start = (f32[32,72,128]{2,1,0:T(8,128)}, f32[32,72,128]{2,1,0:T(8,128)S(1)}, u32[]{:S(2)}, u32[]{:S(2)}) collective-permute-start(f32[32,72,128]{2,1,0:T(8,128)} %gram_send.1), channel_id=1, source_target_pairs={{0,8},{8,0},{1,9},{9,1},{2,10},{10,2},{3,11},{11,3},{4,12},{12,4},... | collective-permute-start | bytes 3538952 | tf_op jit(solution)/shard_map/ppermute | solution.py:313
  12.8 3.4 %gram_keep.1 = f32[32,72,128]{2,1,0:T(8,128)} custom-call(s32[1]{0:T(128)} %bitcast.core_ref.refs_0_, f32[192,512]{1,0:T(8,128)} %a_ref.3, f32[192,768]{1,0:T(8,128)} %refs_5_.1), custom_call_target="tpu_custom_call" | custom-call | flops 125829120 | bytes 2097152 | tf_op jit(solution)/shard_map/gram_keep/pallas_call | solution.py:85
  16.2 0.0 collective-permute-done
  16.2 1.4 %add.3 = f32[32,72,128]{2,1,0:T(8,128)S(1)} add(f32[32,72,128]{2,1,0:T(8,128)} %gram_keep.1, f32[32,72,128]{2,1,0:T(8,128)S(1)} %collective-permute-done) | non-fusion elementwise | flops 294912 | bytes 3538944 | tf_op jit(solution)/shard_map/add | solution.py:313
  17.6 27.4 %all_to_all.20 = f32[32,72,128]{2,1,0:T(8,128)S(1)} all-to-all(f32[32,72,128]{2,1,0:T(8,128)S(1)} %add.3), channel_id=1, replica_groups={{0,16,32,48,64,80,96,112,128,144,160,176,192,208,224,240,256,272,288,30..., dimensions={0} | all-to-all | bytes 2359296 | tf_op jit(solution)/shard_map/all_to_all | solution.py:314
  45.1 0.1 reduce_sum.18
  45.2 16.8 %all_to_all.21 = f32[8,72,128]{2,1,0:T(8,128)S(1)} all-to-all(f32[8,72,128]{2,1,0:T(8,128)S(1)} %broadcast_in_dim.6), channel_id=1, replica_groups={{0,1,2,3,4,5,6,7},{16,17,18,19,20,21,22,23},{32,33,34,35,36,37,38,39},{..., dimensions={0} | all-to-all | bytes 589824 | tf_op jit(solution)/shard_map/all_to_all | solution.py:315
  62.0 15.1 %all_to_all.22 = f32[32,24,128]{2,1,0:T(8,128)S(1)} all-to-all(f32[32,24,128]{2,1,0:T(8,128)S(1)} %broadcast_in_dim.7), channel_id=1, replica_groups={{0,16,32,48,64,80,96,112,128,144,160,176,192,208,224,240,256,272,288,30..., dimensions={0} | all-to-all | bytes 786432 | tf_op jit(solution)/shard_map/all_to_all | solution.py:321
  77.1 0.9 broadcast_in_dim.8
  78.0 4.1 %all-to-all-start.3 = ((f32[32,48,128]{2,1,0:T(8,128)}), f32[32,48,128]{2,1,0:T(8,128)S(1)}, u32[]{:S(2)}, u32[]{:S(2)}) async-start(f32[32,48,128]{2,1,0:T(8,128)} %broadcast_in_dim.8), calls=%async_computation.3 | async-start | bytes 1572864 | tf_op jit(solution)/shard_map/all_to_all | solution.py:321
  82.1 5.7 %collective-permute-start.1 = (f32[768,128]{1,0:T(8,128)S(1)}, f32[768,128]{1,0:T(8,128)S(1)}, u32[]{:S(2)}, u32[]{:S(2)}) collective-permute-start(f32[768,128]{1,0:T(8,128)S(1)} %bitcast.5), channel_id=1, source_target_pairs={{0,8},{8,0},{1,9},{9,1},{2,10},{10,2},{3,11},{11,3},{4,12},{12,4},... | collective-permute-start | bytes 1179656 | tf_op jit(solution)/shard_map/ppermute | solution.py:323
  87.8 9.2 %all-to-all-done.3 = f32[32,48,128]{2,1,0:T(8,128)S(1)} async-done(((f32[32,48,128]{2,1,0:T(8,128)}), f32[32,48,128]{2,1,0:T(8,128)S(1)}, u32[]{:S(2)}, u32[]{:S(2)}) %all-to-all-start.3) | async-done | bytes 786464 | tf_op jit(solution)/shard_map/all_to_all | solution.py:321
  97.0 0.0 copy-start.1
  97.0 7.0 %collective-permute-start.2 = (f32[1536,128]{1,0:T(8,128)S(1)}, f32[1536,128]{1,0:T(8,128)S(1)}, u32[]{:S(2)}, u32[]{:S(2)}) collective-permute-start(f32[1536,128]{1,0:T(8,128)S(1)} %bitcast.3), channel_id=1, source_target_pairs={{0,8},{8,0},{1,9},{9,1},{2,10},{10,2},{3,11},{11,3},{4,12},{12,4},... | collective-permute-start | bytes 2359304 | tf_op jit(solution)/shard_map/ppermute | solution.py:323
  103.9 0.0 collective-permute-done.1.refs_2_
  104.0 18.3 %factor.1 = (f32[512,512]{1,0:T(8,128)S(1)}, f32[512,512]{1,0:T(8,128)}) custom-call(s32[1]{0:T(128)} %bitcast.core_ref.refs_0_, f32[768,128]{1,0:T(8,128)S(1)} %bitcast.6, f32[768,128]{1,0:T(8,128)S(1)} %collective-permute-done.1.refs_2_), custom_call_target="tpu_custom_call" | custom-call | flops 8000000000 | bytes 2097152 | tf_op jit(solution)/shard_map/factor/pallas_call | solution.py:240
  122.2 0.0 copy-done.1
  122.2 0.0 copy-start
  122.2 0.9 basis.1.refs_4_
  123.2 0.0 collective-permute-done.2.refs_3_
  123.2 0.1 copy-done
  123.3 4.1 %update.1 = f32[192,768]{1,0:T(8,128)} custom-call(s32[1]{0:T(128)} %bitcast.core_ref.refs_0_, f32[512,512]{1,0:T(8,128)S(1)} %get-tuple-element.8.x_ref.refs_1_, f32[1536,128]{1,0:T(8,128)S(1)} %bitcast.4, f32[1536,128]{1,0:T(8,128)S(1)} %collective-permute-done.2.refs_3_, f32[192,512]{1,0:T(8,128)S(1)} %basis.1.refs_4_, f32[192,768]{1,0:T(8,128)S(1)} %copy-done), custom_call_target="tpu_custom_call" | custom-call | flops 3000000000 | bytes 4194304 | tf_op jit(solution)/shard_map/update/pallas_call | solution.py:287
  (5 shorter events, 0.1 us)
Async XLA Ops:
  4.1 12.1 %collective-permute-start = (f32[32,72,128]{2,1,0:T(8,128)}, f32[32,72,128]{2,1,0:T(8,128)S(1)}, u32[]{:S(2)}, u32[]{:S(2)}) collective-permute-start(f32[32,72,128]{2,1,0:T(8,128)} %gram_send.1), channel_id=1, source_target_pairs={{0,8},{8,0},{1,9},{9,1},{2,10},{10,2},{3,11},{11,3},{4,12},{12,4},... | collective-permute-start | bytes 3538952 | tf_op jit(solution)/shard_map/ppermute | solution.py:313
  78.0 18.9 %all-to-all-start.3 = ((f32[32,48,128]{2,1,0:T(8,128)}), f32[32,48,128]{2,1,0:T(8,128)S(1)}, u32[]{:S(2)}, u32[]{:S(2)}) async-start(f32[32,48,128]{2,1,0:T(8,128)} %broadcast_in_dim.8), calls=%async_computation.3 | async-start | bytes 1572864 | tf_op jit(solution)/shard_map/all_to_all | solution.py:321
  82.1 21.8 %collective-permute-start.1 = (f32[768,128]{1,0:T(8,128)S(1)}, f32[768,128]{1,0:T(8,128)S(1)}, u32[]{:S(2)}, u32[]{:S(2)}) collective-permute-start(f32[768,128]{1,0:T(8,128)S(1)} %bitcast.5), channel_id=1, source_target_pairs={{0,8},{8,0},{1,9},{9,1},{2,10},{10,2},{3,11},{11,3},{4,12},{12,4},... | collective-permute-start | bytes 1179656 | tf_op jit(solution)/shard_map/ppermute | solution.py:323
  97.0 25.2 %copy-start.1 = (f32[192,512]{1,0:T(8,128)S(1)}, f32[192,512]{1,0:T(8,128)}, u32[]{:S(2)}) copy-start(f32[192,512]{1,0:T(8,128)} %a_ref.3) | copy-start | bytes 1179652
  97.0 26.2 %collective-permute-start.2 = (f32[1536,128]{1,0:T(8,128)S(1)}, f32[1536,128]{1,0:T(8,128)S(1)}, u32[]{:S(2)}, u32[]{:S(2)}) collective-permute-start(f32[1536,128]{1,0:T(8,128)S(1)} %bitcast.3), channel_id=1, source_target_pairs={{0,8},{8,0},{1,9},{9,1},{2,10},{10,2},{3,11},{11,3},{4,12},{12,4},... | collective-permute-start | bytes 2359304 | tf_op jit(solution)/shard_map/ppermute | solution.py:323
  122.2 1.1 copy-start

commit v7 on v6

--- a/solution.py
+++ b/solution.py
@@ -28,7 +28,7 @@
 C_ROWS = C_HALF * B // PARTS
 
 
-def products(mine, core, a_ref, t_ref, out_ref, ready):
+def products(mine, core, a_ref, t_ref, out_ref):
     g_place = {b: (owner, slot) for b, owner, slot in split_half(G_BLOCKS)}
     c_place = {b: (owner, slot) for b, owner, slot in split_half(C_BLOCKS)}
 
@@ -39,7 +39,6 @@
 
     def fill(me):
         owner = me if mine else 1 - me
-        ready(0)
         for i in range(NP):
             cols = [j for j in range(i, NP) if g_place[(i, j)][0] == owner]
             if cols:
@@ -48,7 +47,6 @@
                 for j in cols:
                     put(g[:, (j - lo) * B : (j - lo + 1) * B], g_place[(i, j)][1], 0, G_ROWS)
         put(jnp.zeros((B, B), jnp.float32), G_HALF - 1, 0, G_ROWS)
-        ready(1)
         for i in range(NP):
             cols = [j for j in range(NC) if c_place[(i, j)][0] == owner]
             if cols:
@@ -61,33 +59,25 @@
         pl.when(core == me)(lambda me=me: fill(me))
 
 
-def send_kernel(core_ref, a_hbm, t_hbm, out_ref, a_ref, t_ref, sem):
-    copies = [pltpu.make_async_copy(a_hbm, a_ref, sem.at[0]), pltpu.make_async_copy(t_hbm, t_ref, sem.at[1])]
-    for copy in copies:
-        copy.start()
-    products(False, core_ref[0], a_ref, t_ref, out_ref, lambda k: copies[k].wait())
+def send_kernel(core_ref, a_ref, t_ref, out_ref):
+    products(False, core_ref[0], a_ref, t_ref, out_ref)
 
 
 def keep_kernel(core_ref, a_ref, t_ref, out_ref):
-    products(True, core_ref[0], a_ref, t_ref, out_ref, lambda k: None)
+    products(True, core_ref[0], a_ref, t_ref, out_ref)
 
 
 def gram(core, a, t):
-    out = jax.ShapeDtypeStruct((PARTS, G_ROWS + C_ROWS, B), jnp.float32)
-    cost = pl.CostEstimate(flops=192 * 512 * 1280, bytes_accessed=2 << 20, transcendentals=0)
-    hbm = pl.BlockSpec(memory_space=pltpu.HBM)
-    send = pl.pallas_call(
-        send_kernel,
-        out_shape=out, in_specs=[SM, hbm, hbm], out_specs=VM,
-        scratch_shapes=[pltpu.VMEM(a.shape, a.dtype), pltpu.VMEM(t.shape, t.dtype), pltpu.SemaphoreType.DMA((2,))],
-        cost_estimate=cost, name="gram_send",
-    )(core, a, t)
-    keep = pl.pallas_call(
-        keep_kernel,
-        out_shape=out, in_specs=[SM, VM, VM], out_specs=VM,
-        cost_estimate=cost, name="gram_keep",
-    )(core, a, t)
-    return keep, send
+    return [
+        pl.pallas_call(
+            kernel,
+            out_shape=jax.ShapeDtypeStruct((PARTS, G_ROWS + C_ROWS, B), jnp.float32),
+            in_specs=[SM, VM, VM], out_specs=VM,
+            cost_estimate=pl.CostEstimate(flops=192 * 512 * 1280, bytes_accessed=2 << 20, transcendentals=0),
+            compiler_params=ROOM,
+        )(core, a, t)
+        for kernel in (keep_kernel, send_kernel)
+    ]
 
 
 def stack_pieces(u, order):

time: 128 us -> 126 us (0.984)
  Pallas kernels: 30.1 us -> 25.8 us
  local copies, waits for them, and re-layouts: 1.09 us -> 3.14 us
    pallas_call x2, Pallas kernels: 6.81 us -> 2.41 us  [gram(): pl.pallas_call(kernel, out_shape=jax.ShapeDtypeStruct((PARTS, G_ROWS + C_...]
    unnamed x4 -> x8, local copies, waits for them, and re-layouts: 0.11 us -> 2.15 us
  transfers between devices with their start and end apart: 4 -> 4, of which waited for: 1 -> 2; matrix products, arithmetic and copies ran while one was open for 0% -> 0% of each run, Pallas kernels for 18% -> 16%
where the time goes in v7:
time: 126 us
  blocking collectives  59.2 us (47%)
  starting transfers between devices  26.4 us (21%)
  Pallas kernels  25.8 us (20%)
  waiting for transfers between devices  9.99 us (8%)
  local copies, waits for them, and re-layouts  3.14 us (2%)
    all_to_all x1, blocking collectives, reduce_over_devices(): lax.all_to_all(half, ALL, 0, 0, axis_index_groups=PLANES)  27.4 us
    pallas_call x1, Pallas kernels, factor(): pl.pallas_call(lambda *refs: factor_kernel(row_count, *refs), out_shape=(...  18.3 us
    all_to_all x1, blocking collectives, reduce_over_devices(): lax.all_to_all(jnp.broadcast_to(mine[None], (8,) + mine.shape), ALL, 0, 0...  16.8 us
    all_to_all x1, blocking collectives, spread(): half = lax.all_to_all(copies, ALL, 0, 0, axis_index_groups=PLANES)  15 us
    ppermute x2, starting transfers between devices, spread(): return (half, lax.ppermute(half, 'c', [(0, 1), (1, 0)]))  13.6 us
    all_to_all x1, waiting for transfers between devices, spread(): half = lax.all_to_all(copies, ALL, 0, 0, axis_index_groups=PLANES)  8.74 us
    ppermute x1, starting transfers between devices, reduce_over_devices(): half = keep + lax.ppermute(send, 'c', [(0, 1), (1, 0)])  8.73 us
    pallas_call x1, Pallas kernels, update(): pl.pallas_call(lambda *refs: update_kernel(row_count, *refs), out_shape=j...  4.17 us
  transfers between devices with their start and end apart: 4, of which 2 were waited for; matrix products, arithmetic and copies ran while one was open for 0% of the time, Pallas kernels for 16%

profile of v7, /device:TPU:1, one launch (start us, length us, event | category | flops | bytes accessed | tf_op | source)
XLA Modules:
  0.0 125.6 jit_solution(13284172509986639455)
XLA Ops:
  0.6 0.0 copy-start
  0.6 1.1 copy-done
  1.7 1.0 copy-done.2
  2.7 1.2 shard_map.42
  3.9 8.7 %collective-permute-start = (f32[32,72,128]{2,1,0:T(8,128)S(1)}, f32[32,72,128]{2,1,0:T(8,128)S(1)}, u32[]{:S(2)}, u32[]{:S(2)}) collective-permute-start(f32[32,72,128]{2,1,0:T(8,128)S(1)} %shard_map.42), channel_id=1, source_target_pairs={{0,8},{8,0},{1,9},{9,1},{2,10},{10,2},{3,11},{11,3},{4,12},{12,4},... | collective-permute-start | bytes 3538952 | tf_op jit(solution)/shard_map/ppermute | solution.py:303
  12.7 1.2 shard_map.41
  13.9 1.2 collective-permute-done
  15.1 0.1 add.3
  15.2 27.4 %all_to_all.20 = f32[32,72,128]{2,1,0:T(8,128)S(1)} all-to-all(f32[32,72,128]{2,1,0:T(8,128)S(1)} %add.3), channel_id=1, replica_groups={{0,16,32,48,64,80,96,112,128,144,160,176,192,208,224,240,256,272,288,30..., dimensions={0} | all-to-all | bytes 2359296 | tf_op jit(solution)/shard_map/all_to_all | solution.py:304
  42.7 0.1 reduce_sum.18
  42.8 16.8 %all_to_all.21 = f32[8,72,128]{2,1,0:T(8,128)S(1)} all-to-all(f32[8,72,128]{2,1,0:T(8,128)S(1)} %broadcast_in_dim.6), channel_id=1, replica_groups={{0,1,2,3,4,5,6,7},{16,17,18,19,20,21,22,23},{32,33,34,35,36,37,38,39},{..., dimensions={0} | all-to-all | bytes 589824 | tf_op jit(solution)/shard_map/all_to_all | solution.py:305
  59.6 15.0 %all_to_all.22 = f32[32,24,128]{2,1,0:T(8,128)S(1)} all-to-all(f32[32,24,128]{2,1,0:T(8,128)S(1)} %broadcast_in_dim.7), channel_id=1, replica_groups={{0,16,32,48,64,80,96,112,128,144,160,176,192,208,224,240,256,272,288,30..., dimensions={0} | all-to-all | bytes 786432 | tf_op jit(solution)/shard_map/all_to_all | solution.py:311
  74.6 0.9 broadcast_in_dim.8
  75.6 4.2 %all-to-all-start.3 = ((f32[32,48,128]{2,1,0:T(8,128)}), f32[32,48,128]{2,1,0:T(8,128)S(1)}, u32[]{:S(2)}, u32[]{:S(2)}) async-start(f32[32,48,128]{2,1,0:T(8,128)} %broadcast_in_dim.8), calls=%async_computation.3 | async-start | bytes 1572864 | tf_op jit(solution)/shard_map/all_to_all | solution.py:311
  79.7 6.2 %collective-permute-start.1 = (f32[768,128]{1,0:T(8,128)S(1)}, f32[768,128]{1,0:T(8,128)S(1)}, u32[]{:S(2)}, u32[]{:S(2)}) collective-permute-start(f32[768,128]{1,0:T(8,128)S(1)} %bitcast.5), channel_id=1, source_target_pairs={{0,8},{8,0},{1,9},{9,1},{2,10},{10,2},{3,11},{11,3},{4,12},{12,4},... | collective-permute-start | bytes 1179656 | tf_op jit(solution)/shard_map/ppermute | solution.py:313
  85.9 8.7 %all-to-all-done.3 = f32[32,48,128]{2,1,0:T(8,128)S(1)} async-done(((f32[32,48,128]{2,1,0:T(8,128)}), f32[32,48,128]{2,1,0:T(8,128)S(1)}, u32[]{:S(2)}, u32[]{:S(2)}) %all-to-all-start.3) | async-done | bytes 786464 | tf_op jit(solution)/shard_map/all_to_all | solution.py:311
  94.6 7.4 %collective-permute-start.2 = (f32[1536,128]{1,0:T(8,128)S(1)}, f32[1536,128]{1,0:T(8,128)S(1)}, u32[]{:S(2)}, u32[]{:S(2)}) collective-permute-start(f32[1536,128]{1,0:T(8,128)S(1)} %bitcast.3), channel_id=1, source_target_pairs={{0,8},{8,0},{1,9},{9,1},{2,10},{10,2},{3,11},{11,3},{4,12},{12,4},... | collective-permute-start | bytes 2359304 | tf_op jit(solution)/shard_map/ppermute | solution.py:313
  102.0 0.0 collective-permute-done.1.refs_2_
  102.1 18.3 %factor.1 = (f32[512,512]{1,0:T(8,128)S(1)}, f32[512,512]{1,0:T(8,128)}) custom-call(s32[1]{0:T(128)} %bitcast.core_ref.refs_0_, f32[768,128]{1,0:T(8,128)S(1)} %bitcast.6, f32[768,128]{1,0:T(8,128)S(1)} %collective-permute-done.1.refs_2_), custom_call_target="tpu_custom_call" | custom-call | flops 8000000000 | bytes 2097152 | tf_op jit(solution)/shard_map/factor/pallas_call | solution.py:230
  120.3 0.0 copy-done.3
  120.3 1.0 basis.1.refs_4_
  121.3 0.0 collective-permute-done.2.refs_3_
  121.3 0.1 copy-done.1
  121.4 4.2 %update.1 = f32[192,768]{1,0:T(8,128)} custom-call(s32[1]{0:T(128)} %bitcast.core_ref.refs_0_, f32[512,512]{1,0:T(8,128)S(1)} %get-tuple-element.8.x_ref.refs_1_, f32[1536,128]{1,0:T(8,128)S(1)} %bitcast.4, f32[1536,128]{1,0:T(8,128)S(1)} %collective-permute-done.2.refs_3_, f32[192,512]{1,0:T(8,128)S(1)} %basis.1.refs_4_, f32[192,768]{1,0:T(8,128)S(1)} %copy-done.1), custom_call_target="tpu_custom_call" | custom-call | flops 3000000000 | bytes 4194304 | tf_op jit(solution)/shard_map/update/pallas_call | solution.py:277
  (8 shorter events, 0.1 us)
Async XLA Ops:
  0.6 1.1 copy-start
  1.7 1.0 copy-start.2
  3.9 11.2 %collective-permute-start = (f32[32,72,128]{2,1,0:T(8,128)S(1)}, f32[32,72,128]{2,1,0:T(8,128)S(1)}, u32[]{:S(2)}, u32[]{:S(2)}) collective-permute-start(f32[32,72,128]{2,1,0:T(8,128)S(1)} %shard_map.42), channel_id=1, source_target_pairs={{0,8},{8,0},{1,9},{9,1},{2,10},{10,2},{3,11},{11,3},{4,12},{12,4},... | collective-permute-start | bytes 3538952 | tf_op jit(solution)/shard_map/ppermute | solution.py:303
  75.6 19.1 %all-to-all-start.3 = ((f32[32,48,128]{2,1,0:T(8,128)}), f32[32,48,128]{2,1,0:T(8,128)S(1)}, u32[]{:S(2)}, u32[]{:S(2)}) async-start(f32[32,48,128]{2,1,0:T(8,128)} %broadcast_in_dim.8), calls=%async_computation.3 | async-start | bytes 1572864 | tf_op jit(solution)/shard_map/all_to_all | solution.py:311
  79.7 22.3 %collective-permute-start.1 = (f32[768,128]{1,0:T(8,128)S(1)}, f32[768,128]{1,0:T(8,128)S(1)}, u32[]{:S(2)}, u32[]{:S(2)}) collective-permute-start(f32[768,128]{1,0:T(8,128)S(1)} %bitcast.5), channel_id=1, source_target_pairs={{0,8},{8,0},{1,9},{9,1},{2,10},{10,2},{3,11},{11,3},{4,12},{12,4},... | collective-permute-start | bytes 1179656 | tf_op jit(solution)/shard_map/ppermute | solution.py:313
  94.6 25.7 %copy-start.3 = (f32[192,512]{1,0:T(8,128)S(1)}, f32[192,512]{1,0:T(8,128)}, u32[]{:S(2)}) copy-start(f32[192,512]{1,0:T(8,128)} %a_ref.5) | copy-start | bytes 1179652
  94.6 26.6 %collective-permute-start.2 = (f32[1536,128]{1,0:T(8,128)S(1)}, f32[1536,128]{1,0:T(8,128)S(1)}, u32[]{:S(2)}, u32[]{:S(2)}) collective-permute-start(f32[1536,128]{1,0:T(8,128)S(1)} %bitcast.3), channel_id=1, source_target_pairs={{0,8},{8,0},{1,9},{9,1},{2,10},{10,2},{3,11},{11,3},{4,12},{12,4},... | collective-permute-start | bytes 2359304 | tf_op jit(solution)/shard_map/ppermute | solution.py:313
  120.3 1.1 copy-start.1

commit v8 on v7

--- a/solution.py
+++ b/solution.py
@@ -10,7 +10,7 @@
 NP = 4
 NC = 6
 G_BLOCKS = [(i, j) for i in range(NP) for j in range(i, NP)]
-C_BLOCKS = [(i, j) for i in range(NP) for j in range(NC)]
+C_BLOCKS = [(i, j) for j in range(NC) for i in range(NP)]
 G_HALF = 6
 C_HALF = 12
 VM = pl.BlockSpec(memory_space=pltpu.VMEM)
@@ -239,49 +239,74 @@
 HALF = NP * B // 2
 
 
-def basis_kernel(x_ref, a_ref, q_ref):
+WIDTH = NC * B // 2
+
+
+def project_kernel(row_count, x_ref, c_ref, p_ref, c):
+    for j in range(NC // 2):
+        c[:, j * B : (j + 1) * B] = c_ref[j * NP * B : (j + 1) * NP * B, :] * (1.0 / row_count)
+    for r0 in (0, HALF):
+        r1 = r0 + HALF
+        p_ref[r0:r1, :] = dot(x_ref[r0:r1, :r1], c[:r1, :])
+
+
+def project(row_count, x, c):
+    shape = (NP * B, WIDTH)
+    return pl.pallas_call(
+        lambda *refs: project_kernel(row_count, *refs),
+        out_shape=jax.ShapeDtypeStruct(shape, jnp.float32), in_specs=[VM, VM], out_specs=VM,
+        scratch_shapes=[pltpu.VMEM(shape, jnp.float32)],
+        cost_estimate=pl.CostEstimate(flops=1_500_000_000, bytes_accessed=2 << 20, transcendentals=0),
+        compiler_params=ROOM, name="project",
+    )(x, c)
+
+
+def columns(core):
+    return slice(core * WIDTH, (core + 1) * WIDTH)
+
+
+def basis_kernel(core_ref, x_ref, a_ref, p_ref, t_ref, q_ref, own_ref):
     for r0 in (0, HALF):
         r1 = r0 + HALF
         q_ref[:, r0:r1] = lax.dot_general(
             a_ref[:, :r1], x_ref[r0:r1, :r1], (((1,), (1,)), ((), ())), precision=HI, preferred_element_type=jnp.float32
         )
-
-
-def basis(x, a):
+    own = dot(q_ref[...], p_ref[...])
+    for me in range(2):
+
+        @pl.when(core_ref[0] == me)
+        def _(me=me):
+            own_ref[...] = t_ref[:, columns(me)] - own
+
+
+def basis(core, x, a, p, t):
     return pl.pallas_call(
         basis_kernel,
-        out_shape=jax.ShapeDtypeStruct(a.shape, jnp.float32), in_specs=[VM, VM], out_specs=VM,
-        cost_estimate=pl.CostEstimate(flops=1_000_000_000, bytes_accessed=2 << 20, transcendentals=0),
+        out_shape=(jax.ShapeDtypeStruct(a.shape, jnp.float32), jax.ShapeDtypeStruct((t.shape[0], WIDTH), jnp.float32)),
+        in_specs=[SM] + [VM] * 4, out_specs=[VM, VM],
+        cost_estimate=pl.CostEstimate(flops=1_500_000_000, bytes_accessed=2 << 20, transcendentals=0),
         compiler_params=ROOM, name="basis",
-    )(x, a)
-
-
-def update_kernel(row_count, core_ref, x_ref, cm_ref, co_ref, q_ref, t_ref, out_ref, c, p):
-    scale = 1.0 / row_count
+    )(core, x, a, p, t)
+
+
+def update_kernel(core_ref, q_ref, p_ref, own_ref, t_ref, out_ref):
+    other = dot(q_ref[...], p_ref[...])
     for me in range(2):
 
         @pl.when(core_ref[0] == me)
         def _(me=me):
-            refs = (cm_ref, co_ref) if me == 0 else (co_ref, cm_ref)
-            for (i, j), owner, slot in split_half(C_BLOCKS):
-                c[i * B : (i + 1) * B, j * B : (j + 1) * B] = refs[owner][slot * B : (slot + 1) * B, :] * scale
-
-    for r0 in (0, HALF):
-        r1 = r0 + HALF
-        p[r0:r1, :] = dot(x_ref[r0:r1, :r1], c[:r1, :])
-    out_ref[...] = t_ref[...] - dot(q_ref[...], p[...])
-
-
-def update(row_count, core, x, cm, co, q, t):
-    wide = pltpu.VMEM((NP * B, NC * B), jnp.float32)
+            out_ref[:, columns(me)] = own_ref[...]
+            out_ref[:, columns(1 - me)] = t_ref[:, columns(1 - me)] - other
+
+
+def update(core, q, p, own, t):
     return pl.pallas_call(
-        lambda *refs: update_kernel(row_count, *refs),
+        update_kernel,
         out_shape=jax.ShapeDtypeStruct(t.shape, jnp.float32),
-        in_specs=[SM] + [VM] * 5, out_specs=VM,
-        scratch_shapes=[wide, wide],
-        cost_estimate=pl.CostEstimate(flops=3_000_000_000, bytes_accessed=4 << 20, transcendentals=0),
+        in_specs=[SM] + [VM] * 4, out_specs=VM,
+        cost_estimate=pl.CostEstimate(flops=500_000_000, bytes_accessed=2 << 20, transcendentals=0),
         compiler_params=ROOM, name="update",
-    )(core, x, cm, co, q, t)
+    )(core, q, p, own, t)
 
 
 ALL = ("y", "x", "c", "z")
@@ -308,19 +333,25 @@
 
 def spread(mine):
     copies = jnp.broadcast_to(mine[None], (PARTS,) + mine.shape)
-    half = lax.all_to_all(copies, ALL, 0, 0, axis_index_groups=PLANES)
-    half = half.reshape(-1, B)
-    return half, lax.ppermute(half, "c", [(0, 1), (1, 0)])
+    return lax.all_to_all(copies, ALL, 0, 0, axis_index_groups=PLANES).reshape(-1, B)
+
+
+def from_partner(x):
+    return lax.ppermute(x, "c", [(0, 1), (1, 0)])
 
 
 def local(row_count, panel_block, trailing):
     core = lax.axis_index("c").astype(jnp.int32).reshape(1)
     mine = reduce_over_devices(*gram(core, panel_block, trailing))
     mine_g, mine_c = lax.optimization_barrier((mine[:G_ROWS], mine[G_ROWS:]))
-    gm, go = spread(mine_g)
-    cm, co = spread(mine_c)
-    x, r = factor(row_count, core, gm, go)
-    return r, update(row_count, core, x, cm, co, basis(x, panel_block), trailing)
+    g = spread(mine_g)
+    g_other = from_partner(g)
+    c = spread(mine_c)
+    x, r = factor(row_count, core, g, g_other)
+    p = project(row_count, x, c)
+    p_other = from_partner(p)
+    q, own = basis(core, x, panel_block, p, trailing)
+    return r, update(core, q, p_other, own, trailing)
 
 
 def solution(mesh):

time: 126 us -> 113 us (0.90)
  waiting for transfers between devices: 9.99 us -> 2.62 us
  starting transfers between devices: 26.4 us -> 21.3 us
    all_to_all x1, waiting for transfers between devices: 8.74 us -> 0.01 us  [spread(): lax.all_to_all(copies, ALL, 0, 0, axis_index_groups=PLANES).reshape(-1, B)]
    ppermute x2, starting transfers between devices: 13.6 us -> 8.45 us  [from_partner(): return lax.ppermute(x, 'c', [(0, 1), (1, 0)])]
    ppermute x2, waiting for transfers between devices: 0.01 us -> 1.57 us  [from_partner(): return lax.ppermute(x, 'c', [(0, 1), (1, 0)])]
    pallas_call x2 -> x3, Pallas kernels: 5.12 us -> 4.75 us  [the longest x1 1.68 us: update(): pl.pallas_call(update_kernel, out_shape=jax.ShapeDtypeStruct(t.shape, jnp...]
  transfers between devices with their start and end apart: 4 -> 4, of which waited for: 2 -> 3; matrix products, arithmetic and copies ran while one was open for 0% -> 0% of each run, Pallas kernels for 16% -> 19%
where the time goes in v8:
time: 113 us
  blocking collectives  59.2 us (52%)
  Pallas kernels  25.8 us (23%)
  starting transfers between devices  21.3 us (19%)
  local copies, waits for them, and re-layouts  3.07 us (3%)
  waiting for transfers between devices  2.62 us (2%)
    all_to_all x1, blocking collectives, reduce_over_devices(): lax.all_to_all(half, ALL, 0, 0, axis_index_groups=PLANES)  27.4 us
    pallas_call x1, Pallas kernels, factor(): pl.pallas_call(lambda *refs: factor_kernel(row_count, *refs), out_shape=(...  18.2 us
    all_to_all x1, blocking collectives, reduce_over_devices(): lax.all_to_all(jnp.broadcast_to(mine[None], (8,) + mine.shape), ALL, 0, 0...  16.8 us
    all_to_all x1, blocking collectives, spread(): lax.all_to_all(copies, ALL, 0, 0, axis_index_groups=PLANES).reshape(-1, B)  15 us
    ppermute x1, starting transfers between devices, reduce_over_devices(): half = keep + lax.ppermute(send, 'c', [(0, 1), (1, 0)])  8.75 us
    ppermute x2, starting transfers between devices, from_partner(): return lax.ppermute(x, 'c', [(0, 1), (1, 0)])  8.45 us
    all_to_all x1, starting transfers between devices, spread(): lax.all_to_all(copies, ALL, 0, 0, axis_index_groups=PLANES).reshape(-1, B)  4.15 us
    pallas_call x2, Pallas kernels, gram(): pl.pallas_call(kernel, out_shape=jax.ShapeDtypeStruct((PARTS, G_ROWS + C_...  2.78 us
  transfers between devices with their start and end apart: 4, of which 3 were waited for; matrix products, arithmetic and copies ran while one was open for 0% of the time, Pallas kernels for 19%

profile of v8, /device:TPU:1, one launch (start us, length us, event | category | flops | bytes accessed | tf_op | source)
XLA Modules:
  0.0 113.0 jit_solution(6657396828751811142)
XLA Ops:
  0.6 0.0 copy-start
  0.6 1.1 copy-done
  1.7 1.0 copy-done.2
  2.7 1.4 %shard_map.42 = f32[32,72,128]{2,1,0:T(8,128)S(1)} custom-call(s32[1]{0:T(128)} %bitcast.core_ref.refs_0_, f32[192,512]{1,0:T(8,128)S(1)} %copy-done.2, f32[192,768]{1,0:T(8,128)S(1)} %copy-done), custom_call_target="tpu_custom_call" | custom-call | flops 125829120 | bytes 2097152 | tf_op jit(solution)/shard_map/pallas_call | solution.py:72
  4.1 8.7 %collective-permute-start = (f32[32,72,128]{2,1,0:T(8,128)S(1)}, f32[32,72,128]{2,1,0:T(8,128)S(1)}, u32[]{:S(2)}, u32[]{:S(2)}) collective-permute-start(f32[32,72,128]{2,1,0:T(8,128)S(1)} %shard_map.42), channel_id=1, source_target_pairs={{0,8},{8,0},{1,9},{9,1},{2,10},{10,2},{3,11},{11,3},{4,12},{12,4},... | collective-permute-start | bytes 3538952 | tf_op jit(solution)/shard_map/ppermute | solution.py:328
  12.8 1.4 %shard_map.41 = f32[32,72,128]{2,1,0:T(8,128)S(1)} custom-call(s32[1]{0:T(128)} %bitcast.core_ref.refs_0_, f32[192,512]{1,0:T(8,128)S(1)} %copy-done.2, f32[192,768]{1,0:T(8,128)S(1)} %copy-done), custom_call_target="tpu_custom_call" | custom-call | flops 125829120 | bytes 2097152 | tf_op jit(solution)/shard_map/pallas_call | solution.py:72
  14.3 1.0 collective-permute-done
  15.3 0.1 add.3
  15.4 27.4 %all_to_all.20 = f32[32,72,128]{2,1,0:T(8,128)S(1)} all-to-all(f32[32,72,128]{2,1,0:T(8,128)S(1)} %add.3), channel_id=1, replica_groups={{0,16,32,48,64,80,96,112,128,144,160,176,192,208,224,240,256,272,288,30..., dimensions={0} | all-to-all | bytes 2359296 | tf_op jit(solution)/shard_map/all_to_all | solution.py:329
  42.9 0.1 reduce_sum.18
  43.0 16.8 %all_to_all.21 = f32[8,72,128]{2,1,0:T(8,128)S(1)} all-to-all(f32[8,72,128]{2,1,0:T(8,128)S(1)} %broadcast_in_dim.6), channel_id=1, replica_groups={{0,1,2,3,4,5,6,7},{16,17,18,19,20,21,22,23},{32,33,34,35,36,37,38,39},{..., dimensions={0} | all-to-all | bytes 589824 | tf_op jit(solution)/shard_map/all_to_all | solution.py:330
  59.8 15.0 %all_to_all.22 = f32[32,24,128]{2,1,0:T(8,128)S(1)} all-to-all(f32[32,24,128]{2,1,0:T(8,128)S(1)} %broadcast_in_dim.7), channel_id=1, replica_groups={{0,16,32,48,64,80,96,112,128,144,160,176,192,208,224,240,256,272,288,30..., dimensions={0} | all-to-all | bytes 786432 | tf_op jit(solution)/shard_map/all_to_all | solution.py:336
  74.8 0.9 broadcast_in_dim.8
  75.8 4.2 %all-to-all-start.3 = ((f32[32,48,128]{2,1,0:T(8,128)}), f32[32,48,128]{2,1,0:T(8,128)S(1)}, u32[]{:S(2)}, u32[]{:S(2)}) async-start(f32[32,48,128]{2,1,0:T(8,128)} %broadcast_in_dim.8), calls=%async_computation.3 | async-start | bytes 1572864 | tf_op jit(solution)/shard_map/all_to_all | solution.py:336
  79.9 6.2 %collective-permute-start.1 = (f32[768,128]{1,0:T(8,128)S(1)}, f32[768,128]{1,0:T(8,128)S(1)}, u32[]{:S(2)}, u32[]{:S(2)}) collective-permute-start(f32[768,128]{1,0:T(8,128)S(1)} %bitcast.4), channel_id=1, source_target_pairs={{0,8},{8,0},{1,9},{9,1},{2,10},{10,2},{3,11},{11,3},{4,12},{12,4},... | collective-permute-start | bytes 1179656 | tf_op jit(solution)/shard_map/ppermute | solution.py:340
  86.1 1.3 %collective-permute-done.1.refs_2_ = f32[768,128]{1,0:T(8,128)S(1)} collective-permute-done((f32[768,128]{1,0:T(8,128)S(1)}, f32[768,128]{1,0:T(8,128)S(1)}, u32[]{:S(2)}, u32[]{:S(2)}) %collective-permute-start.1) | collective-permute-done | bytes 393248 | tf_op jit(solution)/shard_map/ppermute | solution.py:340
  87.4 18.2 %factor.1 = (f32[512,512]{1,0:T(8,128)S(1)}, f32[512,512]{1,0:T(8,128)}) custom-call(s32[1]{0:T(128)} %bitcast.core_ref.refs_0_, f32[768,128]{1,0:T(8,128)S(1)} %bitcast.5, f32[768,128]{1,0:T(8,128)S(1)} %collective-permute-done.1.refs_2_), custom_call_target="tpu_custom_call" | custom-call | flops 8000000000 | bytes 2097152 | tf_op jit(solution)/shard_map/factor/pallas_call | solution.py:230
  105.7 0.0 all-to-all-done.3
  105.7 1.4 %project.1.p_ref = f32[512,384]{1,0:T(8,128)S(1)} custom-call(f32[512,512]{1,0:T(8,128)S(1)} %get-tuple-element.10.refs_0_.x_ref, f32[1536,128]{1,0:T(8,128)S(1)} %bitcast.3), custom_call_target="tpu_custom_call" | custom-call | flops 1500000000 | bytes 2097152 | tf_op jit(solution)/shard_map/project/pallas_call | solution.py:255
  107.1 2.3 %collective-permute-start.2 = (f32[512,384]{1,0:T(8,128)S(1)}, f32[512,384]{1,0:T(8,128)S(1)}, u32[]{:S(2)}, u32[]{:S(2)}) collective-permute-start(f32[512,384]{1,0:T(8,128)S(1)} %project.1.p_ref), channel_id=1, source_target_pairs={{0,8},{8,0},{1,9},{9,1},{2,10},{10,2},{3,11},{11,3},{4,12},{12,4},... | collective-permute-start | bytes 2359304 | tf_op jit(solution)/shard_map/ppermute | solution.py:340
  109.4 0.0 copy-done.1
  109.5 1.6 %basis.1 = (f32[192,512]{1,0:T(8,128)S(1)}, f32[192,384]{1,0:T(8,128)S(1)}) custom-call(s32[1]{0:T(128)} %bitcast.core_ref.refs_0_, f32[512,512]{1,0:T(8,128)S(1)} %get-tuple-element.10.refs_0_.x_ref, f32[192,512]{1,0:T(8,128)S(1)} %copy-done.3, f32[512,384]{1,0:T(8,128)S(1)} %project.1.p_ref, f32[192,768]{1,0:T(8,128)S(1)} %copy-done.1), custom_call_target="tpu_custom_call" | custom-call | flops 1500000000 | bytes 2097152 | tf_op jit(solution)/shard_map/basis/pallas_call | solution.py:283
  111.1 0.2 collective-permute-done.2.p_ref
  111.3 1.7 %update.1 = f32[192,768]{1,0:T(8,128)} custom-call(s32[1]{0:T(128)} %bitcast.core_ref.refs_0_, f32[192,512]{1,0:T(8,128)S(1)} %get-tuple-element.12.q_ref, f32[512,384]{1,0:T(8,128)S(1)} %collective-permute-done.2.p_ref, f32[192,384]{1,0:T(8,128)S(1)} %get-tuple-element.13.own_ref, f32[192,768]{1,0:T(8,128)S(1)} %copy-done.1), custom_call_target="tpu_custom_call" | custom-call | flops 500000000 | bytes 2097152 | tf_op jit(solution)/shard_map/update/pallas_call | solution.py:303
  (9 shorter events, 0.1 us)
Async XLA Ops:
  0.6 1.1 copy-start
  1.7 1.0 copy-start.2
  4.1 11.2 %collective-permute-start = (f32[32,72,128]{2,1,0:T(8,128)S(1)}, f32[32,72,128]{2,1,0:T(8,128)S(1)}, u32[]{:S(2)}, u32[]{:S(2)}) collective-permute-start(f32[32,72,128]{2,1,0:T(8,128)S(1)} %shard_map.42), channel_id=1, source_target_pairs={{0,8},{8,0},{1,9},{9,1},{2,10},{10,2},{3,11},{11,3},{4,12},{12,4},... | collective-permute-start | bytes 3538952 | tf_op jit(solution)/shard_map/ppermute | solution.py:328
  75.8 29.9 %all-to-all-start.3 = ((f32[32,48,128]{2,1,0:T(8,128)}), f32[32,48,128]{2,1,0:T(8,128)S(1)}, u32[]{:S(2)}, u32[]{:S(2)}) async-start(f32[32,48,128]{2,1,0:T(8,128)} %broadcast_in_dim.8), calls=%async_computation.3 | async-start | bytes 1572864 | tf_op jit(solution)/shard_map/all_to_all | solution.py:336
  79.9 7.5 %collective-permute-start.1 = (f32[768,128]{1,0:T(8,128)S(1)}, f32[768,128]{1,0:T(8,128)S(1)}, u32[]{:S(2)}, u32[]{:S(2)}) collective-permute-start(f32[768,128]{1,0:T(8,128)S(1)} %bitcast.4), channel_id=1, source_target_pairs={{0,8},{8,0},{1,9},{9,1},{2,10},{10,2},{3,11},{11,3},{4,12},{12,4},... | collective-permute-start | bytes 1179656 | tf_op jit(solution)/shard_map/ppermute | solution.py:340
  105.7 3.8 %copy-start.1 = (f32[192,768]{1,0:T(8,128)S(1)}, f32[192,768]{1,0:T(8,128)}, u32[]{:S(2)}) copy-start(f32[192,768]{1,0:T(8,128)} %t_ref.7) | copy-start | bytes 1769476
  105.7 3.8 %copy-start.3 = (f32[192,512]{1,0:T(8,128)S(1)}, f32[192,512]{1,0:T(8,128)}, u32[]{:S(2)}) copy-start(f32[192,512]{1,0:T(8,128)} %a_ref.5) | copy-start | bytes 1179652
  107.1 4.2 %collective-permute-start.2 = (f32[512,384]{1,0:T(8,128)S(1)}, f32[512,384]{1,0:T(8,128)S(1)}, u32[]{:S(2)}, u32[]{:S(2)}) collective-permute-start(f32[512,384]{1,0:T(8,128)S(1)} %project.1.p_ref), channel_id=1, source_target_pairs={{0,8},{8,0},{1,9},{9,1},{2,10},{10,2},{3,11},{11,3},{4,12},{12,4},... | collective-permute-start | bytes 2359304 | tf_op jit(solution)/shard_map/ppermute | solution.py:340

commit v9 on v8

--- a/solution.py
+++ b/solution.py
@@ -23,6 +23,7 @@
 
 
 PARTS = 32
+UNROLL = 16
 ROOM = pltpu.CompilerParams(vmem_limit_bytes=20 << 20)
 G_ROWS = G_HALF * B // PARTS
 C_ROWS = C_HALF * B // PARTS
@@ -100,14 +101,15 @@
     return jnp.take_along_axis(v, index, axis=1, mode="promise_in_bounds")
 
 
-def eliminate(w_rows, v_rows, w_next, v_next, base):
+def next_columns(rows, base):
+    return [lane_of(rows, jnp.full((8, B), 0, jnp.int32) + jnp.minimum(base + k, B - 1)) for k in range(8)]
+
+
+def eliminate(w_rows, v_rows, cols, w_next, v_next, base):
     sub = lax.broadcasted_iota(jnp.int32, (8, B), 0)
     ahead = jnp.minimum(base + 8 + sub, B - 1)
-    d = {}
-    for k in range(8):
-        col = lane_of(w_rows, jnp.full((8, B), base + k, jnp.int32))
-        for i in range(k + 1):
-            d[i, k] = row_of(col, i)
+    after = next_columns(w_next, base + 8)
+    d = {(i, k): row_of(cols[k], i) for k in range(8) for i in range(k + 1)}
     w = [row_of(w_rows, t) for t in range(8)]
     v = [row_of(v_rows, t) for t in range(8)]
     for t in range(8):
@@ -124,11 +126,12 @@
         weight = lane_of(w[t], ahead)
         w_next = w_next - weight * w[t]
         v_next = v_next - weight * v[t]
+        after = [after[k] - weight * row_of(weight, k) for k in range(8)]
     wo, vo = w[0], v[0]
     for t in range(1, 8):
         wo = jnp.where(sub == t, w[t], wo)
         vo = jnp.where(sub == t, v[t], vo)
-    return wo, vo, w_next, v_next
+    return wo, vo, w_next, v_next, after
 
 
 def apply_rows(w, v, w_next, v_next, base):
@@ -153,7 +156,7 @@
     e[B:, :] = zero
 
     def body(g, carry):
-        w, v, w_last, v_last = carry
+        w, v, w_last, v_last, cols = carry
         base = pl.multiple_of(g * 8, 8)
         rows = pl.ds(base, 8)
         after = pl.ds(base + 8, 8)
@@ -161,14 +164,14 @@
         right = jnp.concatenate([stack_pieces(w_last, RIGHT), stack_pieces(v_last, RIGHT)], axis=1)
         change = lax.dot_general(left, right, (((0,), (0,)), ((), ())), preferred_element_type=jnp.float32)
         w_next, v_next = apply_rows(w_last, v_last, s[after, :], e[after, :], base)
-        w, v, w_next, v_next = eliminate(w, v, w_next, v_next, base)
+        w, v, w_next, v_next, cols = eliminate(w, v, cols, w_next, v_next, base)
         rkk[rows, :] = jnp.where(lane >= sub + base, w, 0.0)
         lkk[rows, :] = v
         s[:B, :] = s[:B, :] - change[:, :B]
         e[:B, :] = e[:B, :] - change[:, B:]
-        return w_next, v_next, w, v
-
-    lax.fori_loop(0, B // 8, body, (s[:8, :], e[:8, :], zero, zero))
+        return w_next, v_next, w, v, cols
+
+    lax.fori_loop(0, B // 8, body, (s[:8, :], e[:8, :], zero, zero, next_columns(s[:8, :], 0)), unroll=UNROLL)
 
 
 def dot(x, y):

time: 113 us -> 109 us (0.965)
  Pallas kernels: 25.8 us -> 21.2 us
    pallas_call x1, Pallas kernels: 18.2 us -> 13.7 us  [factor(): pl.pallas_call(lambda *refs: factor_kernel(row_count, *refs), out_shape=(...]
  transfers between devices with their start and end apart: 4 -> 4, of which waited for: 3 -> 3; matrix products, arithmetic and copies ran while one was open for 0% -> 0% of each run, Pallas kernels for 19% -> 15%
where the time goes in v9:
time: 109 us; the launch traced here: 108 us
  blocking collectives  59.2 us (54%)
  starting transfers between devices  21.4 us (20%)
  Pallas kernels  21.2 us (19%)
  local copies, waits for them, and re-layouts  3.07 us (3%)
  waiting for transfers between devices  2.62 us (2%)
    all_to_all x1, blocking collectives, reduce_over_devices(): lax.all_to_all(half, ALL, 0, 0, axis_index_groups=PLANES)  27.4 us
    all_to_all x1, blocking collectives, reduce_over_devices(): lax.all_to_all(jnp.broadcast_to(mine[None], (8,) + mine.shape), ALL, 0, 0...  16.8 us
    all_to_all x1, blocking collectives, spread(): lax.all_to_all(copies, ALL, 0, 0, axis_index_groups=PLANES).reshape(-1, B)  15 us
    pallas_call x1, Pallas kernels, factor(): pl.pallas_call(lambda *refs: factor_kernel(row_count, *refs), out_shape=(...  13.7 us
    ppermute x1, starting transfers between devices, reduce_over_devices(): half = keep + lax.ppermute(send, 'c', [(0, 1), (1, 0)])  8.75 us
    ppermute x2, starting transfers between devices, from_partner(): return lax.ppermute(x, 'c', [(0, 1), (1, 0)])  8.46 us
    all_to_all x1, starting transfers between devices, spread(): lax.all_to_all(copies, ALL, 0, 0, axis_index_groups=PLANES).reshape(-1, B)  4.16 us
    pallas_call x2, Pallas kernels, gram(): pl.pallas_call(kernel, out_shape=jax.ShapeDtypeStruct((PARTS, G_ROWS + C_...  2.78 us
  transfers between devices with their start and end apart: 4, of which 3 were waited for; matrix products, arithmetic and copies ran while one was open for 0% of the time, Pallas kernels for 15%

profile of v9, /device:TPU:1, one launch (start us, length us, event | category | flops | bytes accessed | tf_op | source)
XLA Modules:
  0.0 108.4 jit_solution(1917504081127316609)
XLA Ops:
  0.6 0.0 copy-start
  0.6 1.1 copy-done
  1.7 1.0 copy-done.2
  2.7 1.4 %shard_map.42 = f32[32,72,128]{2,1,0:T(8,128)S(1)} custom-call(s32[1]{0:T(128)} %bitcast.core_ref.refs_0_, f32[192,512]{1,0:T(8,128)S(1)} %copy-done.2, f32[192,768]{1,0:T(8,128)S(1)} %copy-done), custom_call_target="tpu_custom_call" | custom-call | flops 125829120 | bytes 2097152 | tf_op jit(solution)/shard_map/pallas_call | solution.py:73
  4.1 8.8 %collective-permute-start = (f32[32,72,128]{2,1,0:T(8,128)S(1)}, f32[32,72,128]{2,1,0:T(8,128)S(1)}, u32[]{:S(2)}, u32[]{:S(2)}) collective-permute-start(f32[32,72,128]{2,1,0:T(8,128)S(1)} %shard_map.42), channel_id=1, source_target_pairs={{0,8},{8,0},{1,9},{9,1},{2,10},{10,2},{3,11},{11,3},{4,12},{12,4},... | collective-permute-start | bytes 3538952 | tf_op jit(solution)/shard_map/ppermute | solution.py:331
  12.8 1.4 %shard_map.41 = f32[32,72,128]{2,1,0:T(8,128)S(1)} custom-call(s32[1]{0:T(128)} %bitcast.core_ref.refs_0_, f32[192,512]{1,0:T(8,128)S(1)} %copy-done.2, f32[192,768]{1,0:T(8,128)S(1)} %copy-done), custom_call_target="tpu_custom_call" | custom-call | flops 125829120 | bytes 2097152 | tf_op jit(solution)/shard_map/pallas_call | solution.py:73
  14.2 1.1 collective-permute-done
  15.3 0.1 add.3
  15.4 27.4 %all_to_all.20 = f32[32,72,128]{2,1,0:T(8,128)S(1)} all-to-all(f32[32,72,128]{2,1,0:T(8,128)S(1)} %add.3), channel_id=1, replica_groups={{0,16,32,48,64,80,96,112,128,144,160,176,192,208,224,240,256,272,288,30..., dimensions={0} | all-to-all | bytes 2359296 | tf_op jit(solution)/shard_map/all_to_all | solution.py:332
  42.9 0.1 reduce_sum.18
  43.0 16.8 %all_to_all.21 = f32[8,72,128]{2,1,0:T(8,128)S(1)} all-to-all(f32[8,72,128]{2,1,0:T(8,128)S(1)} %broadcast_in_dim.6), channel_id=1, replica_groups={{0,1,2,3,4,5,6,7},{16,17,18,19,20,21,22,23},{32,33,34,35,36,37,38,39},{..., dimensions={0} | all-to-all | bytes 589824 | tf_op jit(solution)/shard_map/all_to_all | solution.py:333
  59.8 15.0 %all_to_all.22 = f32[32,24,128]{2,1,0:T(8,128)S(1)} all-to-all(f32[32,24,128]{2,1,0:T(8,128)S(1)} %broadcast_in_dim.7), channel_id=1, replica_groups={{0,16,32,48,64,80,96,112,128,144,160,176,192,208,224,240,256,272,288,30..., dimensions={0} | all-to-all | bytes 786432 | tf_op jit(solution)/shard_map/all_to_all | solution.py:339
  74.8 0.9 broadcast_in_dim.8
  75.8 4.2 %all-to-all-start.3 = ((f32[32,48,128]{2,1,0:T(8,128)}), f32[32,48,128]{2,1,0:T(8,128)S(1)}, u32[]{:S(2)}, u32[]{:S(2)}) async-start(f32[32,48,128]{2,1,0:T(8,128)} %broadcast_in_dim.8), calls=%async_computation.3 | async-start | bytes 1572864 | tf_op jit(solution)/shard_map/all_to_all | solution.py:339
  79.9 6.2 %collective-permute-start.1 = (f32[768,128]{1,0:T(8,128)S(1)}, f32[768,128]{1,0:T(8,128)S(1)}, u32[]{:S(2)}, u32[]{:S(2)}) collective-permute-start(f32[768,128]{1,0:T(8,128)S(1)} %bitcast.4), channel_id=1, source_target_pairs={{0,8},{8,0},{1,9},{9,1},{2,10},{10,2},{3,11},{11,3},{4,12},{12,4},... | collective-permute-start | bytes 1179656 | tf_op jit(solution)/shard_map/ppermute | solution.py:343
  86.1 1.3 %collective-permute-done.1.refs_2_ = f32[768,128]{1,0:T(8,128)S(1)} collective-permute-done((f32[768,128]{1,0:T(8,128)S(1)}, f32[768,128]{1,0:T(8,128)S(1)}, u32[]{:S(2)}, u32[]{:S(2)}) %collective-permute-start.1) | collective-permute-done | bytes 393248 | tf_op jit(solution)/shard_map/ppermute | solution.py:343
  87.4 13.7 %factor.1 = (f32[512,512]{1,0:T(8,128)S(1)}, f32[512,512]{1,0:T(8,128)}) custom-call(s32[1]{0:T(128)} %bitcast.core_ref.refs_0_, f32[768,128]{1,0:T(8,128)S(1)} %bitcast.5, f32[768,128]{1,0:T(8,128)S(1)} %collective-permute-done.1.refs_2_), custom_call_target="tpu_custom_call" | custom-call | flops 8000000000 | bytes 2097152 | tf_op jit(solution)/shard_map/factor/pallas_call | solution.py:233
  101.1 0.0 all-to-all-done.3
  101.1 1.4 %project.1.p_ref = f32[512,384]{1,0:T(8,128)S(1)} custom-call(f32[512,512]{1,0:T(8,128)S(1)} %get-tuple-element.10.refs_0_.x_ref, f32[1536,128]{1,0:T(8,128)S(1)} %bitcast.3), custom_call_target="tpu_custom_call" | custom-call | flops 1500000000 | bytes 2097152 | tf_op jit(solution)/shard_map/project/pallas_call | solution.py:258
  102.6 2.3 %collective-permute-start.2 = (f32[512,384]{1,0:T(8,128)S(1)}, f32[512,384]{1,0:T(8,128)S(1)}, u32[]{:S(2)}, u32[]{:S(2)}) collective-permute-start(f32[512,384]{1,0:T(8,128)S(1)} %project.1.p_ref), channel_id=1, source_target_pairs={{0,8},{8,0},{1,9},{9,1},{2,10},{10,2},{3,11},{11,3},{4,12},{12,4},... | collective-permute-start | bytes 2359304 | tf_op jit(solution)/shard_map/ppermute | solution.py:343
  104.9 0.0 copy-done.1
  104.9 1.6 %basis.1 = (f32[192,512]{1,0:T(8,128)S(1)}, f32[192,384]{1,0:T(8,128)S(1)}) custom-call(s32[1]{0:T(128)} %bitcast.core_ref.refs_0_, f32[512,512]{1,0:T(8,128)S(1)} %get-tuple-element.10.refs_0_.x_ref, f32[192,512]{1,0:T(8,128)S(1)} %copy-done.3, f32[512,384]{1,0:T(8,128)S(1)} %project.1.p_ref, f32[192,768]{1,0:T(8,128)S(1)} %copy-done.1), custom_call_target="tpu_custom_call" | custom-call | flops 1500000000 | bytes 2097152 | tf_op jit(solution)/shard_map/basis/pallas_call | solution.py:286
  106.5 0.2 collective-permute-done.2.p_ref
  106.8 1.7 %update.1 = f32[192,768]{1,0:T(8,128)} custom-call(s32[1]{0:T(128)} %bitcast.core_ref.refs_0_, f32[192,512]{1,0:T(8,128)S(1)} %get-tuple-element.12.q_ref, f32[512,384]{1,0:T(8,128)S(1)} %collective-permute-done.2.p_ref, f32[192,384]{1,0:T(8,128)S(1)} %get-tuple-element.13.own_ref, f32[192,768]{1,0:T(8,128)S(1)} %copy-done.1), custom_call_target="tpu_custom_call" | custom-call | flops 500000000 | bytes 2097152 | tf_op jit(solution)/shard_map/update/pallas_call | solution.py:306
  (9 shorter events, 0.1 us)
Async XLA Ops:
  0.6 1.1 copy-start
  1.7 1.0 copy-start.2
  4.1 11.2 %collective-permute-start = (f32[32,72,128]{2,1,0:T(8,128)S(1)}, f32[32,72,128]{2,1,0:T(8,128)S(1)}, u32[]{:S(2)}, u32[]{:S(2)}) collective-permute-start(f32[32,72,128]{2,1,0:T(8,128)S(1)} %shard_map.42), channel_id=1, source_target_pairs={{0,8},{8,0},{1,9},{9,1},{2,10},{10,2},{3,11},{11,3},{4,12},{12,4},... | collective-permute-start | bytes 3538952 | tf_op jit(solution)/shard_map/ppermute | solution.py:331
  75.8 25.3 %all-to-all-start.3 = ((f32[32,48,128]{2,1,0:T(8,128)}), f32[32,48,128]{2,1,0:T(8,128)S(1)}, u32[]{:S(2)}, u32[]{:S(2)}) async-start(f32[32,48,128]{2,1,0:T(8,128)} %broadcast_in_dim.8), calls=%async_computation.3 | async-start | bytes 1572864 | tf_op jit(solution)/shard_map/all_to_all | solution.py:339
  79.9 7.5 %collective-permute-start.1 = (f32[768,128]{1,0:T(8,128)S(1)}, f32[768,128]{1,0:T(8,128)S(1)}, u32[]{:S(2)}, u32[]{:S(2)}) collective-permute-start(f32[768,128]{1,0:T(8,128)S(1)} %bitcast.4), channel_id=1, source_target_pairs={{0,8},{8,0},{1,9},{9,1},{2,10},{10,2},{3,11},{11,3},{4,12},{12,4},... | collective-permute-start | bytes 1179656 | tf_op jit(solution)/shard_map/ppermute | solution.py:343
  101.1 3.8 %copy-start.1 = (f32[192,768]{1,0:T(8,128)S(1)}, f32[192,768]{1,0:T(8,128)}, u32[]{:S(2)}) copy-start(f32[192,768]{1,0:T(8,128)} %t_ref.7) | copy-start | bytes 1769476
  101.1 3.8 %copy-start.3 = (f32[192,512]{1,0:T(8,128)S(1)}, f32[192,512]{1,0:T(8,128)}, u32[]{:S(2)}) copy-start(f32[192,512]{1,0:T(8,128)} %a_ref.5) | copy-start | bytes 1179652
  102.6 4.2 %collective-permute-start.2 = (f32[512,384]{1,0:T(8,128)S(1)}, f32[512,384]{1,0:T(8,128)S(1)}, u32[]{:S(2)}, u32[]{:S(2)}) collective-permute-start(f32[512,384]{1,0:T(8,128)S(1)} %project.1.p_ref), channel_id=1, source_target_pairs={{0,8},{8,0},{1,9},{9,1},{2,10},{10,2},{3,11},{11,3},{4,12},{12,4},... | collective-permute-start | bytes 2359304 | tf_op jit(solution)/shard_map/ppermute | solution.py:343
